TPU v7x, 256 devices: a whole 4x4x8 slice. The times are simulated.
256 devices in a mesh: dp: 64 (over y, z, x_lo), space: 4 (over x_hi, core).
Axes of the slice: x: 4 (x_hi: 2, x_lo: 2; x = x_hi * 2 + x_lo), y: 4, z: 8, core: 2. Of those that a mesh axis runs over, the one named last changes fastest.
Arguments:
- volumes: bfloat16 [256, 32, 64, 512], P('dp', None, 'space'), may hold values from -6 to 6
- first_kernel: bfloat16 [27, 32, 64], replicated, may hold values from -0.21875 to 0.21875
- second_kernel: bfloat16 [27, 64, 128], replicated, may hold values from -0.15625 to 0.15625
- upstream: bfloat16 [256, 128, 16, 32], P(('dp', 'space')), may hold values from -6 to 6
Outputs:
- features: bfloat16 [256, 128, 16, 32], P(('dp', 'space'))
- first_grad: float32 [27, 32, 64], replicated
- second_grad: float32 [27, 64, 128], replicated
All inputs are finite; a program needn't handle non-finite values.
Results may differ from a plain program's by a relative error of at most 0.0059.
Values may be sent and summed in bfloat16 or wider, within the bound.
No kernel may reach another device: no remote copies, remote signals or barrier semaphores. Data moves between devices by JAX's collectives and lax.ppermute only.
A program may use at most 64 MiB of HBM per device.

v0:
```python
import jax
import jax.numpy as jnp
from jax import lax
from jax.sharding import PartitionSpec as P

YD = 32
ZD = 16


def shifted(value, axis, steps):
    count = lax.axis_size(axis)
    initial, last = (max(0, -steps), min(count, count - steps))
    return lax.ppermute(value, axis, [(source, source + steps) for source in range(initial, last)])


def smooth_act(value):
    return 0.3 * value + 0.7 * jax.nn.softplus(value)


def smooth_slope(value):
    return 0.3 + 0.7 * jax.nn.sigmoid(value)


def plane_table(size_y, size_z):
    half_y = size_y // 2
    half_z = size_z // 2
    cells = jnp.arange(half_y * half_z, dtype=jnp.int32)
    out_y = cells // half_z
    out_z = cells % half_z
    source = jnp.arange(size_y * size_z, dtype=jnp.int32)[:, None]
    blocks = []
    for second in range(3):
        for third in range(3):
            read_y = 2 * out_y + second - 1
            read_z = 2 * out_z + third - 1
            index = jnp.where((read_y >= 0) & (read_z >= 0), read_y * size_z + read_z, -1)
            blocks.append((source == index[None, :]).astype(jnp.bfloat16))
    return jnp.concatenate(blocks, 1)


def tap_planes(padded, table):
    return jnp.dot(padded, table, preferred_element_type=jnp.bfloat16)


def tap_rows(planes, first, out_rows):
    group, chans, rows, width = planes.shape
    picked = planes[:, :, first : first + 2 * out_rows : 2]
    return picked.reshape(group, chans, out_rows, 9, width // 9)


def forward_conv(planes, kernel, out_rows):
    total = None
    for first in range(3):
        rows = tap_rows(planes, first, out_rows)
        term = jnp.einsum(
            "scxtm,tco->soxm",
            rows,
            kernel[9 * first : 9 * first + 9],
            preferred_element_type=jnp.float32,
        )
        total = term if total is None else total + term
    return total


def kernel_grad(planes, delta):
    out_rows = delta.shape[2]
    blocks = []
    for first in range(3):
        rows = tap_rows(planes, first, out_rows)
        blocks.append(
            jnp.einsum("scxtm,soxm->tco", rows, delta, preferred_element_type=jnp.float32)
        )
    return jnp.concatenate(blocks, 0)


def input_grad(delta, kernel, table):
    group, outs, out_rows, cells = delta.shape
    chans = kernel.shape[1]
    width = 9 * cells
    parts = []
    for first in range(3):
        term = jnp.einsum(
            "soxm,tco->scxtm",
            delta,
            kernel[9 * first : 9 * first + 9],
            preferred_element_type=jnp.float32,
        )
        parts.append(term.reshape(group, chans, out_rows, width))
    zero_row = jnp.zeros((group, chans, 1, width), jnp.float32)
    even = jnp.concatenate([parts[0], zero_row], 2) + jnp.concatenate([zero_row, parts[2]], 2)
    woven = jnp.stack([even[:, :, :out_rows], parts[1]], 3).reshape(
        group, chans, 2 * out_rows, width
    )
    grad_planes = jnp.concatenate([woven, even[:, :, out_rows:]], 2)
    return jnp.dot(grad_planes, table.T.astype(jnp.float32), precision=lax.Precision.HIGHEST)


def per_device(volumes, first_kernel, second_kernel, upstream):
    group = volumes.shape[0]
    rows_in = volumes.shape[2]
    mid_ch = first_kernel.shape[2]
    scale = 1.0 / (group * lax.axis_size("dp"))
    first_table = plane_table(YD, ZD)
    second_table = plane_table(YD // 2, ZD // 2)
    rim = shifted(volumes[:, :, -1:, :], "space", 1)
    padded = jnp.concatenate([rim, volumes], 2)
    first_planes = tap_planes(padded, first_table)
    pre_first = forward_conv(first_planes, first_kernel, rows_in // 2)
    hidden = smooth_act(pre_first).astype(jnp.bfloat16)
    whole = lax.all_to_all(hidden, "space", split_axis=0, concat_axis=2, tiled=True)
    full_rows = whole.shape[2]
    zero_layer = jnp.zeros((whole.shape[0], mid_ch, 1, whole.shape[3]), jnp.bfloat16)
    hidden_pad = jnp.concatenate([zero_layer, whole], 2)
    second_planes = tap_planes(hidden_pad, second_table)
    pre_second = forward_conv(second_planes, second_kernel, full_rows // 2)
    features = smooth_act(pre_second).astype(jnp.bfloat16)
    delta_second = (upstream.astype(jnp.float32) * smooth_slope(pre_second)).astype(jnp.bfloat16)
    second_term = scale * kernel_grad(second_planes, delta_second)
    back = input_grad(delta_second, second_kernel, second_table)
    back_whole = back[:, :, 1:].astype(jnp.bfloat16)
    back_hidden = lax.all_to_all(back_whole, "space", split_axis=2, concat_axis=0, tiled=True)
    second_grad = lax.psum(second_term, ("dp", "space"))
    delta_first = (back_hidden.astype(jnp.float32) * smooth_slope(pre_first)).astype(jnp.bfloat16)
    first_grad = lax.psum(scale * kernel_grad(first_planes, delta_first), ("dp", "space"))
    return (features, first_grad, second_grad)


def solution(mesh):
    in_specs = (P("dp", None, "space", None), P(), P(), P(("dp", "space"), None, None, None))
    out_specs = (P(("dp", "space"), None, None, None), P(), P())
    return jax.shard_map(
        per_device, mesh=mesh, in_specs=in_specs, out_specs=out_specs, check_vma=False
    )
```

profile of v0, /device:TPU:1, one launch (start us, length us, event | category | flops | bytes accessed | tf_op | source)
XLA Modules:
  0.0 365.0 jit_solution(14419749668418056123)
XLA Ops:
  7.2 2.8 copy.45
  9.9 6.0 %collective-permute-start = (bf16[4,32,1,512]{3,1,2,0:T(8,128)(2,1)S(1)}, bf16[4,32,1,512]{3,1,2,0:T(8,128)(2,1)S(1)}, u32[]{:S(2)}, u32[]{:S(2)}) collective-permute-start(bf16[4,32,1,512]{3,1,2,0:T(8,128)(2,1)S(1)} %slice.74), channel_id=1, source_target_pairs={{0,1},{1,2},{2,3},{4,5},{5,6},{6,7},{8,9},{9,10},{10,11},{12,13},{... | collective-permute-start | bytes 393224 | tf_op jit(solution)/shard_map/ppermute | solution.py:13
  17.9 3.3 fusion.15
  22.7 1.8 copy_bitcast_fusion
  26.7 2.4 fusion.56
  29.1 5.6 %all-to-all-start = ((bf16[4,64,8,128]{3,1,2,0:T(8,128)(2,1)}), bf16[4,64,8,128]{3,1,2,0:T(8,128)(2,1)S(1)}, u32[]{:S(2)}, u32[]{:S(2)}) async-start(bf16[4,64,8,128]{3,1,2,0:T(8,128)(2,1)} %get-tuple-element.11), calls=%async_computation | async-start | bytes 1048576 | tf_op jit(solution)/shard_map/all_to_all | solution.py:110
  34.9 9.2 %all-to-all-done = bf16[4,64,8,128]{3,1,2,0:T(8,128)(2,1)S(1)} async-done(((bf16[4,64,8,128]{3,1,2,0:T(8,128)(2,1)}), bf16[4,64,8,128]{3,1,2,0:T(8,128)(2,1)S(1)}, u32[]{:S(2)}, u32[]{:S(2)}) %all-to-all-start) | async-done | bytes 524320 | tf_op jit(solution)/shard_map/all_to_all | solution.py:110
  47.5 1.9 copy.54
  49.5 1.6 convolution_bitcast_fusion.4
  54.8 1.9 fusion.76
  56.7 2.0 fusion.79
  58.7 1.9 fusion.82
  60.6 2.2 copy.57
  62.8 2.2 copy.56
  66.4 2.3 copy.58
  69.7 1.6 fusion.41
  72.2 5.1 %all-to-all-start.1 = ((bf16[1,64,32,128]{3,1,0,2:T(8,128)(2,1)}), bf16[1,64,32,128]{3,1,0,2:T(8,128)(2,1)}, u32[]{:S(2)}, u32[]{:S(2)}) async-start(bf16[1,64,32,128]{3,1,0,2:T(8,128)(2,1)} %slice_bitcast_fusion), calls=%async_computation.1 | async-start | bytes 1048576 | tf_op jit(solution)/shard_map/all_to_all | solution.py:121
  77.8 1.6 convolution_bitcast_fusion.1
  79.3 1.9 maximum_multiply_fusion
  81.3 5.4 %all-to-all-done.1 = bf16[1,64,32,128]{3,1,0,2:T(8,128)(2,1)} async-done(((bf16[1,64,32,128]{3,1,0,2:T(8,128)(2,1)}), bf16[1,64,32,128]{3,1,0,2:T(8,128)(2,1)}, u32[]{:S(2)}, u32[]{:S(2)}) %all-to-all-start.1) | async-done | bytes 524320 | tf_op jit(solution)/shard_map/all_to_all | solution.py:121
  86.7 1.7 fusion.57
  94.2 260.0 %all-reduce.6.cloned.1.call-done = (f32[27,32,64]{2,1,0:T(8,128)}, f32[27,64,128]{2,1,0:T(8,128)}) async-done(((f32[27,32,64]{2,1,0:T(8,128)}, f32[27,64,128]{2,1,0:T(8,128)}), (f32[27,32,64]{2,1,0:T(8,128)}, f32[27,64,128]{2,1,0:T(8,128)})) %all-reduce.6.cloned.1.call-update) | async-done | bytes 1105936 | tf_op jit(solution)/shard_map/psum | solution.py:124
  354.2 1.8 copy.139
  356.0 2.2 copy.140
  (100 shorter events, 22.1 us)
Async XLA Ops:
  9.9 8.0 %collective-permute-start = (bf16[4,32,1,512]{3,1,2,0:T(8,128)(2,1)S(1)}, bf16[4,32,1,512]{3,1,2,0:T(8,128)(2,1)S(1)}, u32[]{:S(2)}, u32[]{:S(2)}) collective-permute-start(bf16[4,32,1,512]{3,1,2,0:T(8,128)(2,1)S(1)} %slice.74), channel_id=1, source_target_pairs={{0,1},{1,2},{2,3},{4,5},{5,6},{6,7},{8,9},{9,10},{10,11},{12,13},{... | collective-permute-start | bytes 393224 | tf_op jit(solution)/shard_map/ppermute | solution.py:13
  22.7 1.9 copy-start.4
  22.7 1.9 copy-start.17
  24.6 1.5 copy-start.6
  24.6 2.2 copy-start.11
  29.1 15.0 %all-to-all-start = ((bf16[4,64,8,128]{3,1,2,0:T(8,128)(2,1)}), bf16[4,64,8,128]{3,1,2,0:T(8,128)(2,1)S(1)}, u32[]{:S(2)}, u32[]{:S(2)}) async-start(bf16[4,64,8,128]{3,1,2,0:T(8,128)(2,1)} %get-tuple-element.11), calls=%async_computation | async-start | bytes 1048576 | tf_op jit(solution)/shard_map/all_to_all | solution.py:110
  34.9 9.2 %copy-start.15 = (pred[128,288]{0,1:T(8,128)(4,1)}, pred[128,288]{0,1:T(8,128)(4,1)S(1)}, u32[]{:S(2)}) copy-start(pred[128,288]{0,1:T(8,128)(4,1)S(1)} %constant_dynamic-update-slice_fusion) | copy-start | bytes 110596
  47.5 4.9 %copy-start = (bf16[1,64,16,288]{1,3,2,0:T(8,128)(2,1)}, bf16[1,64,16,288]{1,3,2,0:T(8,128)(2,1)S(1)}, u32[]{:S(2)}) copy-start(bf16[1,64,16,288]{1,3,2,0:T(8,128)(2,1)S(1)} %copy.55) | copy-start | bytes 1769476
  49.5 4.1 %copy-start.2 = (bf16[1,64,16,288]{1,3,2,0:T(8,128)(2,1)}, bf16[1,64,16,288]{1,3,2,0:T(8,128)(2,1)S(1)}, u32[]{:S(2)}) copy-start(bf16[1,64,16,288]{1,3,2,0:T(8,128)(2,1)S(1)} %copy.54) | copy-start | bytes 1769476
  49.5 2.9 copy-start.13
  49.5 2.9 copy-start.18
  53.6 5.1 %copy-start.9 = (bf16[1,128,16,32]{1,3,2,0:T(8,128)(2,1)}, bf16[1,128,16,32]{1,3,2,0:T(8,128)(2,1)S(1)}, u32[]{:S(2)}) copy-start(bf16[1,128,16,32]{1,3,2,0:T(8,128)(2,1)S(1)} %get-tuple-element.13) | copy-start | bytes 393220
  66.4 2.3 copy-start.8
  68.9 0.8 copy-start.16
  69.7 7.5 %copy-start.3 = (bf16[1,64,16,288]{1,3,2,0:T(8,128)(2,1)S(1)}, bf16[1,64,16,288]{1,3,2,0:T(8,128)(2,1)}, u32[]{:S(2)}) copy-start(bf16[1,64,16,288]{1,3,2,0:T(8,128)(2,1)} %copy-done.2) | copy-start | bytes 1769476
  69.7 7.5 %copy-start.10 = (bf16[1,128,16,32]{1,3,2,0:T(8,128)(2,1)S(1)}, bf16[1,128,16,32]{1,3,2,0:T(8,128)(2,1)}, u32[]{:S(2)}) copy-start(bf16[1,128,16,32]{1,3,2,0:T(8,128)(2,1)} %copy-done.9) | copy-start | bytes 393220
  71.3 6.5 %copy-start.1 = (bf16[1,64,16,288]{1,3,2,0:T(8,128)(2,1)S(1)}, bf16[1,64,16,288]{1,3,2,0:T(8,128)(2,1)}, u32[]{:S(2)}) copy-start(bf16[1,64,16,288]{1,3,2,0:T(8,128)(2,1)} %copy-done) | copy-start | bytes 1769476
  72.2 14.5 %all-to-all-start.1 = ((bf16[1,64,32,128]{3,1,0,2:T(8,128)(2,1)}), bf16[1,64,32,128]{3,1,0,2:T(8,128)(2,1)}, u32[]{:S(2)}, u32[]{:S(2)}) async-start(bf16[1,64,32,128]{3,1,0,2:T(8,128)(2,1)} %slice_bitcast_fusion), calls=%async_computation.1 | async-start | bytes 1048576 | tf_op jit(solution)/shard_map/all_to_all | solution.py:121
  77.2 277.0 %all-reduce.6.cloned.1.call-start = ((), (), s32[]{:S(2)}) async-start(), calls=%async_computation.2 | async-start | bytes 2654208 | tf_op jit(solution)/shard_map/psum | solution.py:124
  77.7 10.7 %copy-start.7 = (bf16[4,32,8,9,128]{4,2,3,1,0:T(8,128)(2,1)S(1)}, bf16[4,32,8,9,128]{4,2,3,1,0:T(8,128)(2,1)}, u32[]{:S(2)}) copy-start(bf16[4,32,8,9,128]{4,2,3,1,0:T(8,128)(2,1)} %copy-done.6) | copy-start | bytes 7077892
  88.4 1.7 copy-start.12
  90.1 1.7 copy-start.5
  91.8 1.6 copy-start.14
Sparse Core Ops, SparseCore 0:
  93.5 260.6 all-reduce.5
where the time goes:
time: 366 us; the launch traced here: 365 us
  waiting for transfers between devices  275 us (75%)
  local copies, waits for them, and re-layouts  25.8 us (7%)
  matrix products  24.6 us (7%)
  starting transfers between devices  16.7 us (5%)
  between operations  14.5 us (4%)
  other arithmetic  8.36 us (2%)
    psum x1, waiting for transfers between devices, per_device(): lax.psum(scale * kernel_grad(first_planes, delta_first), ('dp', 'space'))  260 us
    unnamed x41, local copies, waits for them, and re-layouts  9.79 us
    all_to_all x1, waiting for transfers between devices, per_device(): lax.all_to_all(hidden, 'space', split_axis=0, concat_axis=2, tiled=True)  9.19 us
    dot_general x6, matrix products, forward_conv(): jnp.einsum('scxtm,tco->soxm', rows, kernel[9 * first:9 * first + 9], pref...  7.8 us
  transfers between devices with their start and end apart: 4, of which 4 were waited for; matrix products, arithmetic and copies ran while one was open for 2% of the time, Pallas kernels for 0%

commit v1 on v0

--- a/solution.py
+++ b/solution.py
@@ -1,10 +1,13 @@
 import jax
 import jax.numpy as jnp
 from jax import lax
+from jax.sharding import Mesh
 from jax.sharding import PartitionSpec as P
 
 YD = 32
 ZD = 16
+DP = ("y", "z", "xl")
+SPACE = ("xh", "c")
 
 
 def shifted(value, axis, steps):
@@ -95,19 +98,59 @@
     return jnp.dot(grad_planes, table.T.astype(jnp.float32), precision=lax.Precision.HIGHEST)
 
 
+X_GROUP = ("xl", "xh", "c")
+LANES = 128
+ROWS = 2304
+
+
+def exchange(chunks, axis):
+    return lax.all_to_all(chunks, axis, split_axis=0, concat_axis=0, tiled=True)
+
+
+def reduce_stage(rows, axis, parts):
+    got = exchange(rows.reshape(parts, -1, LANES), axis)
+    return jnp.sum(got.astype(jnp.float32), 0).astype(jnp.bfloat16)
+
+
+def gather_stage(rows, axis, parts):
+    copies = jnp.broadcast_to(rows[None], (parts,) + rows.shape)
+    return exchange(copies, axis).reshape(-1, LANES)
+
+
+def sum_everywhere(first_term, second_term):
+    taps, ins, outs = first_term.shape
+    flat = first_term.reshape(taps * ins, outs)
+    half = flat.shape[0] // 2
+    packed = jnp.concatenate([flat[:half], flat[half:]], 1)
+    wide = second_term.reshape(-1, LANES)
+    used = half + wide.shape[0]
+    pad = jnp.zeros((ROWS - used, LANES), jnp.float32)
+    rows = jnp.concatenate([wide, packed, pad], 0).astype(jnp.bfloat16)
+    rows = reduce_stage(rows, X_GROUP, 8)
+    rows = reduce_stage(rows, "y", 4)
+    got = exchange(jnp.broadcast_to(rows[None], (8,) + rows.shape), "z")
+    rows = jnp.sum(got.astype(jnp.float32), 0).astype(jnp.bfloat16)
+    rows = gather_stage(rows, "y", 4)
+    rows = gather_stage(rows, X_GROUP, 8).astype(jnp.float32)
+    second = rows[: wide.shape[0]].reshape(second_term.shape)
+    packed = rows[wide.shape[0] : used]
+    flat = jnp.concatenate([packed[:, :outs], packed[:, outs:]], 0)
+    return flat.reshape(first_term.shape), second
+
+
 def per_device(volumes, first_kernel, second_kernel, upstream):
     group = volumes.shape[0]
     rows_in = volumes.shape[2]
     mid_ch = first_kernel.shape[2]
-    scale = 1.0 / (group * lax.axis_size("dp"))
+    scale = 1.0 / (group * lax.axis_size(DP))
     first_table = plane_table(YD, ZD)
     second_table = plane_table(YD // 2, ZD // 2)
-    rim = shifted(volumes[:, :, -1:, :], "space", 1)
+    rim = shifted(volumes[:, :, -1:, :], SPACE, 1)
     padded = jnp.concatenate([rim, volumes], 2)
     first_planes = tap_planes(padded, first_table)
     pre_first = forward_conv(first_planes, first_kernel, rows_in // 2)
     hidden = smooth_act(pre_first).astype(jnp.bfloat16)
-    whole = lax.all_to_all(hidden, "space", split_axis=0, concat_axis=2, tiled=True)
+    whole = lax.all_to_all(hidden, SPACE, split_axis=0, concat_axis=2, tiled=True)
     full_rows = whole.shape[2]
     zero_layer = jnp.zeros((whole.shape[0], mid_ch, 1, whole.shape[3]), jnp.bfloat16)
     hidden_pad = jnp.concatenate([zero_layer, whole], 2)
@@ -118,16 +161,17 @@
     second_term = scale * kernel_grad(second_planes, delta_second)
     back = input_grad(delta_second, second_kernel, second_table)
     back_whole = back[:, :, 1:].astype(jnp.bfloat16)
-    back_hidden = lax.all_to_all(back_whole, "space", split_axis=2, concat_axis=0, tiled=True)
-    second_grad = lax.psum(second_term, ("dp", "space"))
+    back_hidden = lax.all_to_all(back_whole, SPACE, split_axis=2, concat_axis=0, tiled=True)
     delta_first = (back_hidden.astype(jnp.float32) * smooth_slope(pre_first)).astype(jnp.bfloat16)
-    first_grad = lax.psum(scale * kernel_grad(first_planes, delta_first), ("dp", "space"))
+    first_term = scale * kernel_grad(first_planes, delta_first)
+    first_grad, second_grad = sum_everywhere(first_term, second_term)
     return (features, first_grad, second_grad)
 
 
 def solution(mesh):
-    in_specs = (P("dp", None, "space", None), P(), P(), P(("dp", "space"), None, None, None))
-    out_specs = (P(("dp", "space"), None, None, None), P(), P())
+    fine = Mesh(mesh.devices.reshape(4, 8, 2, 2, 2), ("y", "z", "xl", "xh", "c"))
+    in_specs = (P(DP, None, SPACE, None), P(), P(), P(DP + SPACE, None, None, None))
+    out_specs = (P(DP + SPACE, None, None, None), P(), P())
     return jax.shard_map(
-        per_device, mesh=mesh, in_specs=in_specs, out_specs=out_specs, check_vma=False
+        per_device, mesh=fine, in_specs=in_specs, out_specs=out_specs, check_vma=False
     )

time: 366 us -> 151 us (0.41)
  waiting for transfers between devices: 275 us -> 24.9 us
  blocking collectives: 0 us -> 45.2 us
  between operations: 14.5 us -> 1.17 us
  starting transfers between devices: 16.7 us -> 24.2 us
  local copies, waits for them, and re-layouts: 25.8 us -> 21.7 us
    psum x1 -> x0, waiting for transfers between devices: 260 us -> none  [per_device(): lax.psum(scale * kernel_grad(first_planes, delta_first), ('dp', 'space'))]
    all_to_all x0 -> x4, blocking collectives: none -> 45.2 us  [exchange(): return lax.all_to_all(chunks, axis, split_axis=0, concat_axis=0, tiled=True)]
    all_to_all x2 -> x3, waiting for transfers between devices: 14.6 us -> 24.5 us  [the longest x1 9.19 us: per_device(): lax.all_to_all(hidden, SPACE, split_axis=0, concat_axis=2, tiled=True)]
    all_to_all x2 -> x3, starting transfers between devices: 10.7 us -> 18.1 us  [the longest x1 8.12 us: exchange(): return lax.all_to_all(chunks, axis, split_axis=0, concat_axis=0, tiled=True)]
    unnamed x41 -> x29, local copies, waits for them, and re-layouts: 9.79 us -> 5.32 us
  transfers between devices with their start and end apart: 4 -> 4, of which waited for: 4 -> 4; matrix products, arithmetic and copies ran while one was open for 2% -> 3% of each run, Pallas kernels for 0% -> 0%
where the time goes in v1:
time: 151 us; the launch traced here: 150 us
  blocking collectives  45.2 us (30%)
  waiting for transfers between devices  24.9 us (16%)
  starting transfers between devices  24.2 us (16%)
  matrix products  24.2 us (16%)
  local copies, waits for them, and re-layouts  21.7 us (14%)
  other arithmetic  8.89 us (6%)
    all_to_all x4, blocking collectives, exchange(): return lax.all_to_all(chunks, axis, split_axis=0, concat_axis=0, tiled=True)  45.2 us
    all_to_all x1, waiting for transfers between devices, per_device(): lax.all_to_all(hidden, SPACE, split_axis=0, concat_axis=2, tiled=True)  9.19 us
    all_to_all x1, waiting for transfers between devices, exchange(): return lax.all_to_all(chunks, axis, split_axis=0, concat_axis=0, tiled=True)  8.52 us
    all_to_all x1, starting transfers between devices, exchange(): return lax.all_to_all(chunks, axis, split_axis=0, concat_axis=0, tiled=True)  8.12 us
    dot_general x6, matrix products, forward_conv(): jnp.einsum('scxtm,tco->soxm', rows, kernel[9 * first:9 * first + 9], pref...  7.63 us
    all_to_all x1, waiting for transfers between devices, per_device(): lax.all_to_all(back_whole, SPACE, split_axis=2, concat_axis=0, tiled=True)  6.78 us
    ppermute x1, starting transfers between devices, shifted(): lax.ppermute(value, axis, [(source, source + steps) for source in range(i...  6.03 us
    dot_general x6, matrix products, kernel_grad(): jnp.einsum('scxtm,soxm->tco', rows, delta, preferred_element_type=jnp.flo...  5.9 us
  transfers between devices with their start and end apart: 4, of which 4 were waited for; matrix products, arithmetic and copies ran while one was open for 3% of the time, Pallas kernels for 0%

profile of v1, /device:TPU:1, one launch (start us, length us, event | category | flops | bytes accessed | tf_op | source)
XLA Modules:
  0.0 150.2 jit_solution(13719015900625374975)
XLA Ops:
  0.6 2.8 %copy.67 = bf16[4,32,16,512]{3,1,2,0:T(8,128)(2,1)S(1)} copy(bf16[4,32,16,512]{3,2,1,0:T(8,128)(2,1)} %param.4) | data formatting | bytes 4194304 | tf_op args[0]
  3.4 6.0 %collective-permute-start = (bf16[4,32,1,512]{3,1,2,0:T(8,128)(2,1)S(1)}, bf16[4,32,1,512]{3,1,2,0:T(8,128)(2,1)S(1)}, u32[]{:S(2)}, u32[]{:S(2)}) collective-permute-start(bf16[4,32,1,512]{3,1,2,0:T(8,128)(2,1)S(1)} %slice.100), channel_id=1, source_target_pairs={{0,1},{1,2},{2,3},{4,5},{5,6},{6,7},{8,9},{9,10},{10,11},{12,13},{... | collective-permute-start | bytes 393224 | tf_op jit(solution)/shard_map/ppermute | solution.py:16
  11.4 3.3 %fusion.15 = bf16[4,32,17,1152]{3,1,2,0:T(8,128)(2,1)S(1)} fusion(pred[512,1152]{1,0:T(8,128)(4,1)S(1)} %fusion.77, bf16[4,32,16,512]{3,1,2,0:T(8,128)(2,1)S(1)} %copy.67, bf16[4,32,1,512]{3,1,2,0:T(8,128)(2,1)S(1)} %collective-permute-done), kind=kOutput, calls=%fused_computation.21 | convolution fusion | flops 2568028160 | bytes 7831552 | tf_op jit(solution)/shard_map/dot_general | solution.py:45
  16.2 1.8 %copy_bitcast_fusion = (bf16[4,32,8,9,128]{4,2,3,1,0:T(8,128)(2,1)S(1)}, bf16[4,32,8,9,128]{4,2,3,1,0:T(8,128)(2,1)S(1)}) fusion(bf16[4,32,8,1152]{3,1,2,0:T(8,128)(2,1)S(1)} %get-tuple-element.3, bf16[4,32,8,1152]{3,1,2,0:T(8,128)(2,1)S(1)} %get-tuple-element.4), kind=kLoop, calls=%fused_computation.14 | loop fusion | bytes 9437184 | tf_op jit(solution)/shard_map/reshape | solution.py:51
  20.2 2.4 %fusion.56 = (bf16[4,64,8,128]{3,1,2,0:T(8,128)(2,1)}, f32[4,64,8,128]{3,1,2,0:T(8,128)}) fusion(f32[4,8,128,64]{2,3,1,0:T(8,128)S(1)} %fusion.37, bf16[27,32,64]{2,1,0:T(8,128)(2,1)S(1)} %copy-done.12, bf16[4,32,8,9,128]{4,2,3,1,0:T(8,128)(2,1)S(1)} %get-tuple-element.17), kind=kOutput, calls=%fused_computation.53 | convolution fusion | flops 153878528 | bytes 5054464 | tf_op jit(solution)/shard_map/scxtm,tco->soxm/dot_general | solution.py:58
  22.5 5.6 %all-to-all-start = ((bf16[4,64,8,128]{3,1,2,0:T(8,128)(2,1)}), bf16[4,64,8,128]{3,1,2,0:T(8,128)(2,1)S(1)}, u32[]{:S(2)}, u32[]{:S(2)}) async-start(bf16[4,64,8,128]{3,1,2,0:T(8,128)(2,1)} %get-tuple-element.13), calls=%async_computation | async-start | bytes 1048576 | tf_op jit(solution)/shard_map/all_to_all | solution.py:153
  28.3 9.2 %all-to-all-done = bf16[4,64,8,128]{3,1,2,0:T(8,128)(2,1)S(1)} async-done(((bf16[4,64,8,128]{3,1,2,0:T(8,128)(2,1)}), bf16[4,64,8,128]{3,1,2,0:T(8,128)(2,1)S(1)}, u32[]{:S(2)}, u32[]{:S(2)}) %all-to-all-start) | async-done | bytes 524320 | tf_op jit(solution)/shard_map/all_to_all | solution.py:153
  46.7 1.9 %fusion.84 = f32[16,32,9,64]{3,1,2,0:T(8,128)} fusion(bf16[1,128,16,32]{1,3,2,0:T(8,128)(2,1)S(1)} %get-tuple-element.15, bf16[27,64,128]{2,1,0:T(8,128)(2,1)S(1)} %copy-done.9), kind=kOutput, calls=%fused_computation.98 | convolution fusion | flops 75497472 | bytes 1458176 | tf_op jit(solution)/shard_map/soxm,tco->scxtm/dot_general | solution.py:85
  48.6 2.0 %fusion.78 = f32[16,32,9,64]{3,1,2,0:T(8,128)} fusion(bf16[1,128,16,32]{1,3,2,0:T(8,128)(2,1)S(1)} %get-tuple-element.15, bf16[27,64,128]{2,1,0:T(8,128)(2,1)S(1)} %copy-done.9), kind=kOutput, calls=%fused_computation.92 | convolution fusion | flops 75497472 | bytes 1458176 | tf_op jit(solution)/shard_map/soxm,tco->scxtm/dot_general | solution.py:85
  50.5 2.2 %copy.81 = f32[1,64,16,288]{3,1,2,0:T(8,128)S(1)} copy(f32[1,64,16,288]{1,3,2,0:T(8,128)} %bitcast.237) | data formatting | bytes 2359296 | tf_op jit(solution)/shard_map/reshape | solution.py:91
  52.7 2.2 %copy.82 = f32[1,64,16,288]{3,1,2,0:T(8,128)S(1)} copy(f32[1,64,16,288]{1,3,2,0:T(8,128)} %bitcast.236) | data formatting | bytes 2359296 | tf_op jit(solution)/shard_map/reshape | solution.py:91
  57.7 2.0 %copy.83 = f32[1,64,16,1,288]{4,1,2,3,0:T(8,128)} copy(f32[1,64,16,1,288]{1,4,2,3,0:T(8,128)S(1)} %bitcast.238) | data formatting | bytes 2359296 | tf_op jit(solution)/shard_map/stack;reshape | solution.py:94
  59.8 2.1 %pad_maximum_fusion = f32[1,64,16,2,288]{4,1,2,3,0:T(8,128)S(1)} fusion(f32[1,64,16,1,288]{4,1,2,3,0:T(8,128)} %copy.83, f32[1,64,16,1,288]{4,1,2,3,0:T(8,128)} %fusion.21), kind=kLoop, calls=%fused_computation.4 | loop fusion | flops 589824 | bytes 4718592 | tf_op jit(solution)/shard_map/stack | solution.py:94
  62.2 1.6 %fusion.41 = bf16[1,64,33,128]{3,1,2,0:T(8,128)(2,1)S(1)} fusion(f32[1,64,1,288]{3,1,2,0:T(8,128)S(1)} %pad_add_fusion, f32[1,64,32,288]{3,1,2,0:T(8,128)S(1)} %bitcast.229, pred[128,288]{0,1:T(8,128)(4,1)S(1)} %constant_dynamic-update-slice_fusion), kind=kOutput, calls=%fused_computation.38 | convolution fusion | flops 935159808 | bytes 3010560 | tf_op jit(solution)/shard_map/dot_general | solution.py:98
  64.6 4.4 %all-to-all-start.1 = ((bf16[1,64,32,128]{3,1,0,2:T(8,128)(2,1)}), bf16[1,64,32,128]{3,1,0,2:T(8,128)(2,1)S(1)}, u32[]{:S(2)}, u32[]{:S(2)}) async-start(bf16[1,64,32,128]{3,1,0,2:T(8,128)(2,1)} %slice_bitcast_fusion), calls=%async_computation.1 | async-start | bytes 1048576 | tf_op jit(solution)/shard_map/all_to_all | solution.py:164
  69.5 1.9 %convolution_bitcast_fusion.3 = f32[9,64,128]{2,1,0:T(8,128)S(1)} fusion(bf16[64,16,9,32]{0,3,2,1:T(8,128)(2,1)} %bitcast.239, bf16[1,128,16,32]{1,3,2,0:T(8,128)(2,1)S(1)} %get-tuple-element.15), kind=kOutput, calls=%fused_computation.41 | convolution fusion | flops 75497472 | bytes 1015808 | tf_op jit(solution)/shard_map/scxtm,soxm->tco/dot_general | solution.py:74
  71.6 6.8 %all-to-all-done.1 = bf16[1,64,32,128]{3,1,0,2:T(8,128)(2,1)S(1)} async-done(((bf16[1,64,32,128]{3,1,0,2:T(8,128)(2,1)}), bf16[1,64,32,128]{3,1,0,2:T(8,128)(2,1)S(1)}, u32[]{:S(2)}, u32[]{:S(2)}) %all-to-all-start.1) | async-done | bytes 524320 | tf_op jit(solution)/shard_map/all_to_all | solution.py:164
  78.4 1.6 %fusion.57 = bf16[4,64,8,128]{3,1,2,0:T(8,128)(2,1)S(1)} fusion(bf16[1,64,4,8,128]{4,1,3,2,0:T(8,128)(2,1)S(1)} %bitcast.243, f32[4,64,8,128]{3,1,2,0:T(8,128)} %get-tuple-element.14), kind=kLoop, calls=%fused_computation.55 | loop fusion | flops 2097152 | bytes 2097152 | tf_op jit(solution)/shard_map/convert_element_type | solution.py:165
  84.5 13.6 %all_to_all.52 = bf16[8,288,128]{2,1,0:T(8,128)(2,1)S(1)} all-to-all(bf16[8,288,128]{2,1,0:T(8,128)(2,1)S(1)} %bitcast.241), channel_id=1, replica_groups=mesh['y'=4,'z'=8,'xl'=2,'xh'=2,'c'=2] {'xl','xh','c'}, dimensions={0} | all-to-all | bytes 1179648 | tf_op jit(solution)/shard_map/all_to_all | solution.py:107
  98.2 8.5 %all_to_all.53 = bf16[4,72,128]{2,1,0:T(8,128)(2,1)S(1)} all-to-all(bf16[4,72,128]{2,1,0:T(8,128)(2,1)S(1)} %bitcast.249), channel_id=1, replica_groups=mesh['y'=4,'z'=8,'xl'=2,'xh'=2,'c'=2] {'y'}, dimensions={0} | all-to-all | bytes 147456 | tf_op jit(solution)/shard_map/all_to_all | solution.py:107
  106.8 16.2 %all_to_all.54 = bf16[8,72,128]{2,1,0:T(8,128)(2,1)S(1)} all-to-all(bf16[8,72,128]{2,1,0:T(8,128)(2,1)S(1)} %broadcast_in_dim.31), channel_id=1, replica_groups=mesh['y'=4,'z'=8,'xl'=2,'xh'=2,'c'=2] {'z'}, dimensions={0} | all-to-all | bytes 294912 | tf_op jit(solution)/shard_map/all_to_all | solution.py:107
  123.0 6.9 %all_to_all.55 = bf16[4,72,128]{2,1,0:T(8,128)(2,1)S(1)} all-to-all(bf16[4,72,128]{2,1,0:T(8,128)(2,1)S(1)} %broadcast_in_dim.32), channel_id=1, replica_groups=mesh['y'=4,'z'=8,'xl'=2,'xh'=2,'c'=2] {'y'}, dimensions={0} | all-to-all | bytes 147456 | tf_op jit(solution)/shard_map/all_to_all | solution.py:107
  130.8 8.1 %all-to-all-start.6 = ((bf16[8,288,128]{2,1,0:T(8,128)(2,1)}), bf16[8,288,128]{2,1,0:T(8,128)(2,1)S(1)}, u32[]{:S(2)}, u32[]{:S(2)}) async-start(bf16[8,288,128]{2,1,0:T(8,128)(2,1)} %broadcast_in_dim.34), calls=%async_computation.6 | async-start | bytes 1179648 | tf_op jit(solution)/shard_map/all_to_all | solution.py:107
  139.7 8.5 %all-to-all-done.6 = bf16[8,288,128]{2,1,0:T(8,128)(2,1)S(1)} async-done(((bf16[8,288,128]{2,1,0:T(8,128)(2,1)}), bf16[8,288,128]{2,1,0:T(8,128)(2,1)S(1)}, u32[]{:S(2)}, u32[]{:S(2)}) %all-to-all-start.6) | async-done | bytes 589856 | tf_op jit(solution)/shard_map/all_to_all | solution.py:107
  (105 shorter events, 27.5 us)
Async XLA Ops:
  3.4 8.0 %collective-permute-start = (bf16[4,32,1,512]{3,1,2,0:T(8,128)(2,1)S(1)}, bf16[4,32,1,512]{3,1,2,0:T(8,128)(2,1)S(1)}, u32[]{:S(2)}, u32[]{:S(2)}) collective-permute-start(bf16[4,32,1,512]{3,1,2,0:T(8,128)(2,1)S(1)} %slice.100), channel_id=1, source_target_pairs={{0,1},{1,2},{2,3},{4,5},{5,6},{6,7},{8,9},{9,10},{10,11},{12,13},{... | collective-permute-start | bytes 393224 | tf_op jit(solution)/shard_map/ppermute | solution.py:16
  16.2 1.9 %copy-start.2 = (bf16[4,32,8,1152]{3,2,1,0:T(8,128)(2,1)}, bf16[4,32,8,1152]{3,2,1,0:T(8,128)(2,1)S(1)}, u32[]{:S(2)}) copy-start(bf16[4,32,8,1152]{3,2,1,0:T(8,128)(2,1)S(1)} %copy.142) | copy-start | bytes 7077892
  16.2 1.9 %copy-start.12 = (bf16[27,32,64]{2,1,0:T(8,128)(2,1)S(1)}, bf16[27,32,64]{2,1,0:T(8,128)(2,1)}, u32[]{:S(2)}) copy-start(bf16[27,32,64]{2,1,0:T(8,128)(2,1)} %param.5) | copy-start | bytes 331780
  18.0 1.4 copy-start.4
  18.0 2.1 %copy-start.7 = (bf16[4,32,8,9,128]{4,2,3,1,0:T(8,128)(2,1)}, bf16[4,32,8,9,128]{4,2,3,1,0:T(8,128)(2,1)S(1)}, u32[]{:S(2)}) copy-start(bf16[4,32,8,9,128]{4,2,3,1,0:T(8,128)(2,1)S(1)} %get-tuple-element.17) | copy-start | bytes 7077892
  22.5 15.0 %all-to-all-start = ((bf16[4,64,8,128]{3,1,2,0:T(8,128)(2,1)}), bf16[4,64,8,128]{3,1,2,0:T(8,128)(2,1)S(1)}, u32[]{:S(2)}, u32[]{:S(2)}) async-start(bf16[4,64,8,128]{3,1,2,0:T(8,128)(2,1)} %get-tuple-element.13), calls=%async_computation | async-start | bytes 1048576 | tf_op jit(solution)/shard_map/all_to_all | solution.py:153
  40.7 3.6 %copy-start = (bf16[1,64,16,288]{1,3,2,0:T(8,128)(2,1)}, bf16[1,64,16,288]{1,3,2,0:T(8,128)(2,1)S(1)}, u32[]{:S(2)}) copy-start(bf16[1,64,16,288]{1,3,2,0:T(8,128)(2,1)S(1)} %copy.77) | copy-start | bytes 1769476
  40.7 3.6 %copy-start.13 = (bf16[1,128,16,32]{1,3,2,0:T(8,128)(2,1)S(1)}, bf16[1,128,16,32]{1,3,2,0:T(8,128)(2,1)}, u32[]{:S(2)}) copy-start(bf16[1,128,16,32]{1,3,2,0:T(8,128)(2,1)} %param.7) | copy-start | bytes 393220
  41.5 2.8 %copy-start.6 = (bf16[1,64,16,288]{1,3,2,0:T(8,128)(2,1)S(1)}, bf16[1,64,16,288]{1,3,2,0:T(8,128)(2,1)}, u32[]{:S(2)}) copy-start(bf16[1,64,16,288]{1,3,2,0:T(8,128)(2,1)} %copy.75) | copy-start | bytes 1769476
  41.5 2.8 %copy-start.9 = (bf16[27,64,128]{2,1,0:T(8,128)(2,1)S(1)}, bf16[27,64,128]{2,1,0:T(8,128)(2,1)}, u32[]{:S(2)}) copy-start(bf16[27,64,128]{2,1,0:T(8,128)(2,1)} %param.6) | copy-start | bytes 1327108
  62.2 6.8 %copy-start.1 = (bf16[1,64,16,288]{1,3,2,0:T(8,128)(2,1)S(1)}, bf16[1,64,16,288]{1,3,2,0:T(8,128)(2,1)}, u32[]{:S(2)}) copy-start(bf16[1,64,16,288]{1,3,2,0:T(8,128)(2,1)} %copy-done) | copy-start | bytes 1769476
  64.6 13.8 %all-to-all-start.1 = ((bf16[1,64,32,128]{3,1,0,2:T(8,128)(2,1)}), bf16[1,64,32,128]{3,1,0,2:T(8,128)(2,1)S(1)}, u32[]{:S(2)}, u32[]{:S(2)}) async-start(bf16[1,64,32,128]{3,1,0,2:T(8,128)(2,1)} %slice_bitcast_fusion), calls=%async_computation.1 | async-start | bytes 1048576 | tf_op jit(solution)/shard_map/all_to_all | solution.py:164
  69.0 2.5 %copy-start.10 = (f32[9,64,128]{2,1,0:T(8,128)S(1)}, f32[9,64,128]{2,1,0:T(8,128)}, u32[]{:S(2)}) copy-start(f32[9,64,128]{2,1,0:T(8,128)} %convolution_bitcast_fusion.2) | copy-start | bytes 884740
  69.5 10.4 %copy-start.5 = (bf16[4,32,8,9,128]{4,2,3,1,0:T(8,128)(2,1)S(1)}, bf16[4,32,8,9,128]{4,2,3,1,0:T(8,128)(2,1)}, u32[]{:S(2)}) copy-start(bf16[4,32,8,9,128]{4,2,3,1,0:T(8,128)(2,1)} %copy-done.4) | copy-start | bytes 7077892
  79.9 1.7 %copy-start.8 = (bf16[4,32,8,9,128]{4,2,3,1,0:T(8,128)(2,1)S(1)}, bf16[4,32,8,9,128]{4,2,3,1,0:T(8,128)(2,1)}, u32[]{:S(2)}) copy-start(bf16[4,32,8,9,128]{4,2,3,1,0:T(8,128)(2,1)} %copy-done.7) | copy-start | bytes 7077892
  81.6 1.7 %copy-start.3 = (bf16[4,32,8,1152]{3,2,1,0:T(8,128)(2,1)S(1)}, bf16[4,32,8,1152]{3,2,1,0:T(8,128)(2,1)}, u32[]{:S(2)}) copy-start(bf16[4,32,8,1152]{3,2,1,0:T(8,128)(2,1)} %copy-done.2) | copy-start | bytes 7077892
  84.5 54.4 %copy-start.11 = (f32[128,16,32]{0,2,1:T(8,128)S(1)}, f32[128,16,32]{0,2,1:T(8,128)}, u32[]{:S(2)}) copy-start(f32[128,16,32]{0,2,1:T(8,128)} %get-tuple-element.16) | copy-start | bytes 786436
  130.8 17.5 %all-to-all-start.6 = ((bf16[8,288,128]{2,1,0:T(8,128)(2,1)}), bf16[8,288,128]{2,1,0:T(8,128)(2,1)S(1)}, u32[]{:S(2)}, u32[]{:S(2)}) async-start(bf16[8,288,128]{2,1,0:T(8,128)(2,1)} %broadcast_in_dim.34), calls=%async_computation.6 | async-start | bytes 1179648 | tf_op jit(solution)/shard_map/all_to_all | solution.py:107

commit v2 on v0

v2 whole, which is shorter than its diff:
```python
import jax
import jax.numpy as jnp
import numpy as np
from jax import lax
from jax.experimental import pallas as pl
from jax.experimental.pallas import tpu as pltpu
from jax.sharding import Mesh
from jax.sharding import PartitionSpec as P

YD = 32
ZD = 16
LANES = 128
DP = ("y", "z", "xl")
SPACE = ("xh", "c")
X_GROUP = ("xl", "xh", "c")
BF = jnp.bfloat16
F32 = jnp.float32
INTERPRET = False


def shifted(value, axis, steps):
    count = lax.axis_size(axis)
    initial, last = (max(0, -steps), min(count, count - steps))
    return lax.ppermute(value, axis, [(source, source + steps) for source in range(initial, last)])


def plane_table(size_y, size_z, copies):
    half_y, half_z = size_y // 2, size_z // 2
    cells = half_y * half_z
    table = np.zeros((copies, size_y * size_z, 9, copies, cells), np.float32)
    for second in range(3):
        for third in range(3):
            for out_y in range(half_y):
                for out_z in range(half_z):
                    y, z = 2 * out_y + second - 1, 2 * out_z + third - 1
                    if y >= 0 and z >= 0:
                        for k in range(copies):
                            table[k, y * size_z + z, 3 * second + third, k, out_y * half_z + out_z] = 1
    return jnp.asarray(table.reshape(copies * size_y * size_z, 9 * copies * cells), BF)


def row_order(chans, rows):
    shape = (rows * chans, chans * rows)
    at = lax.broadcasted_iota(jnp.int32, shape, 0)
    source = lax.broadcasted_iota(jnp.int32, shape, 1)
    block = at // chans
    row = (block % (rows // 2)) * 2 + block // (rows // 2)
    return (source == (at % chans) * rows + row).astype(F32).astype(BF)


def turned(value):
    size = value.shape[1]
    row = lax.broadcasted_iota(jnp.int32, (size, size), 0)
    col = lax.broadcasted_iota(jnp.int32, (size, size), 1)
    return dot_nt((row == col).astype(F32).astype(BF), value)


def dot(a, b):
    return jnp.dot(a, b, preferred_element_type=F32)


def dot_nt(a, b):
    return lax.dot_general(a, b, (((1,), (1,)), ((), ())), preferred_element_type=F32)


def act_and_slope(v):
    e = jnp.exp(-jnp.abs(v))
    act = 0.3 * v + 0.7 * (jnp.maximum(v, 0.0) + jnp.log(1.0 + e))
    slope = 0.3 + 0.7 * jnp.where(v >= 0, 1.0, e) / (1.0 + e)
    return act, slope


def first_body(v_ref, table_ref, w_ref, im_ref, pre_ref, order_ref, wt_ref, z_ref):
    @pl.when(pl.program_id(0) == 0)
    def _():
        order_ref[...] = row_order(32, 16)
        wt_ref[...] = turned(w_ref[...]).astype(BF)

    v = v_ref[0].reshape(512, 512)
    rows = dot(order_ref[...], v).astype(BF)
    z_ref[...] = dot(rows, table_ref[...]).astype(BF)
    for o1 in range(8):
        for a in range(3):
            x = 2 * o1 + a - 1
            for t in range(9):
                if x < 0:
                    block = jnp.zeros((32, LANES), BF)
                else:
                    at = ((x % 2) * 8 + x // 2) * 32
                    block = z_ref[at : at + 32, t * LANES : (t + 1) * LANES]
                k = (9 * a + t) * 32
                im_ref[0, k : k + 32, o1 * LANES : (o1 + 1) * LANES] = block
    pre_ref[0] = dot(wt_ref[...], im_ref[0])


def rim_body(pre_ref, rim_ref, table_ref, w_ref, hid_ref, last_ref, slope_ref, rimz_ref):
    z = dot(rim_ref[...].reshape(128, 512), table_ref[...]).astype(BF)
    wt = turned(w_ref[:288]).astype(BF)
    for s in range(4):
        im = jnp.concatenate(
            [z[32 * s : 32 * s + 32, t * LANES : (t + 1) * LANES] for t in range(9)], 0
        )
        rimz_ref[s] = im
        extra = dot(wt, im)
        for r in range(8):
            lanes = slice(r * LANES, (r + 1) * LANES)
            pre = pre_ref[s, :, lanes]
            if r == 0:
                pre = pre + extra
            act, slope = act_and_slope(pre)
            hidden = act.astype(BF)
            hid_ref[s, :, lanes] = hidden
            slope_ref[s, :, lanes] = slope
            if r == 7:
                last_ref[s] = hidden


def second_body(hid_ref, table_ref, w_ref, im_ref, pre_ref):
    for s in range(4):
        row = lambda r: (
            hid_ref[s, :, r * LANES : (r + 1) * LANES] if r >= 0 else jnp.zeros((64, LANES), BF)
        )
        left = jnp.concatenate(
            [jnp.concatenate([row(2 * o1 + a - 1) for o1 in range(4)], 1) for a in range(3)], 0
        )
        z = dot(left, table_ref[...]).astype(BF)
        for a in range(3):
            for t in range(9):
                k = (9 * a + t) * 64
                im_ref[k : k + 64, s * LANES : (s + 1) * LANES] = z[
                    64 * a : 64 * a + 64, t * LANES : (t + 1) * LANES
                ]
    pre_ref[...] = dot(turned(w_ref[...]).astype(BF), im_ref[...])


def halo_body(halo_ref, pre_ref, up_ref, table_ref, w_ref, feat_ref, delta_ref, edge_ref, imh_ref):
    z = dot(halo_ref[...].reshape(256, LANES), table_ref[:LANES, :]).astype(BF)
    for s in range(4):
        for t in range(9):
            imh_ref[t * 64 : t * 64 + 64, s * LANES : (s + 1) * LANES] = z[
                64 * s : 64 * s + 64, t * LANES : (t + 1) * LANES
            ]
    pre = pre_ref[...] + dot(turned(w_ref[:576]).astype(BF), imh_ref[...])
    lane = lax.broadcasted_iota(jnp.int32, (128, LANES), 1)
    edge = jnp.zeros((128, LANES), F32)
    for s in range(4):
        act, slope = act_and_slope(pre[:, s * LANES : (s + 1) * LANES])
        feat_ref[s] = turned(act.astype(BF)).astype(BF)
        delta = (turned(up_ref[s]) * slope).astype(BF)
        delta_ref[:, s * LANES : (s + 1) * LANES] = delta
        moved = delta.astype(F32)
        if s:
            moved = pltpu.roll(moved, 32 * s, 1)
        edge = jnp.where(lane // 32 == s, moved, edge)
    edge_ref[...] = edge.astype(BF)


def second_grad_body(im_ref, imh_ref, delta_ref, out_ref):
    scale = 1.0 / 256
    delta = delta_ref[...]
    out_ref[:576] = (dot_nt(im_ref[:576] + imh_ref[...], delta) * scale).astype(BF)
    out_ref[576:] = (dot_nt(im_ref[576:], delta) * scale).astype(BF)


def back_body(
    delta_ref, edge_ref, k_ref, table_ref, slope_ref, im_ref, rimz_ref, out_ref, kodd_ref, acc_ref
):
    s = pl.program_id(0)

    @pl.when(s == 0)
    def _():
        acc_ref[...] = jnp.zeros_like(acc_ref)
        kodd_ref[:, :128] = k_ref[:576]
        kodd_ref[:, 128:] = k_ref[1152:]

    lane = lax.broadcasted_iota(jnp.int32, (128, LANES), 1)
    own = delta_ref[...]
    moved = pltpu.roll(own.astype(F32), 96, 1)
    rim = edge_ref[...].astype(F32)
    ends = rim
    for k in range(3):
        ends = jnp.where(s == k, pltpu.roll(rim, 96 - 32 * k, 1), ends)
    ahead = jnp.where(lane < 96, moved, ends).astype(BF)
    even = dot(k_ref[576:1152], own)
    odd = dot(kodd_ref[...], jnp.concatenate([ahead, own], 0))
    parts = []
    for grad in (even, odd):
        flat = jnp.concatenate([grad[64 * t : 64 * t + 64] for t in range(9)], 1)
        high = flat.astype(BF)
        parts += [high, (flat - high.astype(F32)).astype(BF)]
    got = dot_nt(jnp.concatenate(parts, 0), table_ref[...])
    rows = []
    for r in range(8):
        base = 128 * (r % 2)
        lanes = slice((r // 2) * LANES, (r // 2 + 1) * LANES)
        back = (got[base : base + 64, lanes] + got[base + 64 : base + 128, lanes]).astype(BF)
        slope = slope_ref[0, :, r * LANES : (r + 1) * LANES]
        rows.append((back.astype(F32) * slope).astype(BF))
    delta_first = jnp.concatenate(rows, 1)
    term = dot_nt(im_ref[0], delta_first)
    rim_term = dot_nt(rimz_ref[0], rows[0])

    acc_ref[...] += term
    acc_ref[:288] += rim_term

    @pl.when(s == 3)
    def _():
        acc = acc_ref[...] * (1.0 / 256)
        out_ref[...] = jnp.concatenate([acc[:432], acc[432:]], 1).astype(BF)


def finish_body(rows_ref, first_ref, second_ref):
    second_ref[...] = rows_ref[:1728].astype(F32)
    packed = rows_ref[1728:2160].astype(F32)
    first_ref[:432] = packed[:, :64]
    first_ref[432:] = packed[:, 64:]


def call(body, outs, ins=None, grid=(), out_specs=None, scratch=(), mib=16):
    whole = lambda shape: pl.BlockSpec(shape, lambda *_: (0,) * len(shape))

    def run(*args):
        in_specs = [
            whole(arg.shape) if spec is None else spec
            for arg, spec in zip(args, ins or (None,) * len(args))
        ]
        shapes = [
            pltpu.HBM(*out[:2]) if out[2:] and not INTERPRET else jax.ShapeDtypeStruct(*out[:2])
            for out in outs
        ]
        return pl.pallas_call(
            body,
            grid=grid,
            in_specs=in_specs,
            out_specs=out_specs or [whole(out[0]) for out in outs],
            out_shape=shapes,
            scratch_shapes=list(scratch),
            compiler_params=pltpu.CompilerParams(vmem_limit_bytes=mib * 1024 * 1024),
            interpret=INTERPRET,
        )(*args)

    return run


def exchange(chunks, axis):
    return lax.all_to_all(chunks, axis, split_axis=0, concat_axis=0, tiled=True)


def reduce_stage(rows, axis):
    got = exchange(rows.reshape(lax.axis_size(axis), -1, LANES), axis)
    return jnp.sum(got.astype(F32), 0).astype(BF)


def gather_stage(rows, axis):
    copies = jnp.broadcast_to(rows[None], (lax.axis_size(axis),) + rows.shape)
    return exchange(copies, axis).reshape(-1, LANES)


def sum_everywhere(packed, wide, features):
    pad = jnp.zeros((144, LANES), BF)
    rows = jnp.concatenate([wide, packed, pad], 0).reshape(lax.axis_size(X_GROUP), -1, LANES)
    chunk = rows.shape[1]
    twin = lax.axis_size("xl")
    feats = jnp.concatenate([features] * twin, 0)
    got = exchange(jnp.concatenate([rows, feats], 1), X_GROUP)
    mine = lax.dynamic_slice_in_dim(got, 4 * lax.axis_index("xl"), 4, 0)[:, chunk:]
    rows = jnp.sum(got[:, :chunk].astype(F32), 0).astype(BF)
    rows = reduce_stage(rows, "y")
    got = exchange(jnp.broadcast_to(rows[None], (lax.axis_size("z"),) + rows.shape), "z")
    rows = jnp.sum(got.astype(F32), 0).astype(BF)
    rows = gather_stage(rows, "y")
    rows = gather_stage(rows, X_GROUP)
    first, second = call(finish_body, [((864, 64), F32), ((1728, 128), F32)])(rows)
    return first.reshape(27, 32, 64), second.reshape(27, 64, 128), mine


def per_device(volumes, first_kernel, second_kernel, upstream):
    table = plane_table(YD, ZD, 1)
    table2 = plane_table(YD // 2, ZD // 2, 4)
    rim = shifted(volumes[:, :, 15, :], SPACE, 1)
    up = exchange(upstream.reshape(128, 4, 128).transpose(1, 2, 0), SPACE)
    w1 = first_kernel.reshape(864, 64)
    k2 = second_kernel.reshape(1728, 128)
    volumes = pltpu.with_memory_space_constraint(volumes, pltpu.HBM)
    im1, pre1 = call(
        first_body,
        [((4, 864, 1024), BF, True), ((4, 64, 1024), F32)],
        ins=(pl.BlockSpec((1, 32, 16, 512), lambda s: (s, 0, 0, 0)), None, None),
        grid=(4,),
        out_specs=[
            pl.BlockSpec((1, 864, 1024), lambda s: (s, 0, 0)),
            pl.BlockSpec((1, 64, 1024), lambda s: (s, 0, 0)),
        ],
        scratch=[
            pltpu.VMEM((512, 512), BF),
            pltpu.VMEM((64, 864), BF),
            pltpu.VMEM((512, 1152), BF),
        ],
    )(volumes, table, w1)
    hidden, last, slope1, rimz = call(
        rim_body,
        [
            ((4, 64, 1024), BF),
            ((4, 64, 128), BF),
            ((4, 64, 1024), F32, True),
            ((4, 288, 128), BF),
        ],
    )(pre1, rim, table, w1)
    halo = shifted(last, SPACE, 1)
    im2, pre2 = call(second_body, [((1728, 512), BF, True), ((128, 512), F32)])(hidden, table2, k2)
    features, delta2, edge, im2h = call(
        halo_body,
        [((4, 128, 128), BF), ((128, 512), BF), ((128, 128), BF), ((576, 512), BF)],
    )(halo, pre2, up, table2, k2)
    edge = shifted(edge, SPACE, -1)
    (wide,) = call(second_grad_body, [((1728, 128), BF)])(im2, im2h, delta2)
    (packed,) = call(
        back_body,
        [((432, 128), BF)],
        ins=(
            pl.BlockSpec((128, 128), lambda s: (0, s)),
            None,
            None,
            None,
            pl.BlockSpec((1, 64, 1024), lambda s: (s, 0, 0)),
            pl.BlockSpec((1, 864, 1024), lambda s: (s, 0, 0)),
            pl.BlockSpec((1, 288, 128), lambda s: (s, 0, 0)),
        ),
        grid=(4,),
        scratch=[pltpu.VMEM((576, 256), BF), pltpu.VMEM((864, 64), F32)],
    )(delta2, edge, k2, table2, slope1, im1, rimz)
    first_grad, second_grad, features = sum_everywhere(packed, wide, features)
    features = features.transpose(2, 0, 1).reshape(1, 128, 16, 32)
    return (features, first_grad, second_grad)


def solution(mesh):
    fine = Mesh(mesh.devices.reshape(4, 8, 2, 2, 2), ("y", "z", "xl", "xh", "c"))
    in_specs = (P(DP, None, SPACE, None), P(), P(), P(DP + SPACE, None, None, None))
    out_specs = (P(DP + SPACE, None, None, None), P(), P())
    return jax.shard_map(
        per_device, mesh=fine, in_specs=in_specs, out_specs=out_specs, check_vma=False
    )
```

time: 366 us -> 114 us (0.31)
  waiting for transfers between devices: 275 us -> 12.8 us
  blocking collectives: 0 us -> 46.3 us
  matrix products: 24.6 us -> 0 us
  Pallas kernels: 0 us -> 23 us
  local copies, waits for them, and re-layouts: 25.8 us -> 7.25 us
  between operations: 14.5 us -> 0.8 us
  other arithmetic: 8.36 us -> 0.56 us
  starting transfers between devices: 16.7 us -> 23 us
    psum x1 -> x0, waiting for transfers between devices: 260 us -> none  [per_device(): lax.psum(scale * kernel_grad(first_planes, delta_first), ('dp', 'space'))]
    all_to_all x0 -> x4, blocking collectives: none -> 46.3 us  [exchange(): return lax.all_to_all(chunks, axis, split_axis=0, concat_axis=0, tiled=True)]
    dot_general x18 -> x0, matrix products: 24.6 us -> none  [the longest x6 7.8 us: forward_conv(): jnp.einsum('scxtm,tco->soxm', rows, kernel[9 * first:9 * first + 9], pref...]
    pallas_call x0 -> x7, Pallas kernels: none -> 23 us  [run(): pl.pallas_call(body, grid=grid, in_specs=in_specs, out_specs=out_specs or...]
    reshape x3 -> x0, local copies, waits for them, and re-layouts: 6.23 us -> none  [the longest x2 4.41 us: input_grad(): parts.append(term.reshape(group, chans, out_rows, width))]
    all_to_all x2, waiting for transfers between devices: 14.6 us -> 8.7 us  [exchange(): return lax.all_to_all(chunks, axis, split_axis=0, concat_axis=0, tiled=True)]
    unnamed x41 -> x15, local copies, waits for them, and re-layouts: 9.79 us -> 3.98 us
    ppermute x1 -> x3, starting transfers between devices: 6.03 us -> 11.6 us  [shifted(): lax.ppermute(value, axis, [(source, source + steps) for source in range(i...]
  transfers between devices with their start and end apart: 4 -> 5, of which waited for: 4 -> 2; matrix products, arithmetic and copies ran while one was open for 2% -> 1% of each run, Pallas kernels for 0% -> 14%
where the time goes in v2:
time: 114 us
  blocking collectives  46.3 us (41%)
  starting transfers between devices  23 us (20%)
  Pallas kernels  23 us (20%)
  waiting for transfers between devices  12.8 us (11%)
  local copies, waits for them, and re-layouts  7.25 us (6%)
    all_to_all x4, blocking collectives, exchange(): return lax.all_to_all(chunks, axis, split_axis=0, concat_axis=0, tiled=True)  46.3 us
    pallas_call x7, Pallas kernels, run(): pl.pallas_call(body, grid=grid, in_specs=in_specs, out_specs=out_specs or...  23 us
    ppermute x3, starting transfers between devices, shifted(): lax.ppermute(value, axis, [(source, source + steps) for source in range(i...  11.6 us
    all_to_all x2, starting transfers between devices, exchange(): return lax.all_to_all(chunks, axis, split_axis=0, concat_axis=0, tiled=True)  11.5 us
    all_to_all x2, waiting for transfers between devices, exchange(): return lax.all_to_all(chunks, axis, split_axis=0, concat_axis=0, tiled=True)  8.7 us
    ppermute x3, waiting for transfers between devices, shifted(): lax.ppermute(value, axis, [(source, source + steps) for source in range(i...  4.09 us
    unnamed x15, local copies, waits for them, and re-layouts  3.98 us
  transfers between devices with their start and end apart: 5, of which 2 were waited for; matrix products, arithmetic and copies ran while one was open for 1% of the time, Pallas kernels for 14%

profile of v2, /device:TPU:1, one launch (start us, length us, event | category | flops | bytes accessed | tf_op | source)
XLA Modules:
  0.0 113.7 jit_solution(9310636453051617930)
XLA Ops:
  0.6 1.6 %slice.9 = bf16[4,32,1,512]{3,2,1,0:T(2,128)(2,1)S(1)} slice(bf16[4,32,16,512]{3,2,1,0:T(8,128)(2,1)} %v_ref.1), slice={[0:4], [0:32], [15:16], [0:512]} | slice | bytes 262144 | tf_op jit(solution)/shard_map/slice | solution.py:280
  2.3 6.0 %collective-permute-start = (bf16[4,32,512]{2,1,0:T(8,128)(2,1)S(1)}, bf16[4,32,512]{2,1,0:T(8,128)(2,1)S(1)}, u32[]{:S(2)}, u32[]{:S(2)}) collective-permute-start(bf16[4,32,512]{2,1,0:T(8,128)(2,1)S(1)} %bitcast.26), channel_id=1, source_target_pairs={{0,1},{1,2},{2,3},{4,5},{5,6},{6,7},{8,9},{9,10},{10,11},{12,13},{... | collective-permute-start | bytes 393224 | tf_op jit(solution)/shard_map/ppermute | solution.py:24
  8.3 3.3 %all-to-all-start = ((bf16[4,128,128]{2,1,0:T(8,128)(2,1)}), bf16[4,128,128]{2,1,0:T(8,128)(2,1)S(1)}, u32[]{:S(2)}, u32[]{:S(2)}) async-start(bf16[4,128,128]{2,1,0:T(8,128)(2,1)} %bitcast.27), calls=%async_computation | async-start | bytes 262144 | tf_op jit(solution)/shard_map/all_to_all | solution.py:246
  11.7 0.9 copy-done.6
  12.6 10.1 %shard_map.85 = (bf16[4,864,1024]{2,1,0:T(8,128)(2,1)}, f32[4,64,1024]{2,1,0:T(8,128)S(1)}) custom-call(bf16[4,32,16,512]{3,2,1,0:T(8,128)(2,1)} %v_ref.1, bf16[512,1152]{1,0:T(8,128)(2,1)S(1)} %copy-done.2, bf16[864,64]{1,0:T(8,128)(2,1)S(1)} %bitcast.21), custom_call_target="tpu_custom_call" | custom-call | tf_op jit(solution)/shard_map/pallas_call | solution.py:231
  22.7 2.2 %shard_map.86 = (bf16[4,64,1024]{2,1,0:T(8,128)(2,1)S(1)}, bf16[4,64,128]{2,1,0:T(8,128)(2,1)S(1)}, f32[4,64,1024]{2,1,0:T(8,128)}, bf16[4,288,128]{2,1,0:T(8,128)(2,1)S(1)}) custom-call(f32[4,64,1024]{2,1,0:T(8,128)S(1)} %get-tuple-element.17.pre_ref, bf16[4,32,512]{2,1,0:T(8,128)(2,1)S(1)} %collective-permute-done.rim_ref, ...), custom_call_target="tpu_custom_call" | custom-call | tf_op jit(solution)/shard_map/pallas_call | solution.py:231
  24.9 3.5 %collective-permute-start.1 = (bf16[4,64,128]{2,1,0:T(8,128)(2,1)S(1)}, bf16[4,64,128]{2,1,0:T(8,128)(2,1)S(1)}, u32[]{:S(2)}, u32[]{:S(2)}) collective-permute-start(bf16[4,64,128]{2,1,0:T(8,128)(2,1)S(1)} %get-tuple-element.20), channel_id=1, source_target_pairs={{0,1},{1,2},{2,3},{4,5},{5,6},{6,7},{8,9},{9,10},{10,11},{12,13},{... | collective-permute-start | bytes 196616 | tf_op jit(solution)/shard_map/ppermute | solution.py:24
  28.4 2.5 %shard_map.87 = (bf16[1728,512]{1,0:T(8,128)(2,1)}, f32[128,512]{1,0:T(8,128)S(1)}) custom-call(bf16[4,64,1024]{2,1,0:T(8,128)(2,1)S(1)} %get-tuple-element.18.hid_ref, bf16[512,1152]{1,0:T(8,128)(2,1)S(1)} %copy-done, bf16[1728,128]{1,0:T(8,128)(2,1)S(1)} %bitcast.17), custom_call_target="tpu_custom_call" | custom-call | tf_op jit(solution)/shard_map/pallas_call | solution.py:231
  30.9 0.9 shard_map.88
  31.8 2.1 %collective-permute-start.2 = (bf16[128,128]{1,0:T(8,128)(2,1)S(1)}, bf16[128,128]{1,0:T(8,128)(2,1)S(1)}, u32[]{:S(2)}, u32[]{:S(2)}) collective-permute-start(bf16[128,128]{1,0:T(8,128)(2,1)S(1)} %get-tuple-element.24), channel_id=1, source_target_pairs={{1,0},{2,1},{3,2},{5,4},{6,5},{7,6},{9,8},{10,9},{11,10},{13,12},{... | collective-permute-start | bytes 98312 | tf_op jit(solution)/shard_map/ppermute | solution.py:24
  34.0 0.6 shard_map.89
  34.6 4.1 %collective-permute-done.2.edge_ref = bf16[128,128]{1,0:T(8,128)(2,1)S(1)} collective-permute-done((bf16[128,128]{1,0:T(8,128)(2,1)S(1)}, bf16[128,128]{1,0:T(8,128)(2,1)S(1)}, u32[]{:S(2)}, u32[]{:S(2)}) %collective-permute-start.2) | collective-permute-done | bytes 32800 | tf_op jit(solution)/shard_map/ppermute | solution.py:24
  38.7 3.0 %copy-done.1 = bf16[4,864,1024]{2,1,0:T(8,128)(2,1)S(1)} copy-done((bf16[4,864,1024]{2,1,0:T(8,128)(2,1)S(1)}, bf16[4,864,1024]{2,1,0:T(8,128)(2,1)}, u32[]{:S(2)}) %copy-start.1) | copy-done | bytes 7077912
  41.7 5.5 %shard_map.90 = bf16[432,128]{1,0:T(8,128)(2,1)S(1)} custom-call(bf16[128,512]{1,0:T(8,128)(2,1)S(1)} %get-tuple-element.23.delta_ref, bf16[128,128]{1,0:T(8,128)(2,1)S(1)} %collective-permute-done.2.edge_ref, bf16[1728,128]{1,0:T(8,128)(2,1)S(1)} %bitcast.19, bf16[512,1152]{1,0:T(8,128)(2,1)S(1)} %copy-done, f32[4,64,1024]{2,1,0:T(8,128)S(1)} %copy-done.5, ...), custom_call_target="tpu_custom_call" | custom-call | tf_op jit(solution)/shard_map/pallas_call | solution.py:231
  47.3 0.4 maximum_maximum_fusion.1
  47.7 14.7 %all_to_all.30 = bf16[8,416,128]{2,1,0:T(8,128)(2,1)S(1)} all-to-all(bf16[8,416,128]{2,1,0:T(8,128)(2,1)S(1)} %maximum_maximum_fusion), channel_id=1, replica_groups=mesh['y'=4,'z'=8,'xl'=2,'xh'=2,'c'=2] {'xl','xh','c'}, dimensions={0} | all-to-all | bytes 1703936 | tf_op jit(solution)/shard_map/all_to_all | solution.py:246
  62.5 8.5 %all_to_all.31 = bf16[4,72,128]{2,1,0:T(8,128)(2,1)S(1)} all-to-all(bf16[4,72,128]{2,1,0:T(8,128)(2,1)S(1)} %bitcast.25), channel_id=1, replica_groups=mesh['y'=4,'z'=8,'xl'=2,'xh'=2,'c'=2] {'y'}, dimensions={0} | all-to-all | bytes 147456 | tf_op jit(solution)/shard_map/all_to_all | solution.py:246
  71.1 16.2 %all_to_all.32 = bf16[8,72,128]{2,1,0:T(8,128)(2,1)S(1)} all-to-all(bf16[8,72,128]{2,1,0:T(8,128)(2,1)S(1)} %broadcast_in_dim.11), channel_id=1, replica_groups=mesh['y'=4,'z'=8,'xl'=2,'xh'=2,'c'=2] {'z'}, dimensions={0} | all-to-all | bytes 294912 | tf_op jit(solution)/shard_map/all_to_all | solution.py:246
  87.3 6.9 %all_to_all.33 = bf16[4,72,128]{2,1,0:T(8,128)(2,1)S(1)} all-to-all(bf16[4,72,128]{2,1,0:T(8,128)(2,1)S(1)} %broadcast_in_dim.24), channel_id=1, replica_groups=mesh['y'=4,'z'=8,'xl'=2,'xh'=2,'c'=2] {'y'}, dimensions={0} | all-to-all | bytes 147456 | tf_op jit(solution)/shard_map/all_to_all | solution.py:246
  94.2 0.9 broadcast_in_dim.26
  95.1 8.1 %all-to-all-start.5 = ((bf16[8,288,128]{2,1,0:T(8,128)(2,1)}), bf16[8,288,128]{2,1,0:T(8,128)(2,1)S(1)}, u32[]{:S(2)}, u32[]{:S(2)}) async-start(bf16[8,288,128]{2,1,0:T(8,128)(2,1)} %broadcast_in_dim.26), calls=%async_computation.5 | async-start | bytes 1179648 | tf_op jit(solution)/shard_map/all_to_all | solution.py:246
  103.2 0.7 constant_dynamic-slice_fusion
  103.9 8.7 %all-to-all-done.5 = bf16[8,288,128]{2,1,0:T(8,128)(2,1)S(1)} async-done(((bf16[8,288,128]{2,1,0:T(8,128)(2,1)}), bf16[8,288,128]{2,1,0:T(8,128)(2,1)S(1)}, u32[]{:S(2)}, u32[]{:S(2)}) %all-to-all-start.5) | async-done | bytes 589856 | tf_op jit(solution)/shard_map/all_to_all | solution.py:246
  112.6 1.1 shard_map.91
  (24 shorter events, 0.4 us)
Async XLA Ops:
  0.6 11.0 %copy-start.2 = (bf16[512,1152]{1,0:T(8,128)(2,1)S(1)}, bf16[512,1152]{1,0:T(8,128)(2,1)}, u32[]{:S(2)}) copy-start(bf16[512,1152]{1,0:T(8,128)(2,1)} %constant.22.clone.table_ref) | copy-start | bytes 3538948
  2.3 20.4 %collective-permute-start = (bf16[4,32,512]{2,1,0:T(8,128)(2,1)S(1)}, bf16[4,32,512]{2,1,0:T(8,128)(2,1)S(1)}, u32[]{:S(2)}, u32[]{:S(2)}) collective-permute-start(bf16[4,32,512]{2,1,0:T(8,128)(2,1)S(1)} %bitcast.26), channel_id=1, source_target_pairs={{0,1},{1,2},{2,3},{4,5},{5,6},{6,7},{8,9},{9,10},{10,11},{12,13},{... | collective-permute-start | bytes 393224 | tf_op jit(solution)/shard_map/ppermute | solution.py:24
  8.3 22.6 %all-to-all-start = ((bf16[4,128,128]{2,1,0:T(8,128)(2,1)}), bf16[4,128,128]{2,1,0:T(8,128)(2,1)S(1)}, u32[]{:S(2)}, u32[]{:S(2)}) async-start(bf16[4,128,128]{2,1,0:T(8,128)(2,1)} %bitcast.27), calls=%async_computation | async-start | bytes 262144 | tf_op jit(solution)/shard_map/all_to_all | solution.py:246
  11.7 0.9 copy-start.6
  22.7 5.7 %copy-start = (bf16[512,1152]{1,0:T(8,128)(2,1)S(1)}, bf16[512,1152]{1,0:T(8,128)(2,1)}, u32[]{:S(2)}) copy-start(bf16[512,1152]{1,0:T(8,128)(2,1)} %constant.23.clone.table_ref) | copy-start | bytes 3538948
  22.7 5.7 %copy-start.3 = (bf16[27,64,128]{2,1,0:T(8,128)(2,1)S(1)}, bf16[27,64,128]{2,1,0:T(8,128)(2,1)}, u32[]{:S(2)}) copy-start(bf16[27,64,128]{2,1,0:T(8,128)(2,1)} %param.8) | copy-start | bytes 1327108
  24.9 6.0 %collective-permute-start.1 = (bf16[4,64,128]{2,1,0:T(8,128)(2,1)S(1)}, bf16[4,64,128]{2,1,0:T(8,128)(2,1)S(1)}, u32[]{:S(2)}, u32[]{:S(2)}) collective-permute-start(bf16[4,64,128]{2,1,0:T(8,128)(2,1)S(1)} %get-tuple-element.20), channel_id=1, source_target_pairs={{0,1},{1,2},{2,3},{4,5},{5,6},{6,7},{8,9},{9,10},{10,11},{12,13},{... | collective-permute-start | bytes 196616 | tf_op jit(solution)/shard_map/ppermute | solution.py:24
  30.9 3.0 %copy-start.4 = (bf16[1728,512]{1,0:T(8,128)(2,1)S(1)}, bf16[1728,512]{1,0:T(8,128)(2,1)}, u32[]{:S(2)}) copy-start(bf16[1728,512]{1,0:T(8,128)(2,1)} %get-tuple-element.19.im_ref) | copy-start | bytes 5308420
  31.8 6.9 %copy-start.5 = (f32[4,64,1024]{2,1,0:T(8,128)S(1)}, f32[4,64,1024]{2,1,0:T(8,128)}, u32[]{:S(2)}) copy-start(f32[4,64,1024]{2,1,0:T(8,128)} %get-tuple-element.25.slope_ref) | copy-start | bytes 3145732
  31.8 6.9 %collective-permute-start.2 = (bf16[128,128]{1,0:T(8,128)(2,1)S(1)}, bf16[128,128]{1,0:T(8,128)(2,1)S(1)}, u32[]{:S(2)}, u32[]{:S(2)}) collective-permute-start(bf16[128,128]{1,0:T(8,128)(2,1)S(1)} %get-tuple-element.24), channel_id=1, source_target_pairs={{1,0},{2,1},{3,2},{5,4},{6,5},{7,6},{9,8},{10,9},{11,10},{13,12},{... | collective-permute-start | bytes 98312 | tf_op jit(solution)/shard_map/ppermute | solution.py:24
  38.7 3.0 %copy-start.1 = (bf16[4,864,1024]{2,1,0:T(8,128)(2,1)S(1)}, bf16[4,864,1024]{2,1,0:T(8,128)(2,1)}, u32[]{:S(2)}) copy-start(bf16[4,864,1024]{2,1,0:T(8,128)(2,1)} %get-tuple-element.26.im_ref) | copy-start | bytes 21233668
  95.1 17.5 %all-to-all-start.5 = ((bf16[8,288,128]{2,1,0:T(8,128)(2,1)}), bf16[8,288,128]{2,1,0:T(8,128)(2,1)S(1)}, u32[]{:S(2)}, u32[]{:S(2)}) async-start(bf16[8,288,128]{2,1,0:T(8,128)(2,1)} %broadcast_in_dim.26), calls=%async_computation.5 | async-start | bytes 1179648 | tf_op jit(solution)/shard_map/all_to_all | solution.py:246

commit v3 on v2

v3 whole, which is shorter than its diff:
```python
import jax
import jax.numpy as jnp
import numpy as np
from jax import lax
from jax.experimental import pallas as pl
from jax.experimental.pallas import tpu as pltpu
from jax.sharding import Mesh
from jax.sharding import PartitionSpec as P

YD = 32
ZD = 16
LANES = 128
DP = ("y", "z", "xl")
SPACE = ("xh", "c")
XY_GROUP = ("y", "xl", "xh", "c")
BF = jnp.bfloat16
F32 = jnp.float32
INTERPRET = False


def shifted(value, axis, steps):
    count = lax.axis_size(axis)
    initial, last = (max(0, -steps), min(count, count - steps))
    return lax.ppermute(value, axis, [(source, source + steps) for source in range(initial, last)])


def plane_table(size_y, size_z, copies):
    half_y, half_z = size_y // 2, size_z // 2
    cells = half_y * half_z
    table = np.zeros((copies, size_y * size_z, 9, copies, cells), np.float32)
    for second in range(3):
        for third in range(3):
            for out_y in range(half_y):
                for out_z in range(half_z):
                    y, z = 2 * out_y + second - 1, 2 * out_z + third - 1
                    if y >= 0 and z >= 0:
                        for k in range(copies):
                            table[k, y * size_z + z, 3 * second + third, k, out_y * half_z + out_z] = 1
    return jnp.asarray(table.reshape(copies * size_y * size_z, 9 * copies * cells), BF)


def row_order(chans, rows):
    shape = (rows * chans, chans * rows)
    at = lax.broadcasted_iota(jnp.int32, shape, 0)
    source = lax.broadcasted_iota(jnp.int32, shape, 1)
    block = at // chans
    row = (block % (rows // 2)) * 2 + block // (rows // 2)
    return (source == (at % chans) * rows + row).astype(F32).astype(BF)


def turned(value):
    size = value.shape[1]
    row = lax.broadcasted_iota(jnp.int32, (size, size), 0)
    col = lax.broadcasted_iota(jnp.int32, (size, size), 1)
    return dot_nt((row == col).astype(F32).astype(BF), value)


def dot(a, b):
    return jnp.dot(a, b, preferred_element_type=F32)


def dot_nt(a, b):
    return lax.dot_general(a, b, (((1,), (1,)), ((), ())), preferred_element_type=F32)


def act_and_slope(v):
    e = jnp.exp(-jnp.abs(v))
    act = 0.3 * v + 0.7 * (jnp.maximum(v, 0.0) + jnp.log(1.0 + e))
    slope = 0.3 + 0.7 * jnp.where(v >= 0, 1.0, e) / (1.0 + e)
    return act, slope


def first_body(v_ref, table_ref, w_ref, im_ref, pre_ref, order_ref, z_ref):
    order_ref[...] = row_order(32, 16)
    wt = turned(w_ref[...]).astype(BF)

    def one(s, carry):
        rows = dot(order_ref[...], v_ref[s].reshape(512, 512)).astype(BF)
        z_ref[...] = dot(rows, table_ref[...]).astype(BF)
        for o1 in range(8):
            for a in range(3):
                x = 2 * o1 + a - 1
                for t in range(9):
                    if x < 0:
                        block = jnp.zeros((32, LANES), BF)
                    else:
                        at = ((x % 2) * 8 + x // 2) * 32
                        block = z_ref[at : at + 32, t * LANES : (t + 1) * LANES]
                    k = (9 * a + t) * 32
                    im_ref[s, k : k + 32, o1 * LANES : (o1 + 1) * LANES] = block
        pre_ref[s] = dot(wt, im_ref[s])
        return carry

    lax.fori_loop(0, 4, one, 0)


def rim_body(pre_ref, rim_ref, table_ref, w_ref, hid_ref, last_ref, slope_ref, rimz_ref):
    z = dot(rim_ref[...].reshape(128, 512), table_ref[...]).astype(BF)
    wt = turned(w_ref[:288]).astype(BF)
    for s in range(4):
        im = jnp.concatenate(
            [z[32 * s : 32 * s + 32, t * LANES : (t + 1) * LANES] for t in range(9)], 0
        )
        rimz_ref[s] = im
        extra = dot(wt, im)
        for r in range(8):
            lanes = slice(r * LANES, (r + 1) * LANES)
            pre = pre_ref[s, :, lanes]
            if r == 0:
                pre = pre + extra
            act, slope = act_and_slope(pre)
            hidden = act.astype(BF)
            hid_ref[s, :, lanes] = hidden
            slope_ref[s, :, lanes] = slope
            if r == 7:
                last_ref[s] = hidden


def second_body(hid_ref, table_ref, w_ref, im_ref, pre_ref):
    for s in range(4):
        row = lambda r: (
            hid_ref[s, :, r * LANES : (r + 1) * LANES] if r >= 0 else jnp.zeros((64, LANES), BF)
        )
        left = jnp.concatenate(
            [jnp.concatenate([row(2 * o1 + a - 1) for o1 in range(4)], 1) for a in range(3)], 0
        )
        z = dot(left, table_ref[...]).astype(BF)
        for a in range(3):
            for t in range(9):
                k = (9 * a + t) * 64
                im_ref[k : k + 64, s * LANES : (s + 1) * LANES] = z[
                    64 * a : 64 * a + 64, t * LANES : (t + 1) * LANES
                ]
    pre_ref[...] = dot(turned(w_ref[...]).astype(BF), im_ref[...])


def pick_body(me_ref, up_ref, *out_refs):
    for m in range(4):
        out_refs[m][...] = up_ref[me_ref[0] ^ m]


def halo_body(me_ref, halo_ref, pre_ref, up0, up1, up2, up3, table_ref, w_ref, *refs):
    feat_refs, (delta_ref, edge_ref, imh_ref, up_ref, feat_ref) = refs[:4], refs[4:]
    me = me_ref[0]
    for m, ref in enumerate((up0, up1, up2, up3)):
        up_ref[me ^ m] = ref[...]
    z = dot(halo_ref[...].reshape(256, LANES), table_ref[:LANES, :]).astype(BF)
    for s in range(4):
        for t in range(9):
            imh_ref[t * 64 : t * 64 + 64, s * LANES : (s + 1) * LANES] = z[
                64 * s : 64 * s + 64, t * LANES : (t + 1) * LANES
            ]
    pre = pre_ref[...] + dot(turned(w_ref[:576]).astype(BF), imh_ref[...])
    lane = lax.broadcasted_iota(jnp.int32, (128, LANES), 1)
    edge = jnp.zeros((128, LANES), F32)
    for s in range(4):
        act, slope = act_and_slope(pre[:, s * LANES : (s + 1) * LANES])
        feat_ref[s] = turned(act.astype(BF)).astype(BF)
        delta = (turned(up_ref[s]) * slope).astype(BF)
        delta_ref[s] = delta
        moved = delta.astype(F32)
        if s:
            moved = pltpu.roll(moved, 32 * s, 1)
        edge = jnp.where(lane // 32 == s, moved, edge)
    edge_ref[...] = edge.astype(BF)
    for m in range(4):
        feat_refs[m][...] = feat_ref[me ^ m]


def second_grad_body(im_ref, imh_ref, delta_ref, out_ref):
    scale = 1.0 / 256
    delta = jnp.concatenate([delta_ref[s] for s in range(4)], 1)
    out_ref[:576] = (dot_nt(im_ref[:576] + imh_ref[...], delta) * scale).astype(BF)
    out_ref[576:] = (dot_nt(im_ref[576:], delta) * scale).astype(BF)


def back_body(
    delta_ref, edge_ref, k_ref, table_ref, slope_ref, im_ref, rimz_ref, out_ref, kodd_ref, ahead_ref, acc_ref
):
    lane = lax.broadcasted_iota(jnp.int32, (128, LANES), 1)
    acc_ref[...] = jnp.zeros_like(acc_ref)
    kodd_ref[:, :128] = k_ref[:576]
    kodd_ref[:, 128:] = k_ref[1152:]
    rim = edge_ref[...].astype(F32)
    for s in range(4):
        own = delta_ref[s]
        moved = pltpu.roll(own.astype(F32), 96, 1)
        ends = pltpu.roll(rim, 96 - 32 * s, 1) if s != 3 else rim
        ahead_ref[s, :128] = jnp.where(lane < 96, moved, ends).astype(BF)
        ahead_ref[s, 128:] = own

    def one(s, carry):
        even = dot(k_ref[576:1152], delta_ref[s])
        odd = dot(kodd_ref[...], ahead_ref[s])
        parts = []
        for grad in (even, odd):
            flat = jnp.concatenate([grad[64 * t : 64 * t + 64] for t in range(9)], 1)
            high = flat.astype(BF)
            parts += [high, (flat - high.astype(F32)).astype(BF)]
        got = dot_nt(jnp.concatenate(parts, 0), table_ref[...])
        rows = []
        for r in range(8):
            base = 128 * (r % 2)
            lanes = slice((r // 2) * LANES, (r // 2 + 1) * LANES)
            back = (got[base : base + 64, lanes] + got[base + 64 : base + 128, lanes]).astype(BF)
            slope = slope_ref[s, :, r * LANES : (r + 1) * LANES]
            rows.append((back.astype(F32) * slope).astype(BF))
        acc_ref[...] += dot_nt(im_ref[s], jnp.concatenate(rows, 1))
        acc_ref[:288] += dot_nt(rimz_ref[s], rows[0])
        return carry

    lax.fori_loop(0, 4, one, 0)
    acc = acc_ref[...] * (1.0 / 256)
    out_ref[...] = jnp.concatenate([acc[:432], acc[432:]], 1).astype(BF)


def finish_body(me_ref, rows_ref, f0, f1, f2, f3, first_ref, second_ref, feat_ref):
    for m, ref in enumerate((f0, f1, f2, f3)):
        feat_ref[me_ref[0] ^ m] = ref[...]
    second_ref[...] = rows_ref[:1728].astype(F32)
    packed = rows_ref[1728:2160].astype(F32)
    first_ref[:432] = packed[:, :64]
    first_ref[432:] = packed[:, 64:]


def call(body, outs, scratch=(), mib=24, final=False):
    here = pl.BlockSpec(memory_space=pltpu.VMEM)

    def run(*args):
        return pl.pallas_call(
            body,
            in_specs=[
                pl.BlockSpec(memory_space=pltpu.SMEM) if arg.shape == (1,) else here for arg in args
            ],
            out_specs=[here] * len(outs),
            out_shape=[
                jax.ShapeDtypeStruct(*out) if INTERPRET or final else pltpu.VMEM(*out) for out in outs
            ],
            scratch_shapes=list(scratch),
            compiler_params=pltpu.CompilerParams(vmem_limit_bytes=mib * 1024 * 1024),
            interpret=INTERPRET,
        )(*args)

    return run


def exchange(chunks, axis):
    return lax.all_to_all(chunks, axis, split_axis=0, concat_axis=0, tiled=True)


def reduce_stage(rows, axis):
    got = exchange(rows.reshape(lax.axis_size(axis), -1, LANES), axis)
    return jnp.sum(got.astype(F32), 0).astype(BF)


def gather_stage(rows, axis):
    copies = jnp.broadcast_to(rows[None], (lax.axis_size(axis),) + rows.shape)
    return exchange(copies, axis).reshape(-1, LANES)


def sum_everywhere(packed, wide):
    pad = jnp.zeros((144, LANES), BF)
    rows = reduce_stage(jnp.concatenate([wide, packed, pad], 0), XY_GROUP)
    got = exchange(jnp.broadcast_to(rows[None], (lax.axis_size("z"),) + rows.shape), "z")
    rows = jnp.sum(got.astype(F32), 0).astype(BF)
    return gather_stage(rows, XY_GROUP)


def swap_all(pieces):
    return [pieces[0]] + [
        lax.ppermute(pieces[m], SPACE, [(i, i ^ m) for i in range(4)]) for m in range(1, 4)
    ]


def per_device(volumes, first_kernel, second_kernel, upstream):
    table = plane_table(YD, ZD, 1)
    table2 = plane_table(YD // 2, ZD // 2, 4)
    rim = shifted(volumes[:, :, 15, :], SPACE, 1)
    me = lax.axis_index(SPACE).reshape(1)
    tile = ((128, 128), BF)
    up = upstream.reshape(128, 4, 128).transpose(1, 2, 0)
    ups = swap_all(call(pick_body, [tile] * 4)(me, up))
    w1 = first_kernel.reshape(864, 64)
    k2 = second_kernel.reshape(1728, 128)
    im1, pre1 = call(
        first_body,
        [((4, 864, 1024), BF), ((4, 64, 1024), F32)],
        scratch=[pltpu.VMEM((512, 512), BF), pltpu.VMEM((512, 1152), BF)],
    )(volumes, table, w1)
    hidden, last, slope1, rimz = call(
        rim_body,
        [((4, 64, 1024), BF), ((4, 64, 128), BF), ((4, 64, 1024), F32), ((4, 288, 128), BF)],
    )(pre1, rim, table, w1)
    halo = shifted(last, SPACE, 1)
    im2, pre2 = call(second_body, [((1728, 512), BF), ((128, 512), F32)])(hidden, table2, k2)
    *feats, delta2, edge, im2h = call(
        halo_body,
        [tile] * 4 + [((4, 128, 128), BF), tile, ((576, 512), BF)],
        scratch=[pltpu.VMEM((4, 128, 128), BF), pltpu.VMEM((4, 128, 128), BF)],
    )(me, halo, pre2, *ups, table2, k2)
    edge = shifted(edge, SPACE, -1)
    feats = swap_all(feats)
    (wide,) = call(second_grad_body, [((1728, 128), BF)])(im2, im2h, delta2)
    (packed,) = call(
        back_body,
        [((432, 128), BF)],
        scratch=[
            pltpu.VMEM((576, 256), BF),
            pltpu.VMEM((4, 256, 128), BF),
            pltpu.VMEM((864, 64), F32),
        ],
    )(delta2, edge, k2, table2, slope1, im1, rimz)
    packed, wide, *feats = lax.optimization_barrier((packed, wide, *feats))
    rows = sum_everywhere(packed, wide)
    first_grad, second_grad, features = call(
        finish_body,
        [((864, 64), F32), ((1728, 128), F32), ((4, 128, 128), BF)],
        final=True,
    )(me, rows, *feats)
    features = features.transpose(2, 0, 1).reshape(1, 128, 16, 32)
    return (features, first_grad.reshape(27, 32, 64), second_grad.reshape(27, 64, 128))


def solution(mesh):
    fine = Mesh(mesh.devices.reshape(4, 8, 2, 2, 2), ("y", "z", "xl", "xh", "c"))
    in_specs = (P(DP, None, SPACE, None), P(), P(), P(DP + SPACE, None, None, None))
    out_specs = (P(DP + SPACE, None, None, None), P(), P())
    return jax.shard_map(
        per_device, mesh=fine, in_specs=in_specs, out_specs=out_specs, check_vma=False
    )
```

time: 114 us -> 102 us (0.89)
  waiting for transfers between devices: 12.8 us -> 0.84 us
  blocking collectives: 46.3 us -> 52.8 us
  starting transfers between devices: 23 us -> 17.7 us
  Pallas kernels: 23 us -> 19.5 us
  local copies, waits for them, and re-layouts: 7.25 us -> 9.28 us
    all_to_all x2 -> x0, starting transfers between devices: 11.5 us -> none  [exchange(): return lax.all_to_all(chunks, axis, split_axis=0, concat_axis=0, tiled=True)]
    all_to_all x2 -> x0, waiting for transfers between devices: 8.7 us -> none  [exchange(): return lax.all_to_all(chunks, axis, split_axis=0, concat_axis=0, tiled=True)]
    ppermute x0 -> x6, starting transfers between devices: none -> 7.54 us  [swap_all(): lax.ppermute(pieces[m], SPACE, [(i, i ^ m) for i in range(4)])]
    all_to_all x4 -> x3, blocking collectives: 46.3 us -> 52.8 us  [exchange(): return lax.all_to_all(chunks, axis, split_axis=0, concat_axis=0, tiled=True)]
    ppermute x3, waiting for transfers between devices: 4.09 us -> 0.37 us  [shifted(): lax.ppermute(value, axis, [(source, source + steps) for source in range(i...]
    unnamed x15 -> x19, local copies, waits for them, and re-layouts: 3.98 us -> 7.6 us
    pallas_call x7 -> x8, Pallas kernels: 23 us -> 19.5 us  [run(): pl.pallas_call(body, in_specs=[pl.BlockSpec(memory_space=pltpu.SMEM) if a...]
    ppermute x3, starting transfers between devices: 11.6 us -> 10.2 us  [shifted(): lax.ppermute(value, axis, [(source, source + steps) for source in range(i...]
  transfers between devices with their start and end apart: 5 -> 9, of which waited for: 2 -> 2; matrix products, arithmetic and copies ran while one was open for 1% -> 0% of each run, Pallas kernels for 14% -> 16%
where the time goes in v3:
time: 102 us; the launch traced here: 101 us
  blocking collectives  52.8 us (52%)
  Pallas kernels  19.5 us (19%)
  starting transfers between devices  17.7 us (17%)
  local copies, waits for them, and re-layouts  9.28 us (9%)
    all_to_all x3, blocking collectives, exchange(): return lax.all_to_all(chunks, axis, split_axis=0, concat_axis=0, tiled=True)  52.8 us
    pallas_call x8, Pallas kernels, run(): pl.pallas_call(body, in_specs=[pl.BlockSpec(memory_space=pltpu.SMEM) if a...  19.5 us
    ppermute x3, starting transfers between devices, shifted(): lax.ppermute(value, axis, [(source, source + steps) for source in range(i...  10.2 us
    unnamed x19, local copies, waits for them, and re-layouts  7.6 us
    ppermute x6, starting transfers between devices, swap_all(): lax.ppermute(pieces[m], SPACE, [(i, i ^ m) for i in range(4)])  7.54 us
  transfers between devices with their start and end apart: 9, of which 2 were waited for; matrix products, arithmetic and copies ran while one was open for 0% of the time, Pallas kernels for 16%

profile of v3, /device:TPU:1, one launch (start us, length us, event | category | flops | bytes accessed | tf_op | source)
XLA Modules:
  0.0 101.4 jit_solution(3529797642316357566)
XLA Ops:
  0.6 1.5 %slice.3 = bf16[4,32,1,512]{3,2,1,0:T(2,128)(2,1)S(1)} slice(bf16[4,32,16,512]{3,2,1,0:T(8,128)(2,1)} %v_ref.1), slice={[0:4], [0:32], [15:16], [0:512]} | slice | bytes 262144 | tf_op jit(solution)/shard_map/slice | solution.py:278
  2.2 6.0 %collective-permute-start = (bf16[4,32,512]{2,1,0:T(8,128)(2,1)S(1)}, bf16[4,32,512]{2,1,0:T(8,128)(2,1)S(1)}, u32[]{:S(2)}, u32[]{:S(2)}) collective-permute-start(bf16[4,32,512]{2,1,0:T(8,128)(2,1)S(1)} %bitcast.24), channel_id=1, source_target_pairs={{0,1},{1,2},{2,3},{4,5},{5,6},{6,7},{8,9},{9,10},{10,11},{12,13},{... | collective-permute-start | bytes 393224 | tf_op jit(solution)/shard_map/ppermute | solution.py:24
  8.2 1.3 %copy-done.3 = bf16[512,1152]{1,0:T(8,128)(2,1)S(1)} copy-done((bf16[512,1152]{1,0:T(8,128)(2,1)S(1)}, bf16[512,1152]{1,0:T(8,128)(2,1)}, u32[]{:S(2)}) %copy-start.3) | copy-done | bytes 1179672
  9.5 1.6 %copy-done.6 = bf16[4,32,16,512]{3,2,1,0:T(8,128)(2,1)S(1)} copy-done((bf16[4,32,16,512]{3,2,1,0:T(8,128)(2,1)S(1)}, bf16[4,32,16,512]{3,2,1,0:T(8,128)(2,1)}, u32[]{:S(2)}) %copy-start.6) | copy-done | bytes 2097176
  11.1 0.9 copy-done.7
  12.0 8.3 %shard_map.85 = (bf16[4,864,1024]{2,1,0:T(8,128)(2,1)S(1)}, f32[4,64,1024]{2,1,0:T(8,128)S(1)}) custom-call(bf16[4,32,16,512]{3,2,1,0:T(8,128)(2,1)S(1)} %copy-done.6, bf16[512,1152]{1,0:T(8,128)(2,1)S(1)} %copy-done.3, bf16[864,64]{1,0:T(8,128)(2,1)S(1)} %bitcast.20), custom_call_target="tpu_custom_call" | custom-call | tf_op jit(solution)/shard_map/pallas_call | solution.py:230
  20.3 2.9 %copy-done.1 = bf16[4,864,1024]{2,1,0:T(8,128)(2,1)} copy-done((bf16[4,864,1024]{2,1,0:T(8,128)(2,1)}, bf16[4,864,1024]{2,1,0:T(8,128)(2,1)S(1)}, u32[]{:S(2)}) %copy-start.1) | copy-done | bytes 7077912
  23.2 1.7 %shard_map.86 = (bf16[4,64,1024]{2,1,0:T(8,128)(2,1)S(1)}, bf16[4,64,128]{2,1,0:T(8,128)(2,1)}, f32[4,64,1024]{2,1,0:T(8,128)S(1)}, bf16[4,288,128]{2,1,0:T(8,128)(2,1)S(1)}) custom-call(f32[4,64,1024]{2,1,0:T(8,128)S(1)} %get-tuple-element.31.pre_ref, bf16[4,32,512]{2,1,0:T(8,128)(2,1)S(1)} %collective-permute-done.rim_ref, ...), custom_call_target="tpu_custom_call" | custom-call | tf_op jit(solution)/shard_map/pallas_call | solution.py:230
  24.9 1.9 %collective-permute-start.1 = (bf16[4,64,128]{2,1,0:T(8,128)(2,1)}, bf16[4,64,128]{2,1,0:T(8,128)(2,1)S(1)}, u32[]{:S(2)}, u32[]{:S(2)}) collective-permute-start(bf16[4,64,128]{2,1,0:T(8,128)(2,1)} %get-tuple-element.32), channel_id=1, source_target_pairs={{0,1},{1,2},{2,3},{4,5},{5,6},{6,7},{8,9},{9,10},{10,11},{12,13},{... | collective-permute-start | bytes 196616 | tf_op jit(solution)/shard_map/ppermute | solution.py:24
  26.8 0.9 copy-done.8
  27.7 0.6 collective-permute-start.2
  28.3 3.2 %collective-permute-start.4 = (bf16[128,128]{1,0:T(8,128)(2,1)S(1)}, bf16[128,128]{1,0:T(8,128)(2,1)S(1)}, u32[]{:S(2)}, u32[]{:S(2)}) collective-permute-start(bf16[128,128]{1,0:T(8,128)(2,1)S(1)} %get-tuple-element.38), channel_id=1, source_target_pairs={{0,3},{1,2},{2,1},{3,0},{4,7},{5,6},{6,5},{7,4},{8,11},{9,10},{10,... | collective-permute-start | bytes 98312 | tf_op jit(solution)/shard_map/ppermute | solution.py:271
  31.6 1.6 %shard_map.87 = (bf16[1728,512]{1,0:T(8,128)(2,1)S(1)}, f32[128,512]{1,0:T(8,128)S(1)}) custom-call(bf16[4,64,1024]{2,1,0:T(8,128)(2,1)S(1)} %get-tuple-element.33.hid_ref, bf16[512,1152]{1,0:T(8,128)(2,1)S(1)} %copy-done, bf16[1728,128]{1,0:T(8,128)(2,1)S(1)} %bitcast.16), custom_call_target="tpu_custom_call" | custom-call | tf_op jit(solution)/shard_map/pallas_call | solution.py:230
  33.2 0.5 collective-permute-done.4.up3
  33.6 0.9 shard_map.89
  34.5 2.2 %collective-permute-start.5 = (bf16[128,128]{1,0:T(8,128)(2,1)S(1)}, bf16[128,128]{1,0:T(8,128)(2,1)S(1)}, u32[]{:S(2)}, u32[]{:S(2)}) collective-permute-start(bf16[128,128]{1,0:T(8,128)(2,1)S(1)} %get-tuple-element.40), channel_id=1, source_target_pairs={{1,0},{2,1},{3,2},{5,4},{6,5},{7,6},{9,8},{10,9},{11,10},{13,12},{... | collective-permute-start | bytes 98312 | tf_op jit(solution)/shard_map/ppermute | solution.py:24
  36.9 3.0 %collective-permute-start.7 = (bf16[128,128]{1,0:T(8,128)(2,1)S(1)}, bf16[128,128]{1,0:T(8,128)(2,1)S(1)}, u32[]{:S(2)}, u32[]{:S(2)}) collective-permute-start(bf16[128,128]{1,0:T(8,128)(2,1)S(1)} %get-tuple-element.48), channel_id=1, source_target_pairs={{0,2},{1,3},{2,0},{3,1},{4,6},{5,7},{6,4},{7,5},{8,10},{9,11},{10,... | collective-permute-start | bytes 98312 | tf_op jit(solution)/shard_map/ppermute | solution.py:271
  39.9 0.6 collective-permute-start.8
  40.6 0.6 shard_map.91
  41.6 5.2 %shard_map.90 = bf16[432,128]{1,0:T(8,128)(2,1)S(1)} custom-call(bf16[4,128,128]{2,1,0:T(8,128)(2,1)S(1)} %get-tuple-element.39.delta_ref, bf16[128,128]{1,0:T(8,128)(2,1)S(1)} %collective-permute-done.5.edge_ref, bf16[1728,128]{1,0:T(8,128)(2,1)S(1)} %bitcast.18, bf16[512,1152]{1,0:T(8,128)(2,1)S(1)} %copy-done, ...), custom_call_target="tpu_custom_call" | custom-call | tf_op jit(solution)/shard_map/pallas_call | solution.py:230
  47.2 18.7 %all_to_all.15 = bf16[32,72,128]{2,1,0:T(8,128)(2,1)S(1)} all-to-all(bf16[32,72,128]{2,1,0:T(8,128)(2,1)S(1)} %bitcast.23), channel_id=1, replica_groups=mesh['y'=4,'z'=8,'xl'=2,'xh'=2,'c'=2] {'y','xl','xh','c'}, dimensions={0} | all-to-all | bytes 1179648 | tf_op jit(solution)/shard_map/all_to_all | solution.py:248
  66.0 17.0 %all_to_all.16 = bf16[8,72,128]{2,1,0:T(8,128)(2,1)S(1)} all-to-all(bf16[8,72,128]{2,1,0:T(8,128)(2,1)S(1)} %broadcast_in_dim.7), channel_id=1, replica_groups=mesh['y'=4,'z'=8,'xl'=2,'xh'=2,'c'=2] {'z'}, dimensions={0} | all-to-all | bytes 294912 | tf_op jit(solution)/shard_map/all_to_all | solution.py:248
  83.2 17.1 %all_to_all.17 = bf16[32,72,128]{2,1,0:T(8,128)(2,1)S(1)} all-to-all(bf16[32,72,128]{2,1,0:T(8,128)(2,1)S(1)} %broadcast_in_dim.8), channel_id=1, replica_groups=mesh['y'=4,'z'=8,'xl'=2,'xh'=2,'c'=2] {'y','xl','xh','c'}, dimensions={0} | all-to-all | bytes 1179648 | tf_op jit(solution)/shard_map/all_to_all | solution.py:248
  100.2 1.2 %shard_map.92 = (f32[864,64]{1,0:T(8,128)}, f32[1728,128]{1,0:T(8,128)}, bf16[4,128,128]{2,1,0:T(8,128)(2,1)}) custom-call(s32[1]{0:T(128)} %bitcast.me_ref, bf16[2304,128]{1,0:T(8,128)(2,1)S(1)} %bitcast.19, bf16[128,128]{1,0:T(8,128)(2,1)S(1)} %get-tuple-element.52.f0, bf16[128,128]{1,0:T(8,128)(2,1)S(1)} %collective-permute-done.6.f1, ...), custom_call_target="tpu_custom_call" | custom-call | tf_op jit(solution)/shard_map/pallas_call | solution.py:230
  (32 shorter events, 1.2 us)
Async XLA Ops:
  2.2 21.0 %collective-permute-start = (bf16[4,32,512]{2,1,0:T(8,128)(2,1)S(1)}, bf16[4,32,512]{2,1,0:T(8,128)(2,1)S(1)}, u32[]{:S(2)}, u32[]{:S(2)}) collective-permute-start(bf16[4,32,512]{2,1,0:T(8,128)(2,1)S(1)} %bitcast.24), channel_id=1, source_target_pairs={{0,1},{1,2},{2,3},{4,5},{5,6},{6,7},{8,9},{9,10},{10,11},{12,13},{... | collective-permute-start | bytes 393224 | tf_op jit(solution)/shard_map/ppermute | solution.py:24
  8.2 1.3 %copy-start.3 = (bf16[512,1152]{1,0:T(8,128)(2,1)S(1)}, bf16[512,1152]{1,0:T(8,128)(2,1)}, u32[]{:S(2)}) copy-start(bf16[512,1152]{1,0:T(8,128)(2,1)} %constant.17.clone.table_ref) | copy-start | bytes 3538948
  9.5 1.6 %copy-start.6 = (bf16[4,32,16,512]{3,2,1,0:T(8,128)(2,1)S(1)}, bf16[4,32,16,512]{3,2,1,0:T(8,128)(2,1)}, u32[]{:S(2)}) copy-start(bf16[4,32,16,512]{3,2,1,0:T(8,128)(2,1)} %v_ref.1) | copy-start | bytes 6291460
  11.1 0.9 copy-start.7
  12.0 11.2 %copy-start.4 = (bf16[512,1152]{1,0:T(8,128)(2,1)S(1)}, bf16[512,1152]{1,0:T(8,128)(2,1)}, u32[]{:S(2)}) copy-start(bf16[512,1152]{1,0:T(8,128)(2,1)} %constant.17.clone.table_ref) | copy-start | bytes 3538948
  20.3 2.9 %copy-start.1 = (bf16[4,864,1024]{2,1,0:T(8,128)(2,1)}, bf16[4,864,1024]{2,1,0:T(8,128)(2,1)S(1)}, u32[]{:S(2)}) copy-start(bf16[4,864,1024]{2,1,0:T(8,128)(2,1)S(1)} %get-tuple-element.42.im_ref) | copy-start | bytes 21233668
  23.2 8.3 %copy-start = (bf16[512,1152]{1,0:T(8,128)(2,1)S(1)}, bf16[512,1152]{1,0:T(8,128)(2,1)}, u32[]{:S(2)}) copy-start(bf16[512,1152]{1,0:T(8,128)(2,1)} %constant.18.clone.table_ref) | copy-start | bytes 3538948
  23.2 8.3 %copy-start.5 = (bf16[27,64,128]{2,1,0:T(8,128)(2,1)S(1)}, bf16[27,64,128]{2,1,0:T(8,128)(2,1)}, u32[]{:S(2)}) copy-start(bf16[27,64,128]{2,1,0:T(8,128)(2,1)} %param.8) | copy-start | bytes 1327108
  24.9 8.8 %collective-permute-start.1 = (bf16[4,64,128]{2,1,0:T(8,128)(2,1)}, bf16[4,64,128]{2,1,0:T(8,128)(2,1)S(1)}, u32[]{:S(2)}, u32[]{:S(2)}) collective-permute-start(bf16[4,64,128]{2,1,0:T(8,128)(2,1)} %get-tuple-element.32), channel_id=1, source_target_pairs={{0,1},{1,2},{2,3},{4,5},{5,6},{6,7},{8,9},{9,10},{10,11},{12,13},{... | collective-permute-start | bytes 196616 | tf_op jit(solution)/shard_map/ppermute | solution.py:24
  26.8 0.9 copy-start.8
  27.7 5.4 %collective-permute-start.2 = (bf16[128,128]{1,0:T(8,128)(2,1)S(1)}, bf16[128,128]{1,0:T(8,128)(2,1)S(1)}, u32[]{:S(2)}, u32[]{:S(2)}) collective-permute-start(bf16[128,128]{1,0:T(8,128)(2,1)S(1)} %get-tuple-element.36), channel_id=1, source_target_pairs={{0,1},{1,0},{2,3},{3,2},{4,5},{5,4},{6,7},{7,6},{8,9},{9,8},{10,11... | collective-permute-start | bytes 98312 | tf_op jit(solution)/shard_map/ppermute | solution.py:271
  28.3 4.9 %collective-permute-start.3 = (bf16[128,128]{1,0:T(8,128)(2,1)S(1)}, bf16[128,128]{1,0:T(8,128)(2,1)S(1)}, u32[]{:S(2)}, u32[]{:S(2)}) collective-permute-start(bf16[128,128]{1,0:T(8,128)(2,1)S(1)} %get-tuple-element.37), channel_id=1, source_target_pairs={{0,2},{1,3},{2,0},{3,1},{4,6},{5,7},{6,4},{7,5},{8,10},{9,11},{10,... | collective-permute-start | bytes 98312 | tf_op jit(solution)/shard_map/ppermute | solution.py:271
  28.3 5.3 %collective-permute-start.4 = (bf16[128,128]{1,0:T(8,128)(2,1)S(1)}, bf16[128,128]{1,0:T(8,128)(2,1)S(1)}, u32[]{:S(2)}, u32[]{:S(2)}) collective-permute-start(bf16[128,128]{1,0:T(8,128)(2,1)S(1)} %get-tuple-element.38), channel_id=1, source_target_pairs={{0,3},{1,2},{2,1},{3,0},{4,7},{5,6},{6,5},{7,4},{8,11},{9,10},{10,... | collective-permute-start | bytes 98312 | tf_op jit(solution)/shard_map/ppermute | solution.py:271
  31.6 10.0 %copy-start.2 = (bf16[4,864,1024]{2,1,0:T(8,128)(2,1)S(1)}, bf16[4,864,1024]{2,1,0:T(8,128)(2,1)}, u32[]{:S(2)}) copy-start(bf16[4,864,1024]{2,1,0:T(8,128)(2,1)} %copy-done.1) | copy-start | bytes 21233668
  34.5 7.1 %collective-permute-start.5 = (bf16[128,128]{1,0:T(8,128)(2,1)S(1)}, bf16[128,128]{1,0:T(8,128)(2,1)S(1)}, u32[]{:S(2)}, u32[]{:S(2)}) collective-permute-start(bf16[128,128]{1,0:T(8,128)(2,1)S(1)} %get-tuple-element.40), channel_id=1, source_target_pairs={{1,0},{2,1},{3,2},{5,4},{6,5},{7,6},{9,8},{10,9},{11,10},{13,12},{... | collective-permute-start | bytes 98312 | tf_op jit(solution)/shard_map/ppermute | solution.py:24
  36.8 10.1 %collective-permute-start.6 = (bf16[128,128]{1,0:T(8,128)(2,1)S(1)}, bf16[128,128]{1,0:T(8,128)(2,1)S(1)}, u32[]{:S(2)}, u32[]{:S(2)}) collective-permute-start(bf16[128,128]{1,0:T(8,128)(2,1)S(1)} %get-tuple-element.47), channel_id=1, source_target_pairs={{0,1},{1,0},{2,3},{3,2},{4,5},{5,4},{6,7},{7,6},{8,9},{9,8},{10,11... | collective-permute-start | bytes 98312 | tf_op jit(solution)/shard_map/ppermute | solution.py:271
  36.9 10.0 %collective-permute-start.7 = (bf16[128,128]{1,0:T(8,128)(2,1)S(1)}, bf16[128,128]{1,0:T(8,128)(2,1)S(1)}, u32[]{:S(2)}, u32[]{:S(2)}) collective-permute-start(bf16[128,128]{1,0:T(8,128)(2,1)S(1)} %get-tuple-element.48), channel_id=1, source_target_pairs={{0,2},{1,3},{2,0},{3,1},{4,6},{5,7},{6,4},{7,5},{8,10},{9,11},{10,... | collective-permute-start | bytes 98312 | tf_op jit(solution)/shard_map/ppermute | solution.py:271
  39.9 7.0 %collective-permute-start.8 = (bf16[128,128]{1,0:T(8,128)(2,1)S(1)}, bf16[128,128]{1,0:T(8,128)(2,1)S(1)}, u32[]{:S(2)}, u32[]{:S(2)}) collective-permute-start(bf16[128,128]{1,0:T(8,128)(2,1)S(1)} %get-tuple-element.49), channel_id=1, source_target_pairs={{0,3},{1,2},{2,1},{3,0},{4,7},{5,6},{6,5},{7,4},{8,11},{9,10},{10,... | collective-permute-start | bytes 98312 | tf_op jit(solution)/shard_map/ppermute | solution.py:271

commit v4 on v3

--- a/solution.py
+++ b/solution.py
@@ -70,39 +70,60 @@
     return act, slope
 
 
-def first_body(v_ref, table_ref, w_ref, im_ref, pre_ref, order_ref, z_ref):
+def first_body(
+    v_hbm, table_hbm, w_hbm, im_hbm, pre_ref, wt0_ref, v_ref, table_ref, w_ref, order_ref, z_ref, im_ref, sems, v_sems, im_sems
+):
+    fetch_w = pltpu.make_async_copy(w_hbm, w_ref, sems.at[0])
+    fetch_table = pltpu.make_async_copy(table_hbm, table_ref, sems.at[1])
+    fetch_w.start()
+    fetch_v = [pltpu.make_async_copy(v_hbm.at[s], v_ref.at[s], v_sems.at[s]) for s in range(4)]
+    fetch_v[0].start()
+    fetch_table.start()
+    for s in range(1, 4):
+        fetch_v[s].start()
     order_ref[...] = row_order(32, 16)
-    wt = turned(w_ref[...]).astype(BF)
+    fetch_w.wait()
+    w = w_ref[...]
+    below = jnp.concatenate([jnp.zeros((288, 64), BF), w[:288]], 0)
+    wt = turned(jnp.concatenate([w[288:], below], 1)).astype(BF)
+    wt0_ref[...] = turned(w[:288]).astype(BF)
+    fetch_table.wait()
 
     def one(s, carry):
+        pltpu.make_async_copy(v_hbm.at[s], v_ref.at[s], v_sems.at[s]).wait()
         rows = dot(order_ref[...], v_ref[s].reshape(512, 512)).astype(BF)
         z_ref[...] = dot(rows, table_ref[...]).astype(BF)
-        for o1 in range(8):
-            for a in range(3):
-                x = 2 * o1 + a - 1
+        for half in range(2):
+            for o1 in range(8):
+                at = (half * 8 + o1) * 32
                 for t in range(9):
-                    if x < 0:
-                        block = jnp.zeros((32, LANES), BF)
-                    else:
-                        at = ((x % 2) * 8 + x // 2) * 32
-                        block = z_ref[at : at + 32, t * LANES : (t + 1) * LANES]
-                    k = (9 * a + t) * 32
-                    im_ref[s, k : k + 32, o1 * LANES : (o1 + 1) * LANES] = block
-        pre_ref[s] = dot(wt, im_ref[s])
+                    k = (9 * half + t) * 32
+                    im_ref[s, k : k + 32, o1 * LANES : (o1 + 1) * LANES] = z_ref[
+                        at : at + 32, t * LANES : (t + 1) * LANES
+                    ]
+        pltpu.make_async_copy(im_ref.at[s], im_hbm.at[s], im_sems.at[s]).start()
+        got = dot(wt, im_ref[s])
+        pre_ref[s, :, :LANES] = got[:64, :LANES]
+        pre_ref[s, :, LANES:] = got[:64, LANES:] + got[64:, :-LANES]
         return carry
 
     lax.fori_loop(0, 4, one, 0)
-
-
-def rim_body(pre_ref, rim_ref, table_ref, w_ref, hid_ref, last_ref, slope_ref, rimz_ref):
+    for s in range(4):
+        pltpu.make_async_copy(im_ref.at[s], im_hbm.at[s], im_sems.at[s]).wait()
+
+
+def rim_body(
+    me_ref, up_hbm, pre_ref, rim_ref, table_ref, wt0_ref, hid_ref, send_ref, send2, send3, own_ref, slope_ref, rimz_ref, up_ref, sem
+):
+    fetch = pltpu.make_async_copy(up_hbm, up_ref, sem)
+    fetch.start()
     z = dot(rim_ref[...].reshape(128, 512), table_ref[...]).astype(BF)
-    wt = turned(w_ref[:288]).astype(BF)
     for s in range(4):
         im = jnp.concatenate(
             [z[32 * s : 32 * s + 32, t * LANES : (t + 1) * LANES] for t in range(9)], 0
         )
         rimz_ref[s] = im
-        extra = dot(wt, im)
+        extra = dot(wt0_ref[...], im)
         for r in range(8):
             lanes = slice(r * LANES, (r + 1) * LANES)
             pre = pre_ref[s, :, lanes]
@@ -113,7 +134,13 @@
             hid_ref[s, :, lanes] = hidden
             slope_ref[s, :, lanes] = slope
             if r == 7:
-                last_ref[s] = hidden
+                send_ref[64 * s : 64 * s + 64] = hidden
+    fetch.wait()
+    me = me_ref[0]
+    send_ref[256:] = up_ref[(me + 1) & 3]
+    send2[...] = up_ref[(me + 2) & 3]
+    send3[...] = up_ref[(me + 3) & 3]
+    own_ref[...] = up_ref[me]
 
 
 def second_body(hid_ref, table_ref, w_ref, im_ref, pre_ref):
@@ -134,17 +161,15 @@
     pre_ref[...] = dot(turned(w_ref[...]).astype(BF), im_ref[...])
 
 
-def pick_body(me_ref, up_ref, *out_refs):
-    for m in range(4):
-        out_refs[m][...] = up_ref[me_ref[0] ^ m]
-
-
-def halo_body(me_ref, halo_ref, pre_ref, up0, up1, up2, up3, table_ref, w_ref, *refs):
-    feat_refs, (delta_ref, edge_ref, imh_ref, up_ref, feat_ref) = refs[:4], refs[4:]
+def halo_body(me_ref, got_ref, pre_ref, own_ref, got2, got3, table_ref, w_ref, *refs):
+    send_ref, send2, send3, kept_ref, delta_ref, imh_ref, up_ref, feat_ref = refs
     me = me_ref[0]
-    for m, ref in enumerate((up0, up1, up2, up3)):
-        up_ref[me ^ m] = ref[...]
-    z = dot(halo_ref[...].reshape(256, LANES), table_ref[:LANES, :]).astype(BF)
+    up_ref[me] = own_ref[...]
+    up_ref[(me + 1) & 3] = got3[...]
+    up_ref[(me + 2) & 3] = got2[...]
+    up_ref[(me + 3) & 3] = got_ref[256:]
+    z = dot(got_ref[:256], table_ref[:LANES, :])
+    z = jnp.where(me > 0, z, 0.0).astype(BF)
     for s in range(4):
         for t in range(9):
             imh_ref[t * 64 : t * 64 + 64, s * LANES : (s + 1) * LANES] = z[
@@ -162,9 +187,11 @@
         if s:
             moved = pltpu.roll(moved, 32 * s, 1)
         edge = jnp.where(lane // 32 == s, moved, edge)
-    edge_ref[...] = edge.astype(BF)
-    for m in range(4):
-        feat_refs[m][...] = feat_ref[me ^ m]
+    send_ref[:128] = edge.astype(BF)
+    send_ref[128:] = feat_ref[(me + 3) & 3]
+    send2[...] = feat_ref[(me + 2) & 3]
+    send3[...] = feat_ref[(me + 1) & 3]
+    kept_ref[...] = feat_ref[me]
 
 
 def second_grad_body(im_ref, imh_ref, delta_ref, out_ref):
@@ -175,13 +202,15 @@
 
 
 def back_body(
-    delta_ref, edge_ref, k_ref, table_ref, slope_ref, im_ref, rimz_ref, out_ref, kodd_ref, ahead_ref, acc_ref
+    me_ref, im_hbm, wide_ref, delta_ref, got_ref, k_ref, table_ref, slope_ref, rimz_ref, out_ref, kodd_ref, ahead_ref, acc_ref, im_ref, sems
 ):
+    for s in range(4):
+        pltpu.make_async_copy(im_hbm.at[s], im_ref.at[s], sems.at[s]).start()
     lane = lax.broadcasted_iota(jnp.int32, (128, LANES), 1)
     acc_ref[...] = jnp.zeros_like(acc_ref)
     kodd_ref[:, :128] = k_ref[:576]
     kodd_ref[:, 128:] = k_ref[1152:]
-    rim = edge_ref[...].astype(F32)
+    rim = jnp.where(me_ref[0] < 3, got_ref[:128].astype(F32), 0.0)
     for s in range(4):
         own = delta_ref[s]
         moved = pltpu.roll(own.astype(F32), 96, 1)
@@ -205,37 +234,62 @@
             back = (got[base : base + 64, lanes] + got[base + 64 : base + 128, lanes]).astype(BF)
             slope = slope_ref[s, :, r * LANES : (r + 1) * LANES]
             rows.append((back.astype(F32) * slope).astype(BF))
-        acc_ref[...] += dot_nt(im_ref[s], jnp.concatenate(rows, 1))
-        acc_ref[:288] += dot_nt(rimz_ref[s], rows[0])
+        zero = jnp.zeros((64, LANES), BF)
+        both = jnp.concatenate(
+            [jnp.concatenate(rows, 1), jnp.concatenate(rows[1:] + [zero], 1)], 0
+        )
+        pltpu.make_async_copy(im_hbm.at[s], im_ref.at[s], sems.at[s]).wait()
+        acc_ref[...] += dot_nt(im_ref[s], both)
+        acc_ref[288:] += dot_nt(rimz_ref[s], jnp.concatenate([zero, rows[0]], 0))
         return carry
 
     lax.fori_loop(0, 4, one, 0)
     acc = acc_ref[...] * (1.0 / 256)
-    out_ref[...] = jnp.concatenate([acc[:432], acc[432:]], 1).astype(BF)
-
-
-def finish_body(me_ref, rows_ref, f0, f1, f2, f3, first_ref, second_ref, feat_ref):
-    for m, ref in enumerate((f0, f1, f2, f3)):
-        feat_ref[me_ref[0] ^ m] = ref[...]
+    out_ref[:1728] = wide_ref[...]
+    out_ref[2160:] = jnp.zeros((144, LANES), BF)
+    out_ref[1728:2016] = acc[288:].astype(BF)
+    out_ref[2016:2160] = jnp.concatenate([acc[:144, :64], acc[144:288, :64]], 1).astype(BF)
+
+
+def finish_body(me_ref, rows_ref, kept_ref, got_ref, got2, got3, first_ref, second_ref, feat_ref):
+    me = me_ref[0]
+    feat_ref[me] = kept_ref[...]
+    feat_ref[(me + 1) & 3] = got_ref[128:]
+    feat_ref[(me + 2) & 3] = got2[...]
+    feat_ref[(me + 3) & 3] = got3[...]
     second_ref[...] = rows_ref[:1728].astype(F32)
-    packed = rows_ref[1728:2160].astype(F32)
-    first_ref[:432] = packed[:, :64]
-    first_ref[432:] = packed[:, 64:]
-
-
-def call(body, outs, scratch=(), mib=24, final=False):
+    odd = rows_ref[1728:2016].astype(F32)
+    even = rows_ref[2016:2160].astype(F32)
+    first_ref[:288] = odd[:, 64:]
+    first_ref[288:432] = even[:, :64]
+    first_ref[432:576] = even[:, 64:]
+    first_ref[576:] = odd[:, :64]
+
+
+def call(body, outs, scratch=(), mib=24, final=False, far=(), far_outs=()):
     here = pl.BlockSpec(memory_space=pltpu.VMEM)
+    there = pl.BlockSpec(memory_space=pl.ANY if INTERPRET else pltpu.HBM)
+    scalar = pl.BlockSpec(memory_space=pltpu.SMEM)
+
+    def shape_of(at, out):
+        if INTERPRET or final:
+            return jax.ShapeDtypeStruct(*out)
+        return pltpu.HBM(*out) if at in far_outs else pltpu.VMEM(*out)
 
     def run(*args):
+        if not INTERPRET:
+            args = [
+                pltpu.with_memory_space_constraint(arg, pltpu.HBM) if at in far else arg
+                for at, arg in enumerate(args)
+            ]
         return pl.pallas_call(
             body,
             in_specs=[
-                pl.BlockSpec(memory_space=pltpu.SMEM) if arg.shape == (1,) else here for arg in args
+                scalar if arg.shape == (1,) else there if at in far else here
+                for at, arg in enumerate(args)
             ],
-            out_specs=[here] * len(outs),
-            out_shape=[
-                jax.ShapeDtypeStruct(*out) if INTERPRET or final else pltpu.VMEM(*out) for out in outs
-            ],
+            out_specs=[there if at in far_outs else here for at in range(len(outs))],
+            out_shape=[shape_of(at, out) for at, out in enumerate(outs)],
             scratch_shapes=list(scratch),
             compiler_params=pltpu.CompilerParams(vmem_limit_bytes=mib * 1024 * 1024),
             interpret=INTERPRET,
@@ -258,18 +312,15 @@
     return exchange(copies, axis).reshape(-1, LANES)
 
 
-def sum_everywhere(packed, wide):
-    pad = jnp.zeros((144, LANES), BF)
-    rows = reduce_stage(jnp.concatenate([wide, packed, pad], 0), XY_GROUP)
+def sum_everywhere(rows):
+    rows = reduce_stage(rows, XY_GROUP)
     got = exchange(jnp.broadcast_to(rows[None], (lax.axis_size("z"),) + rows.shape), "z")
     rows = jnp.sum(got.astype(F32), 0).astype(BF)
     return gather_stage(rows, XY_GROUP)
 
 
-def swap_all(pieces):
-    return [pieces[0]] + [
-        lax.ppermute(pieces[m], SPACE, [(i, i ^ m) for i in range(4)]) for m in range(1, 4)
-    ]
+def rotated(value, steps):
+    return lax.ppermute(value, SPACE, [(i, (i + steps) % 4) for i in range(4)])
 
 
 def per_device(volumes, first_kernel, second_kernel, upstream):
@@ -279,44 +330,71 @@
     me = lax.axis_index(SPACE).reshape(1)
     tile = ((128, 128), BF)
     up = upstream.reshape(128, 4, 128).transpose(1, 2, 0)
-    ups = swap_all(call(pick_body, [tile] * 4)(me, up))
     w1 = first_kernel.reshape(864, 64)
     k2 = second_kernel.reshape(1728, 128)
-    im1, pre1 = call(
+    im1, pre1, wt0 = call(
         first_body,
-        [((4, 864, 1024), BF), ((4, 64, 1024), F32)],
-        scratch=[pltpu.VMEM((512, 512), BF), pltpu.VMEM((512, 1152), BF)],
+        [((4, 576, 1024), BF), ((4, 64, 1024), F32), ((64, 288), BF)],
+        scratch=[
+            pltpu.VMEM((4, 32, 16, 512), BF),
+            pltpu.VMEM((512, 1152), BF),
+            pltpu.VMEM((864, 64), BF),
+            pltpu.VMEM((512, 512), BF),
+            pltpu.VMEM((512, 1152), BF),
+            pltpu.VMEM((4, 576, 1024), BF),
+            pltpu.SemaphoreType.DMA((2,)),
+            pltpu.SemaphoreType.DMA((4,)),
+            pltpu.SemaphoreType.DMA((4,)),
+        ],
+        far=(0, 1, 2),
+        far_outs=(0,),
     )(volumes, table, w1)
-    hidden, last, slope1, rimz = call(
+    hidden, sent, sent2, sent3, own, slope1, rimz = call(
         rim_body,
-        [((4, 64, 1024), BF), ((4, 64, 128), BF), ((4, 64, 1024), F32), ((4, 288, 128), BF)],
-    )(pre1, rim, table, w1)
-    halo = shifted(last, SPACE, 1)
+        [
+            ((4, 64, 1024), BF),
+            ((384, 128), BF),
+            tile,
+            tile,
+            tile,
+            ((4, 64, 1024), F32),
+            ((4, 288, 128), BF),
+        ],
+        scratch=[pltpu.VMEM((4, 128, 128), BF), pltpu.SemaphoreType.DMA(())],
+        far=(1,),
+    )(me, up, pre1, rim, table, wt0)
+    got = rotated(sent, 1)
+    got2 = rotated(sent2, 2)
+    got3 = rotated(sent3, 3)
     im2, pre2 = call(second_body, [((1728, 512), BF), ((128, 512), F32)])(hidden, table2, k2)
-    *feats, delta2, edge, im2h = call(
+    sent, sent2, sent3, kept, delta2, im2h = call(
         halo_body,
-        [tile] * 4 + [((4, 128, 128), BF), tile, ((576, 512), BF)],
+        [((256, 128), BF), tile, tile, tile, ((4, 128, 128), BF), ((576, 512), BF)],
         scratch=[pltpu.VMEM((4, 128, 128), BF), pltpu.VMEM((4, 128, 128), BF)],
-    )(me, halo, pre2, *ups, table2, k2)
-    edge = shifted(edge, SPACE, -1)
-    feats = swap_all(feats)
+    )(me, got, pre2, own, got2, got3, table2, k2)
+    got = rotated(sent, 3)
+    got2 = rotated(sent2, 2)
+    got3 = rotated(sent3, 1)
     (wide,) = call(second_grad_body, [((1728, 128), BF)])(im2, im2h, delta2)
-    (packed,) = call(
+    (rows,) = call(
         back_body,
-        [((432, 128), BF)],
+        [((2304, 128), BF)],
         scratch=[
             pltpu.VMEM((576, 256), BF),
             pltpu.VMEM((4, 256, 128), BF),
-            pltpu.VMEM((864, 64), F32),
+            pltpu.VMEM((576, 128), F32),
+            pltpu.VMEM((4, 576, 1024), BF),
+            pltpu.SemaphoreType.DMA((4,)),
         ],
-    )(delta2, edge, k2, table2, slope1, im1, rimz)
-    packed, wide, *feats = lax.optimization_barrier((packed, wide, *feats))
-    rows = sum_everywhere(packed, wide)
+        far=(1,),
+    )(me, im1, wide, delta2, got, k2, table2, slope1, rimz)
+    rows, got2, got3 = lax.optimization_barrier((rows, got2, got3))
+    rows = sum_everywhere(rows)
     first_grad, second_grad, features = call(
         finish_body,
         [((864, 64), F32), ((1728, 128), F32), ((4, 128, 128), BF)],
         final=True,
-    )(me, rows, *feats)
+    )(me, rows, kept, got, got2, got3)
     features = features.transpose(2, 0, 1).reshape(1, 128, 16, 32)
     return (features, first_grad.reshape(27, 32, 64), second_grad.reshape(27, 64, 128))
 

time: 102 us -> 91.2 us (0.89)
  local copies, waits for them, and re-layouts: 9.28 us -> 1.64 us
  starting transfers between devices: 17.7 us -> 12.9 us
  waiting for transfers between devices: 0.84 us -> 3.24 us
  Pallas kernels: 19.5 us -> 20.8 us
  blocking collectives: 52.8 us -> 51.5 us
    unnamed x19 -> x7, local copies, waits for them, and re-layouts: 7.6 us -> 0.04 us
    ppermute x3 -> x1, starting transfers between devices: 10.2 us -> 6.16 us  [shifted(): lax.ppermute(value, axis, [(source, source + steps) for source in range(i...]
    ppermute x6, waiting for transfers between devices: 0.47 us -> 3.23 us  [rotated(): return lax.ppermute(value, SPACE, [(i, (i + steps) % 4) for i in range(4)])]
    all_to_all x3, blocking collectives: 52.8 us -> 51.5 us  [exchange(): return lax.all_to_all(chunks, axis, split_axis=0, concat_axis=0, tiled=True)]
    pallas_call x8 -> x7, Pallas kernels: 19.5 us -> 20.8 us  [run(): pl.pallas_call(body, in_specs=[scalar if arg.shape == (1,) else there if...]
  transfers between devices with their start and end apart: 9 -> 7, of which waited for: 2 -> 2; matrix products, arithmetic and copies ran while one was open for 0% -> 0% of each run, Pallas kernels for 16% -> 19%
where the time goes in v4:
time: 91.2 us; the launch traced here: 90.9 us
  blocking collectives  51.5 us (56%)
  Pallas kernels  20.8 us (23%)
  starting transfers between devices  12.9 us (14%)
  waiting for transfers between devices  3.24 us (4%)
  local copies, waits for them, and re-layouts  1.64 us (2%)
    all_to_all x3, blocking collectives, exchange(): return lax.all_to_all(chunks, axis, split_axis=0, concat_axis=0, tiled=True)  51.5 us
    pallas_call x7, Pallas kernels, run(): pl.pallas_call(body, in_specs=[scalar if arg.shape == (1,) else there if...  20.8 us
    ppermute x6, starting transfers between devices, rotated(): return lax.ppermute(value, SPACE, [(i, (i + steps) % 4) for i in range(4)])  6.74 us
    ppermute x1, starting transfers between devices, shifted(): lax.ppermute(value, axis, [(source, source + steps) for source in range(i...  6.16 us
    ppermute x6, waiting for transfers between devices, rotated(): return lax.ppermute(value, SPACE, [(i, (i + steps) % 4) for i in range(4)])  3.23 us
  transfers between devices with their start and end apart: 7, of which 2 were waited for; matrix products, arithmetic and copies ran while one was open for 0% of the time, Pallas kernels for 19%

profile of v4, /device:TPU:1, one launch (start us, length us, event | category | flops | bytes accessed | tf_op | source)
XLA Modules:
  0.0 90.9 jit_solution(13171372059978438059)
XLA Ops:
  0.6 1.5 %slice.3 = bf16[4,32,1,512]{3,2,1,0:T(2,128)(2,1)S(1)} slice(bf16[4,32,16,512]{3,2,1,0:T(8,128)(2,1)} %v_hbm.1), slice={[0:4], [0:32], [15:16], [0:512]} | slice | bytes 262144 | tf_op jit(solution)/shard_map/slice | solution.py:329
  2.2 0.0 copy-start.1
  2.2 6.2 %collective-permute-start = (bf16[4,32,512]{2,1,0:T(8,128)(2,1)S(1)}, bf16[4,32,512]{2,1,0:T(8,128)(2,1)S(1)}, u32[]{:S(2)}, u32[]{:S(2)}) collective-permute-start(bf16[4,32,512]{2,1,0:T(8,128)(2,1)S(1)} %bitcast.23), channel_id=1, source_target_pairs={{0,1},{1,2},{2,3},{4,5},{5,6},{6,7},{8,9},{9,10},{10,11},{12,13},{... | collective-permute-start | bytes 393224 | tf_op jit(solution)/shard_map/ppermute | solution.py:24
  8.4 9.7 %shard_map.85 = (bf16[4,576,1024]{2,1,0:T(8,128)(2,1)}, f32[4,64,1024]{2,1,0:T(8,128)S(1)}, bf16[64,288]{1,0:T(8,128)(2,1)S(1)}) custom-call(bf16[4,32,16,512]{3,2,1,0:T(8,128)(2,1)} %v_hbm.1, bf16[512,1152]{1,0:T(8,128)(2,1)} %constant.16.clone.table_hbm.table_ref, bf16[864,64]{1,0:T(8,128)(2,1)} %bitcast.21), custom_call_target="tpu_custom_call" | custom-call | tf_op jit(solution)/shard_map/pallas_call | solution.py:285
  18.0 0.0 copy-start
  18.0 0.0 copy-start.2
  18.1 1.4 %shard_map.86 = (bf16[4,64,1024]{2,1,0:T(8,128)(2,1)S(1)}, bf16[384,128]{1,0:T(8,128)(2,1)S(1)}, bf16[128,128]{1,0:T(8,128)(2,1)S(1)}, bf16[128,128]{1,0:T(8,128...) custom-call(s32[1]{0:T(128)} %bitcast.me_ref, ...), custom_call_target="tpu_custom_call" | custom-call | tf_op jit(solution)/shard_map/pallas_call | solution.py:285
  19.5 0.1 collective-permute-start.1
  19.6 1.3 %collective-permute-start.2 = (bf16[128,128]{1,0:T(8,128)(2,1)S(1)}, bf16[128,128]{1,0:T(8,128)(2,1)S(1)}, u32[]{:S(2)}, u32[]{:S(2)}) collective-permute-start(bf16[128,128]{1,0:T(8,128)(2,1)S(1)} %get-tuple-element.35), channel_id=1, source_target_pairs={{0,2},{1,3},{2,0},{3,1},{4,6},{5,7},{6,4},{7,5},{8,10},{9,11},{10,... | collective-permute-start | bytes 98312 | tf_op jit(solution)/shard_map/ppermute | solution.py:323
  20.9 1.6 %shard_map.87 = (bf16[1728,512]{1,0:T(8,128)(2,1)S(1)}, f32[128,512]{1,0:T(8,128)S(1)}) custom-call(bf16[4,64,1024]{2,1,0:T(8,128)(2,1)S(1)} %get-tuple-element.30.hid_ref, bf16[512,1152]{1,0:T(8,128)(2,1)S(1)} %copy-done, bf16[1728,128]{1,0:T(8,128)(2,1)S(1)} %bitcast.16), custom_call_target="tpu_custom_call" | custom-call | tf_op jit(solution)/shard_map/pallas_call | solution.py:285
  22.5 1.4 %collective-permute-done.2.got2 = bf16[128,128]{1,0:T(8,128)(2,1)S(1)} collective-permute-done((bf16[128,128]{1,0:T(8,128)(2,1)S(1)}, bf16[128,128]{1,0:T(8,128)(2,1)S(1)}, u32[]{:S(2)}, u32[]{:S(2)}) %collective-permute-start.2) | collective-permute-done | bytes 32800 | tf_op jit(solution)/shard_map/ppermute | solution.py:323
  24.0 1.8 %collective-permute-done.3.got3 = bf16[128,128]{1,0:T(8,128)(2,1)S(1)} collective-permute-done((bf16[128,128]{1,0:T(8,128)(2,1)S(1)}, bf16[128,128]{1,0:T(8,128)(2,1)S(1)}, u32[]{:S(2)}, u32[]{:S(2)}) %collective-permute-start.3) | collective-permute-done | bytes 32800 | tf_op jit(solution)/shard_map/ppermute | solution.py:323
  25.8 0.9 shard_map.88
  26.6 0.1 collective-permute-start.4
  26.7 1.8 %collective-permute-start.5 = (bf16[128,128]{1,0:T(8,128)(2,1)S(1)}, bf16[128,128]{1,0:T(8,128)(2,1)S(1)}, u32[]{:S(2)}, u32[]{:S(2)}) collective-permute-start(bf16[128,128]{1,0:T(8,128)(2,1)S(1)} %get-tuple-element.42), channel_id=1, source_target_pairs={{0,2},{1,3},{2,0},{3,1},{4,6},{5,7},{6,4},{7,5},{8,10},{9,11},{10,... | collective-permute-start | bytes 98312 | tf_op jit(solution)/shard_map/ppermute | solution.py:323
  28.6 3.4 %collective-permute-start.6 = (bf16[128,128]{1,0:T(8,128)(2,1)S(1)}, bf16[128,128]{1,0:T(8,128)(2,1)S(1)}, u32[]{:S(2)}, u32[]{:S(2)}) collective-permute-start(bf16[128,128]{1,0:T(8,128)(2,1)S(1)} %get-tuple-element.43), channel_id=1, source_target_pairs={{0,1},{1,2},{2,3},{3,0},{4,5},{5,6},{6,7},{7,4},{8,9},{9,10},{10,1... | collective-permute-start | bytes 98312 | tf_op jit(solution)/shard_map/ppermute | solution.py:323
  32.0 0.6 shard_map.89.wide_ref
  32.6 5.4 %shard_map.90 = bf16[2304,128]{1,0:T(8,128)(2,1)S(1)} custom-call(s32[1]{0:T(128)} %bitcast.me_ref, bf16[4,576,1024]{2,1,0:T(8,128)(2,1)} %get-tuple-element.27.im_hbm, bf16[1728,128]{1,0:T(8,128)(2,1)S(1)} %shard_map.89.wide_ref, bf16[4,128,128]{2,1,0:T(8,128)(2,1)S(1)} %get-tuple-element.38.delta_ref, bf16[256,128]{1,0:T(8,128)(2,1)S(1)} %collective-permute-done.4.got_ref, ...), custom_call_target="tpu_custom_call" | custom-call | tf_op jit(solution)/shard_map/pallas_call | solution.py:285
  38.0 17.4 %all_to_all.15 = bf16[32,72,128]{2,1,0:T(8,128)(2,1)S(1)} all-to-all(bf16[32,72,128]{2,1,0:T(8,128)(2,1)S(1)} %bitcast.19), channel_id=1, replica_groups=mesh['y'=4,'z'=8,'xl'=2,'xh'=2,'c'=2] {'y','xl','xh','c'}, dimensions={0} | all-to-all | bytes 1179648 | tf_op jit(solution)/shard_map/all_to_all | solution.py:302
  55.4 0.1 reduce_sum.24
  55.6 17.0 %all_to_all.16 = bf16[8,72,128]{2,1,0:T(8,128)(2,1)S(1)} all-to-all(bf16[8,72,128]{2,1,0:T(8,128)(2,1)S(1)} %broadcast_in_dim.4), channel_id=1, replica_groups=mesh['y'=4,'z'=8,'xl'=2,'xh'=2,'c'=2] {'z'}, dimensions={0} | all-to-all | bytes 294912 | tf_op jit(solution)/shard_map/all_to_all | solution.py:302
  72.6 0.1 broadcast_in_dim.5
  72.7 17.1 %all_to_all.17 = bf16[32,72,128]{2,1,0:T(8,128)(2,1)S(1)} all-to-all(bf16[32,72,128]{2,1,0:T(8,128)(2,1)S(1)} %broadcast_in_dim.5), channel_id=1, replica_groups=mesh['y'=4,'z'=8,'xl'=2,'xh'=2,'c'=2] {'y','xl','xh','c'}, dimensions={0} | all-to-all | bytes 1179648 | tf_op jit(solution)/shard_map/all_to_all | solution.py:302
  89.8 1.2 %shard_map.91 = (f32[864,64]{1,0:T(8,128)}, f32[1728,128]{1,0:T(8,128)}, bf16[4,128,128]{2,1,0:T(8,128)(2,1)}) custom-call(s32[1]{0:T(128)} %bitcast.me_ref, bf16[2304,128]{1,0:T(8,128)(2,1)S(1)} %bitcast.20, bf16[128,128]{1,0:T(8,128)(2,1)S(1)} %get-tuple-element.45.kept_ref, bf16[256,128]{1,0:T(8,128)(2,1)S(1)} %collective-permute-done.4.got_ref, ...), custom_call_target="tpu_custom_call" | custom-call | tf_op jit(solution)/shard_map/pallas_call | solution.py:285
  (12 shorter events, 0.1 us)
Async XLA Ops:
  2.2 15.9 %copy-start.1 = (bf16[512,1152]{1,0:T(8,128)(2,1)S(1)}, bf16[512,1152]{1,0:T(8,128)(2,1)}, u32[]{:S(2)}) copy-start(bf16[512,1152]{1,0:T(8,128)(2,1)} %constant.16.clone.table_hbm.table_ref) | copy-start | bytes 3538948
  2.2 15.9 %collective-permute-start = (bf16[4,32,512]{2,1,0:T(8,128)(2,1)S(1)}, bf16[4,32,512]{2,1,0:T(8,128)(2,1)S(1)}, u32[]{:S(2)}, u32[]{:S(2)}) collective-permute-start(bf16[4,32,512]{2,1,0:T(8,128)(2,1)S(1)} %bitcast.23), channel_id=1, source_target_pairs={{0,1},{1,2},{2,3},{4,5},{5,6},{6,7},{8,9},{9,10},{10,11},{12,13},{... | collective-permute-start | bytes 393224 | tf_op jit(solution)/shard_map/ppermute | solution.py:24
  18.0 2.9 %copy-start = (bf16[512,1152]{1,0:T(8,128)(2,1)S(1)}, bf16[512,1152]{1,0:T(8,128)(2,1)}, u32[]{:S(2)}) copy-start(bf16[512,1152]{1,0:T(8,128)(2,1)} %constant.17.clone.table_ref) | copy-start | bytes 3538948
  18.0 2.9 %copy-start.2 = (bf16[27,64,128]{2,1,0:T(8,128)(2,1)S(1)}, bf16[27,64,128]{2,1,0:T(8,128)(2,1)}, u32[]{:S(2)}) copy-start(bf16[27,64,128]{2,1,0:T(8,128)(2,1)} %param.8) | copy-start | bytes 1327108
  19.5 6.2 %collective-permute-start.1 = (bf16[384,128]{1,0:T(8,128)(2,1)S(1)}, bf16[384,128]{1,0:T(8,128)(2,1)S(1)}, u32[]{:S(2)}, u32[]{:S(2)}) collective-permute-start(bf16[384,128]{1,0:T(8,128)(2,1)S(1)} %get-tuple-element.32), channel_id=1, source_target_pairs={{0,1},{1,2},{2,3},{3,0},{4,5},{5,6},{6,7},{7,4},{8,9},{9,10},{10,1... | collective-permute-start | bytes 294920 | tf_op jit(solution)/shard_map/ppermute | solution.py:323
  19.6 4.4 %collective-permute-start.2 = (bf16[128,128]{1,0:T(8,128)(2,1)S(1)}, bf16[128,128]{1,0:T(8,128)(2,1)S(1)}, u32[]{:S(2)}, u32[]{:S(2)}) collective-permute-start(bf16[128,128]{1,0:T(8,128)(2,1)S(1)} %get-tuple-element.35), channel_id=1, source_target_pairs={{0,2},{1,3},{2,0},{3,1},{4,6},{5,7},{6,4},{7,5},{8,10},{9,11},{10,... | collective-permute-start | bytes 98312 | tf_op jit(solution)/shard_map/ppermute | solution.py:323
  20.9 4.8 %collective-permute-start.3 = (bf16[128,128]{1,0:T(8,128)(2,1)S(1)}, bf16[128,128]{1,0:T(8,128)(2,1)S(1)}, u32[]{:S(2)}, u32[]{:S(2)}) collective-permute-start(bf16[128,128]{1,0:T(8,128)(2,1)S(1)} %get-tuple-element.36), channel_id=1, source_target_pairs={{0,3},{1,0},{2,1},{3,2},{4,7},{5,4},{6,5},{7,6},{8,11},{9,8},{10,9... | collective-permute-start | bytes 98312 | tf_op jit(solution)/shard_map/ppermute | solution.py:323
  26.6 6.0 %collective-permute-start.4 = (bf16[256,128]{1,0:T(8,128)(2,1)S(1)}, bf16[256,128]{1,0:T(8,128)(2,1)S(1)}, u32[]{:S(2)}, u32[]{:S(2)}) collective-permute-start(bf16[256,128]{1,0:T(8,128)(2,1)S(1)} %get-tuple-element.39), channel_id=1, source_target_pairs={{0,3},{1,0},{2,1},{3,2},{4,7},{5,4},{6,5},{7,6},{8,11},{9,8},{10,9... | collective-permute-start | bytes 196616 | tf_op jit(solution)/shard_map/ppermute | solution.py:323
  26.7 11.3 %collective-permute-start.5 = (bf16[128,128]{1,0:T(8,128)(2,1)S(1)}, bf16[128,128]{1,0:T(8,128)(2,1)S(1)}, u32[]{:S(2)}, u32[]{:S(2)}) collective-permute-start(bf16[128,128]{1,0:T(8,128)(2,1)S(1)} %get-tuple-element.42), channel_id=1, source_target_pairs={{0,2},{1,3},{2,0},{3,1},{4,6},{5,7},{6,4},{7,5},{8,10},{9,11},{10,... | collective-permute-start | bytes 98312 | tf_op jit(solution)/shard_map/ppermute | solution.py:323
  28.6 9.5 %collective-permute-start.6 = (bf16[128,128]{1,0:T(8,128)(2,1)S(1)}, bf16[128,128]{1,0:T(8,128)(2,1)S(1)}, u32[]{:S(2)}, u32[]{:S(2)}) collective-permute-start(bf16[128,128]{1,0:T(8,128)(2,1)S(1)} %get-tuple-element.43), channel_id=1, source_target_pairs={{0,1},{1,2},{2,3},{3,0},{4,5},{5,6},{6,7},{7,4},{8,9},{9,10},{10,1... | collective-permute-start | bytes 98312 | tf_op jit(solution)/shard_map/ppermute | solution.py:323

commit v5 on v4

--- a/solution.py
+++ b/solution.py
@@ -24,19 +24,45 @@
     return lax.ppermute(value, axis, [(source, source + steps) for source in range(initial, last)])
 
 
-def plane_table(size_y, size_z, copies):
-    half_y, half_z = size_y // 2, size_z // 2
-    cells = half_y * half_z
-    table = np.zeros((copies, size_y * size_z, 9, copies, cells), np.float32)
+def phase_table(size_y, size_z, copies):
+    shape = (copies, size_y // 2, 2, size_z // 2, 2)
+    at = np.arange(np.prod(shape)).reshape(shape).transpose(2, 4, 0, 1, 3).reshape(-1)
+    return jnp.asarray(np.eye(at.size, dtype=np.float32)[:, at], BF)
+
+
+def tap_masks(shape, row, cells):
+    lane = lax.broadcasted_iota(jnp.int32, shape, 1) % cells
+    return lane >= row, lane % row != 0
+
+
+def tap_parts(row):
     for second in range(3):
         for third in range(3):
-            for out_y in range(half_y):
-                for out_z in range(half_z):
-                    y, z = 2 * out_y + second - 1, 2 * out_z + third - 1
-                    if y >= 0 and z >= 0:
-                        for k in range(copies):
-                            table[k, y * size_z + z, 3 * second + third, k, out_y * half_z + out_z] = 1
-    return jnp.asarray(table.reshape(copies * size_y * size_z, 9 * copies * cells), BF)
+            back_y, back_z = second == 0, third == 0
+            yield 2 * (second != 1) + (third != 1), row * back_y + back_z, back_y, back_z
+
+
+def spread(phases, row, cells):
+    in_y, in_z = tap_masks((phases.shape[0], LANES), row, cells)
+    taps = []
+    for phase, steps, back_y, back_z in tap_parts(row):
+        tap = phases[:, phase * LANES : (phase + 1) * LANES]
+        if steps:
+            mask = in_y & in_z if back_y and back_z else in_y if back_y else in_z
+            tap = jnp.where(mask, pltpu.roll(tap, steps, 1), 0.0)
+        taps.append(tap)
+    return taps
+
+
+def collect(taps, row, cells):
+    in_y, in_z = tap_masks(taps[0].shape, row, cells)
+    phases = [None] * 4
+    for tap, (phase, steps, back_y, back_z) in zip(taps, tap_parts(row)):
+        if steps:
+            mask = in_y & in_z if back_y and back_z else in_y if back_y else in_z
+            tap = pltpu.roll(jnp.where(mask, tap, 0.0), LANES - steps, 1)
+        phases[phase] = tap if phases[phase] is None else phases[phase] + tap
+    return jnp.concatenate(phases, 1)
 
 
 def row_order(chans, rows):
@@ -70,39 +96,39 @@
     return act, slope
 
 
-def first_body(
-    v_hbm, table_hbm, w_hbm, im_hbm, pre_ref, wt0_ref, v_ref, table_ref, w_ref, order_ref, z_ref, im_ref, sems, v_sems, im_sems
+def load_body(
+    v_hbm, w_hbm, table_hbm, rows_ref, rim_ref, wt_ref, wt0_ref, table_ref, v_ref, w_ref, sems, v_sems
 ):
     fetch_w = pltpu.make_async_copy(w_hbm, w_ref, sems.at[0])
     fetch_table = pltpu.make_async_copy(table_hbm, table_ref, sems.at[1])
-    fetch_w.start()
     fetch_v = [pltpu.make_async_copy(v_hbm.at[s], v_ref.at[s], v_sems.at[s]) for s in range(4)]
-    fetch_v[0].start()
-    fetch_table.start()
-    for s in range(1, 4):
-        fetch_v[s].start()
-    order_ref[...] = row_order(32, 16)
+    for fetch in [fetch_w] + fetch_v + [fetch_table]:
+        fetch.start()
+    order = row_order(32, 16)
     fetch_w.wait()
     w = w_ref[...]
     below = jnp.concatenate([jnp.zeros((288, 64), BF), w[:288]], 0)
-    wt = turned(jnp.concatenate([w[288:], below], 1)).astype(BF)
+    wt_ref[...] = turned(jnp.concatenate([w[288:], below], 1)).astype(BF)
     wt0_ref[...] = turned(w[:288]).astype(BF)
+    for s in range(4):
+        fetch_v[s].wait()
+        rows = dot(order, v_ref[s].reshape(512, 512)).astype(BF)
+        rows_ref[s] = rows
+        rim_ref[s] = rows[480:]
     fetch_table.wait()
 
+
+def first_body(rows_ref, table_ref, wt_ref, im_hbm, pre_ref, z_ref, im_ref, im_sems):
     def one(s, carry):
-        pltpu.make_async_copy(v_hbm.at[s], v_ref.at[s], v_sems.at[s]).wait()
-        rows = dot(order_ref[...], v_ref[s].reshape(512, 512)).astype(BF)
-        z_ref[...] = dot(rows, table_ref[...]).astype(BF)
+        z_ref[...] = dot(rows_ref[s], table_ref[...])
         for half in range(2):
             for o1 in range(8):
                 at = (half * 8 + o1) * 32
-                for t in range(9):
+                for t, tap in enumerate(spread(z_ref[at : at + 32], 8, 128)):
                     k = (9 * half + t) * 32
-                    im_ref[s, k : k + 32, o1 * LANES : (o1 + 1) * LANES] = z_ref[
-                        at : at + 32, t * LANES : (t + 1) * LANES
-                    ]
+                    im_ref[s, k : k + 32, o1 * LANES : (o1 + 1) * LANES] = tap.astype(BF)
         pltpu.make_async_copy(im_ref.at[s], im_hbm.at[s], im_sems.at[s]).start()
-        got = dot(wt, im_ref[s])
+        got = dot(wt_ref[...], im_ref[s])
         pre_ref[s, :, :LANES] = got[:64, :LANES]
         pre_ref[s, :, LANES:] = got[:64, LANES:] + got[64:, :-LANES]
         return carry
@@ -117,11 +143,9 @@
 ):
     fetch = pltpu.make_async_copy(up_hbm, up_ref, sem)
     fetch.start()
-    z = dot(rim_ref[...].reshape(128, 512), table_ref[...]).astype(BF)
-    for s in range(4):
-        im = jnp.concatenate(
-            [z[32 * s : 32 * s + 32, t * LANES : (t + 1) * LANES] for t in range(9)], 0
-        )
+    taps = spread(dot(rim_ref[...].reshape(128, 512), table_ref[...]), 8, 128)
+    for s in range(4):
+        im = jnp.concatenate([tap[32 * s : 32 * s + 32] for tap in taps], 0).astype(BF)
         rimz_ref[s] = im
         extra = dot(wt0_ref[...], im)
         for r in range(8):
@@ -151,13 +175,12 @@
         left = jnp.concatenate(
             [jnp.concatenate([row(2 * o1 + a - 1) for o1 in range(4)], 1) for a in range(3)], 0
         )
-        z = dot(left, table_ref[...]).astype(BF)
-        for a in range(3):
-            for t in range(9):
+        for t, tap in enumerate(spread(dot(left, table_ref[...]), 4, 32)):
+            for a in range(3):
                 k = (9 * a + t) * 64
-                im_ref[k : k + 64, s * LANES : (s + 1) * LANES] = z[
-                    64 * a : 64 * a + 64, t * LANES : (t + 1) * LANES
-                ]
+                im_ref[k : k + 64, s * LANES : (s + 1) * LANES] = tap[
+                    64 * a : 64 * a + 64
+                ].astype(BF)
     pre_ref[...] = dot(turned(w_ref[...]).astype(BF), im_ref[...])
 
 
@@ -169,12 +192,11 @@
     up_ref[(me + 2) & 3] = got2[...]
     up_ref[(me + 3) & 3] = got_ref[256:]
     z = dot(got_ref[:256], table_ref[:LANES, :])
-    z = jnp.where(me > 0, z, 0.0).astype(BF)
-    for s in range(4):
-        for t in range(9):
-            imh_ref[t * 64 : t * 64 + 64, s * LANES : (s + 1) * LANES] = z[
-                64 * s : 64 * s + 64, t * LANES : (t + 1) * LANES
-            ]
+    for t, tap in enumerate(spread(jnp.where(me > 0, z, 0.0), 4, 32)):
+        for s in range(4):
+            imh_ref[t * 64 : t * 64 + 64, s * LANES : (s + 1) * LANES] = tap[
+                64 * s : 64 * s + 64
+            ].astype(BF)
     pre = pre_ref[...] + dot(turned(w_ref[:576]).astype(BF), imh_ref[...])
     lane = lax.broadcasted_iota(jnp.int32, (128, LANES), 1)
     edge = jnp.zeros((128, LANES), F32)
@@ -223,7 +245,7 @@
         odd = dot(kodd_ref[...], ahead_ref[s])
         parts = []
         for grad in (even, odd):
-            flat = jnp.concatenate([grad[64 * t : 64 * t + 64] for t in range(9)], 1)
+            flat = collect([grad[64 * t : 64 * t + 64] for t in range(9)], 4, 32)
             high = flat.astype(BF)
             parts += [high, (flat - high.astype(F32)).astype(BF)]
         got = dot_nt(jnp.concatenate(parts, 0), table_ref[...])
@@ -324,31 +346,40 @@
 
 
 def per_device(volumes, first_kernel, second_kernel, upstream):
-    table = plane_table(YD, ZD, 1)
-    table2 = plane_table(YD // 2, ZD // 2, 4)
-    rim = shifted(volumes[:, :, 15, :], SPACE, 1)
     me = lax.axis_index(SPACE).reshape(1)
     tile = ((128, 128), BF)
+    table = phase_table(YD, ZD, 1)
+    table2 = phase_table(YD // 2, ZD // 2, 4)
+    k2 = second_kernel.reshape(1728, 128)
     up = upstream.reshape(128, 4, 128).transpose(1, 2, 0)
-    w1 = first_kernel.reshape(864, 64)
-    k2 = second_kernel.reshape(1728, 128)
-    im1, pre1, wt0 = call(
-        first_body,
-        [((4, 576, 1024), BF), ((4, 64, 1024), F32), ((64, 288), BF)],
+    rows, rim, wt, wt0, near_table = call(
+        load_body,
+        [
+            ((4, 512, 512), BF),
+            ((4, 32, 512), BF),
+            ((128, 576), BF),
+            ((64, 288), BF),
+            ((512, 512), BF),
+        ],
         scratch=[
             pltpu.VMEM((4, 32, 16, 512), BF),
-            pltpu.VMEM((512, 1152), BF),
             pltpu.VMEM((864, 64), BF),
-            pltpu.VMEM((512, 512), BF),
-            pltpu.VMEM((512, 1152), BF),
-            pltpu.VMEM((4, 576, 1024), BF),
             pltpu.SemaphoreType.DMA((2,)),
-            pltpu.SemaphoreType.DMA((4,)),
             pltpu.SemaphoreType.DMA((4,)),
         ],
         far=(0, 1, 2),
+    )(volumes, first_kernel.reshape(864, 64), table)
+    rim = shifted(rim, SPACE, 1)
+    im1, pre1 = call(
+        first_body,
+        [((4, 576, 1024), BF), ((4, 64, 1024), F32)],
+        scratch=[
+            pltpu.VMEM((512, 512), F32),
+            pltpu.VMEM((4, 576, 1024), BF),
+            pltpu.SemaphoreType.DMA((4,)),
+        ],
         far_outs=(0,),
-    )(volumes, table, w1)
+    )(rows, near_table, wt)
     hidden, sent, sent2, sent3, own, slope1, rimz = call(
         rim_body,
         [

time: 91.2 us -> 89.7 us (0.984)
  Pallas kernels: 20.8 us -> 18.7 us
  starting transfers between devices: 12.9 us -> 14.9 us
  local copies, waits for them, and re-layouts: 1.64 us -> 0.12 us
    pallas_call x7 -> x8, Pallas kernels: 20.8 us -> 18.7 us  [run(): pl.pallas_call(body, in_specs=[scalar if arg.shape == (1,) else there if...]
    ppermute x6, starting transfers between devices: 6.74 us -> 8.74 us  [rotated(): return lax.ppermute(value, SPACE, [(i, (i + steps) % 4) for i in range(4)])]
    slice x1 -> x0, local copies, waits for them, and re-layouts: 1.5 us -> none  [per_device(): rim = shifted(volumes[:, :, 15, :], SPACE, 1)]
  transfers between devices with their start and end apart: 7 -> 7, of which waited for: 2 -> 2; matrix products, arithmetic and copies ran while one was open for 0% -> 0% of each run, Pallas kernels for 19% -> 13%
where the time goes in v5:
time: 89.7 us; the launch traced here: 89.4 us
  blocking collectives  51.5 us (57%)
  Pallas kernels  18.7 us (21%)
  starting transfers between devices  14.9 us (17%)
  waiting for transfers between devices  3.33 us (4%)
    all_to_all x3, blocking collectives, exchange(): return lax.all_to_all(chunks, axis, split_axis=0, concat_axis=0, tiled=True)  51.5 us
    pallas_call x8, Pallas kernels, run(): pl.pallas_call(body, in_specs=[scalar if arg.shape == (1,) else there if...  18.7 us
    ppermute x6, starting transfers between devices, rotated(): return lax.ppermute(value, SPACE, [(i, (i + steps) % 4) for i in range(4)])  8.74 us
    ppermute x1, starting transfers between devices, shifted(): lax.ppermute(value, axis, [(source, source + steps) for source in range(i...  6.16 us
    ppermute x6, waiting for transfers between devices, rotated(): return lax.ppermute(value, SPACE, [(i, (i + steps) % 4) for i in range(4)])  3.33 us
  transfers between devices with their start and end apart: 7, of which 2 were waited for; matrix products, arithmetic and copies ran while one was open for 0% of the time, Pallas kernels for 13%

profile of v5, /device:TPU:1, one launch (start us, length us, event | category | flops | bytes accessed | tf_op | source)
XLA Modules:
  0.0 89.4 jit_solution(18060142425650540786)
XLA Ops:
  0.6 4.0 %shard_map.85 = (bf16[4,512,512]{2,1,0:T(8,128)(2,1)S(1)}, bf16[4,32,512]{2,1,0:T(8,128)(2,1)}, bf16[128,576]{1,0:T(8,128)(2,1)S(1)}, bf16[64,288]{1,0:T(8,128)(2,1)S(1)}, bf16[512,512]{1,0:T(8,128)(2,1)S(1)}) custom-call(bf16[4,32,16,512]{3,2,1,0:T(8,128)(2,1)} %v_hbm.1, bf16[864,64]{1,0:T(8,128)(2,1)} %bitcast.18, ...), custom_call_target="tpu_custom_call" | custom-call | tf_op jit(solution)/shard_map/pallas_call | solution.py:307
  4.7 0.0 copy-start.2
  4.7 6.2 %collective-permute-start = (bf16[4,32,512]{2,1,0:T(8,128)(2,1)}, bf16[4,32,512]{2,1,0:T(8,128)(2,1)S(1)}, u32[]{:S(2)}, u32[]{:S(2)}) collective-permute-start(bf16[4,32,512]{2,1,0:T(8,128)(2,1)} %get-tuple-element.36), channel_id=1, source_target_pairs={{0,1},{1,2},{2,3},{4,5},{5,6},{6,7},{8,9},{9,10},{10,11},{12,13},{... | collective-permute-start | bytes 393224 | tf_op jit(solution)/shard_map/ppermute | solution.py:24
  10.9 0.0 copy-start
  10.9 0.0 copy-start.1
  10.9 4.4 %shard_map.86 = (bf16[4,576,1024]{2,1,0:T(8,128)(2,1)}, f32[4,64,1024]{2,1,0:T(8,128)S(1)}) custom-call(bf16[4,512,512]{2,1,0:T(8,128)(2,1)S(1)} %get-tuple-element.31.rows_ref, bf16[512,512]{1,0:T(8,128)(2,1)S(1)} %get-tuple-element.32.table_ref, bf16[128,576]{1,0:T(8,128)(2,1)S(1)} %get-tuple-element.33.wt_ref), custom_call_target="tpu_custom_call" | custom-call | tf_op jit(solution)/shard_map/pallas_call | solution.py:307
  15.3 1.4 %shard_map.87 = (bf16[4,64,1024]{2,1,0:T(8,128)(2,1)S(1)}, bf16[384,128]{1,0:T(8,128)(2,1)S(1)}, bf16[128,128]{1,0:T(8,128)(2,1)S(1)}, bf16[128,128]{1,0:T(8,128...) custom-call(s32[1]{0:T(128)} %bitcast.me_ref, ...), custom_call_target="tpu_custom_call" | custom-call | tf_op jit(solution)/shard_map/pallas_call | solution.py:307
  16.8 1.7 %collective-permute-start.1 = (bf16[384,128]{1,0:T(8,128)(2,1)S(1)}, bf16[384,128]{1,0:T(8,128)(2,1)S(1)}, u32[]{:S(2)}, u32[]{:S(2)}) collective-permute-start(bf16[384,128]{1,0:T(8,128)(2,1)S(1)} %get-tuple-element.40), channel_id=1, source_target_pairs={{0,1},{1,2},{2,3},{3,0},{4,5},{5,6},{6,7},{7,4},{8,9},{9,10},{10,1... | collective-permute-start | bytes 294920 | tf_op jit(solution)/shard_map/ppermute | solution.py:345
  18.4 0.5 collective-permute-start.3
  18.9 1.0 %shard_map.88 = (bf16[1728,512]{1,0:T(8,128)(2,1)S(1)}, f32[128,512]{1,0:T(8,128)S(1)}) custom-call(bf16[4,64,1024]{2,1,0:T(8,128)(2,1)S(1)} %get-tuple-element.38.hid_ref, bf16[512,512]{1,0:T(8,128)(2,1)S(1)} %copy-done, bf16[1728,128]{1,0:T(8,128)(2,1)S(1)} %bitcast.13), custom_call_target="tpu_custom_call" | custom-call | tf_op jit(solution)/shard_map/pallas_call | solution.py:307
  19.9 2.7 %collective-permute-done.2.got2 = bf16[128,128]{1,0:T(8,128)(2,1)S(1)} collective-permute-done((bf16[128,128]{1,0:T(8,128)(2,1)S(1)}, bf16[128,128]{1,0:T(8,128)(2,1)S(1)}, u32[]{:S(2)}, u32[]{:S(2)}) %collective-permute-start.2) | collective-permute-done | bytes 32800 | tf_op jit(solution)/shard_map/ppermute | solution.py:345
  22.7 0.6 collective-permute-done.3.got3
  23.3 0.9 shard_map.89
  24.2 0.2 collective-permute-start.4
  24.3 2.9 %collective-permute-start.5 = (bf16[128,128]{1,0:T(8,128)(2,1)S(1)}, bf16[128,128]{1,0:T(8,128)(2,1)S(1)}, u32[]{:S(2)}, u32[]{:S(2)}) collective-permute-start(bf16[128,128]{1,0:T(8,128)(2,1)S(1)} %get-tuple-element.50), channel_id=1, source_target_pairs={{0,2},{1,3},{2,0},{3,1},{4,6},{5,7},{6,4},{7,5},{8,10},{9,11},{10,... | collective-permute-start | bytes 98312 | tf_op jit(solution)/shard_map/ppermute | solution.py:345
  27.3 3.4 %collective-permute-start.6 = (bf16[128,128]{1,0:T(8,128)(2,1)S(1)}, bf16[128,128]{1,0:T(8,128)(2,1)S(1)}, u32[]{:S(2)}, u32[]{:S(2)}) collective-permute-start(bf16[128,128]{1,0:T(8,128)(2,1)S(1)} %get-tuple-element.51), channel_id=1, source_target_pairs={{0,1},{1,2},{2,3},{3,0},{4,5},{5,6},{6,7},{7,4},{8,9},{9,10},{10,1... | collective-permute-start | bytes 98312 | tf_op jit(solution)/shard_map/ppermute | solution.py:345
  30.7 0.6 shard_map.90.wide_ref
  31.4 5.1 %shard_map.91 = bf16[2304,128]{1,0:T(8,128)(2,1)S(1)} custom-call(s32[1]{0:T(128)} %bitcast.me_ref, bf16[4,576,1024]{2,1,0:T(8,128)(2,1)} %get-tuple-element.34.im_hbm, bf16[1728,128]{1,0:T(8,128)(2,1)S(1)} %shard_map.90.wide_ref, bf16[4,128,128]{2,1,0:T(8,128)(2,1)S(1)} %get-tuple-element.46.delta_ref, bf16[256,128]{1,0:T(8,128)(2,1)S(1)} %collective-permute-done.4.got_ref, ...), custom_call_target="tpu_custom_call" | custom-call | tf_op jit(solution)/shard_map/pallas_call | solution.py:307
  36.5 17.4 %all_to_all.15 = bf16[32,72,128]{2,1,0:T(8,128)(2,1)S(1)} all-to-all(bf16[32,72,128]{2,1,0:T(8,128)(2,1)S(1)} %bitcast.16), channel_id=1, replica_groups=mesh['y'=4,'z'=8,'xl'=2,'xh'=2,'c'=2] {'y','xl','xh','c'}, dimensions={0} | all-to-all | bytes 1179648 | tf_op jit(solution)/shard_map/all_to_all | solution.py:324
  53.9 0.1 reduce_sum.24
  54.0 17.0 %all_to_all.16 = bf16[8,72,128]{2,1,0:T(8,128)(2,1)S(1)} all-to-all(bf16[8,72,128]{2,1,0:T(8,128)(2,1)S(1)} %broadcast_in_dim.4), channel_id=1, replica_groups=mesh['y'=4,'z'=8,'xl'=2,'xh'=2,'c'=2] {'z'}, dimensions={0} | all-to-all | bytes 294912 | tf_op jit(solution)/shard_map/all_to_all | solution.py:324
  71.1 0.1 broadcast_in_dim.5
  71.2 17.1 %all_to_all.17 = bf16[32,72,128]{2,1,0:T(8,128)(2,1)S(1)} all-to-all(bf16[32,72,128]{2,1,0:T(8,128)(2,1)S(1)} %broadcast_in_dim.5), channel_id=1, replica_groups=mesh['y'=4,'z'=8,'xl'=2,'xh'=2,'c'=2] {'y','xl','xh','c'}, dimensions={0} | all-to-all | bytes 1179648 | tf_op jit(solution)/shard_map/all_to_all | solution.py:324
  88.2 1.2 %shard_map.92 = (f32[864,64]{1,0:T(8,128)}, f32[1728,128]{1,0:T(8,128)}, bf16[4,128,128]{2,1,0:T(8,128)(2,1)}) custom-call(s32[1]{0:T(128)} %bitcast.me_ref, bf16[2304,128]{1,0:T(8,128)(2,1)S(1)} %bitcast.17, bf16[128,128]{1,0:T(8,128)(2,1)S(1)} %get-tuple-element.53.kept_ref, bf16[256,128]{1,0:T(8,128)(2,1)S(1)} %collective-permute-done.4.got_ref, ...), custom_call_target="tpu_custom_call" | custom-call | tf_op jit(solution)/shard_map/pallas_call | solution.py:307
  (11 shorter events, 0.1 us)
Async XLA Ops:
  4.7 10.7 %copy-start.2 = (bf16[512,512]{1,0:T(8,128)(2,1)S(1)}, bf16[512,512]{1,0:T(8,128)(2,1)}, u32[]{:S(2)}) copy-start(bf16[512,512]{1,0:T(8,128)(2,1)} %constant.16.clone.table_hbm.table_ref) | copy-start | bytes 1572868
  4.7 10.6 %collective-permute-start = (bf16[4,32,512]{2,1,0:T(8,128)(2,1)}, bf16[4,32,512]{2,1,0:T(8,128)(2,1)S(1)}, u32[]{:S(2)}, u32[]{:S(2)}) collective-permute-start(bf16[4,32,512]{2,1,0:T(8,128)(2,1)} %get-tuple-element.36), channel_id=1, source_target_pairs={{0,1},{1,2},{2,3},{4,5},{5,6},{6,7},{8,9},{9,10},{10,11},{12,13},{... | collective-permute-start | bytes 393224 | tf_op jit(solution)/shard_map/ppermute | solution.py:24
  10.9 8.1 %copy-start = (bf16[512,512]{1,0:T(8,128)(2,1)S(1)}, bf16[512,512]{1,0:T(8,128)(2,1)}, u32[]{:S(2)}) copy-start(bf16[512,512]{1,0:T(8,128)(2,1)} %constant.17.clone.table_ref) | copy-start | bytes 1572868
  10.9 8.1 %copy-start.1 = (bf16[27,64,128]{2,1,0:T(8,128)(2,1)S(1)}, bf16[27,64,128]{2,1,0:T(8,128)(2,1)}, u32[]{:S(2)}) copy-start(bf16[27,64,128]{2,1,0:T(8,128)(2,1)} %param.8) | copy-start | bytes 1327108
  16.8 6.5 %collective-permute-start.1 = (bf16[384,128]{1,0:T(8,128)(2,1)S(1)}, bf16[384,128]{1,0:T(8,128)(2,1)S(1)}, u32[]{:S(2)}, u32[]{:S(2)}) collective-permute-start(bf16[384,128]{1,0:T(8,128)(2,1)S(1)} %get-tuple-element.40), channel_id=1, source_target_pairs={{0,1},{1,2},{2,3},{3,0},{4,5},{5,6},{6,7},{7,4},{8,9},{9,10},{10,1... | collective-permute-start | bytes 294920 | tf_op jit(solution)/shard_map/ppermute | solution.py:345
  18.4 4.3 %collective-permute-start.2 = (bf16[128,128]{1,0:T(8,128)(2,1)S(1)}, bf16[128,128]{1,0:T(8,128)(2,1)S(1)}, u32[]{:S(2)}, u32[]{:S(2)}) collective-permute-start(bf16[128,128]{1,0:T(8,128)(2,1)S(1)} %get-tuple-element.43), channel_id=1, source_target_pairs={{0,2},{1,3},{2,0},{3,1},{4,6},{5,7},{6,4},{7,5},{8,10},{9,11},{10,... | collective-permute-start | bytes 98312 | tf_op jit(solution)/shard_map/ppermute | solution.py:345
  18.4 4.8 %collective-permute-start.3 = (bf16[128,128]{1,0:T(8,128)(2,1)S(1)}, bf16[128,128]{1,0:T(8,128)(2,1)S(1)}, u32[]{:S(2)}, u32[]{:S(2)}) collective-permute-start(bf16[128,128]{1,0:T(8,128)(2,1)S(1)} %get-tuple-element.44), channel_id=1, source_target_pairs={{0,3},{1,0},{2,1},{3,2},{4,7},{5,4},{6,5},{7,6},{8,11},{9,8},{10,9... | collective-permute-start | bytes 98312 | tf_op jit(solution)/shard_map/ppermute | solution.py:345
  24.2 7.2 %collective-permute-start.4 = (bf16[256,128]{1,0:T(8,128)(2,1)S(1)}, bf16[256,128]{1,0:T(8,128)(2,1)S(1)}, u32[]{:S(2)}, u32[]{:S(2)}) collective-permute-start(bf16[256,128]{1,0:T(8,128)(2,1)S(1)} %get-tuple-element.47), channel_id=1, source_target_pairs={{0,3},{1,0},{2,1},{3,2},{4,7},{5,4},{6,5},{7,6},{8,11},{9,8},{10,9... | collective-permute-start | bytes 196616 | tf_op jit(solution)/shard_map/ppermute | solution.py:345
  24.3 12.1 %collective-permute-start.5 = (bf16[128,128]{1,0:T(8,128)(2,1)S(1)}, bf16[128,128]{1,0:T(8,128)(2,1)S(1)}, u32[]{:S(2)}, u32[]{:S(2)}) collective-permute-start(bf16[128,128]{1,0:T(8,128)(2,1)S(1)} %get-tuple-element.50), channel_id=1, source_target_pairs={{0,2},{1,3},{2,0},{3,1},{4,6},{5,7},{6,4},{7,5},{8,10},{9,11},{10,... | collective-permute-start | bytes 98312 | tf_op jit(solution)/shard_map/ppermute | solution.py:345
  27.3 9.2 %collective-permute-start.6 = (bf16[128,128]{1,0:T(8,128)(2,1)S(1)}, bf16[128,128]{1,0:T(8,128)(2,1)S(1)}, u32[]{:S(2)}, u32[]{:S(2)}) collective-permute-start(bf16[128,128]{1,0:T(8,128)(2,1)S(1)} %get-tuple-element.51), channel_id=1, source_target_pairs={{0,1},{1,2},{2,3},{3,0},{4,5},{5,6},{6,7},{7,4},{8,9},{9,10},{10,1... | collective-permute-start | bytes 98312 | tf_op jit(solution)/shard_map/ppermute | solution.py:345

commit v6 on v5

--- a/solution.py
+++ b/solution.py
@@ -12,7 +12,7 @@
 LANES = 128
 DP = ("y", "z", "xl")
 SPACE = ("xh", "c")
-XY_GROUP = ("y", "xl", "xh", "c")
+XY_GROUP = ("y", "xl", "xh")
 BF = jnp.bfloat16
 F32 = jnp.float32
 INTERPRET = False
@@ -216,15 +216,29 @@
     kept_ref[...] = feat_ref[me]
 
 
-def second_grad_body(im_ref, imh_ref, delta_ref, out_ref):
+def split_halves(me_ref, all_ref, keep_ref, send_ref):
+    half = keep_ref.shape[0]
+    core = me_ref[0] & 1
+    keep_ref[...] = all_ref[pl.ds(pl.multiple_of(core * half, 8), half), :]
+    send_ref[...] = all_ref[pl.ds(pl.multiple_of((1 - core) * half, 8), half), :].astype(BF)
+
+
+def second_grad_body(me_ref, im_ref, imh_ref, delta_ref, keep_ref, send_ref, all_ref):
     scale = 1.0 / 256
     delta = jnp.concatenate([delta_ref[s] for s in range(4)], 1)
-    out_ref[:576] = (dot_nt(im_ref[:576] + imh_ref[...], delta) * scale).astype(BF)
-    out_ref[576:] = (dot_nt(im_ref[576:], delta) * scale).astype(BF)
+    all_ref[:576] = dot_nt(im_ref[:576] + imh_ref[...], delta) * scale
+    all_ref[576:] = dot_nt(im_ref[576:], delta) * scale
+    split_halves(me_ref, all_ref, keep_ref, send_ref)
+
+
+def join_body(wide_ref, got_wide, packed_ref, got_packed, out_ref):
+    out_ref[:864] = (wide_ref[...] + got_wide[...].astype(F32)).astype(BF)
+    packed = packed_ref[...] + got_packed[...].astype(F32)
+    out_ref[864:] = jnp.concatenate([packed, jnp.zeros((72, LANES), F32)], 0).astype(BF)
 
 
 def back_body(
-    me_ref, im_hbm, wide_ref, delta_ref, got_ref, k_ref, table_ref, slope_ref, rimz_ref, out_ref, kodd_ref, ahead_ref, acc_ref, im_ref, sems
+    me_ref, im_hbm, delta_ref, got_ref, k_ref, table_ref, slope_ref, rimz_ref, keep_ref, send_ref, kodd_ref, ahead_ref, acc_ref, all_ref, im_ref, sems
 ):
     for s in range(4):
         pltpu.make_async_copy(im_hbm.at[s], im_ref.at[s], sems.at[s]).start()
@@ -267,21 +281,25 @@
 
     lax.fori_loop(0, 4, one, 0)
     acc = acc_ref[...] * (1.0 / 256)
-    out_ref[:1728] = wide_ref[...]
-    out_ref[2160:] = jnp.zeros((144, LANES), BF)
-    out_ref[1728:2016] = acc[288:].astype(BF)
-    out_ref[2016:2160] = jnp.concatenate([acc[:144, :64], acc[144:288, :64]], 1).astype(BF)
-
-
-def finish_body(me_ref, rows_ref, kept_ref, got_ref, got2, got3, first_ref, second_ref, feat_ref):
+    all_ref[:288] = acc[288:]
+    all_ref[288:] = jnp.concatenate([acc[:144, :64], acc[144:288, :64]], 1)
+    split_halves(me_ref, all_ref, keep_ref, send_ref)
+
+
+def finish_body(me_ref, rows_ref, other_ref, kept_ref, got_ref, got2, got3, first_ref, second_ref, feat_ref):
     me = me_ref[0]
     feat_ref[me] = kept_ref[...]
     feat_ref[(me + 1) & 3] = got_ref[128:]
     feat_ref[(me + 2) & 3] = got2[...]
     feat_ref[(me + 3) & 3] = got3[...]
-    second_ref[...] = rows_ref[:1728].astype(F32)
-    odd = rows_ref[1728:2016].astype(F32)
-    even = rows_ref[2016:2160].astype(F32)
+    mine, other = rows_ref[...].astype(F32), other_ref[...].astype(F32)
+    front = jnp.where((me & 1) == 0, mine, other)
+    back = jnp.where((me & 1) == 0, other, mine)
+    second_ref[:864] = front[:864]
+    second_ref[864:] = back[:864]
+    low, high = front[864:1080], back[864:1080]
+    odd = jnp.concatenate([low, high[:72]], 0)
+    even = high[72:216]
     first_ref[:288] = odd[:, 64:]
     first_ref[288:432] = even[:, :64]
     first_ref[432:576] = even[:, 64:]
@@ -339,6 +357,10 @@
     got = exchange(jnp.broadcast_to(rows[None], (lax.axis_size("z"),) + rows.shape), "z")
     rows = jnp.sum(got.astype(F32), 0).astype(BF)
     return gather_stage(rows, XY_GROUP)
+
+
+def across(value):
+    return lax.ppermute(value, "c", [(0, 1), (1, 0)])
 
 
 def rotated(value, steps):
@@ -406,26 +428,34 @@
     got = rotated(sent, 3)
     got2 = rotated(sent2, 2)
     got3 = rotated(sent3, 1)
-    (wide,) = call(second_grad_body, [((1728, 128), BF)])(im2, im2h, delta2)
-    (rows,) = call(
+    wide, wide_out = call(
+        second_grad_body,
+        [((864, 128), F32), ((864, 128), BF)],
+        scratch=[pltpu.VMEM((1728, 128), F32)],
+    )(me, im2, im2h, delta2)
+    packed, packed_out = call(
         back_body,
-        [((2304, 128), BF)],
+        [((216, 128), F32), ((216, 128), BF)],
         scratch=[
             pltpu.VMEM((576, 256), BF),
             pltpu.VMEM((4, 256, 128), BF),
             pltpu.VMEM((576, 128), F32),
+            pltpu.VMEM((432, 128), F32),
             pltpu.VMEM((4, 576, 1024), BF),
             pltpu.SemaphoreType.DMA((4,)),
         ],
         far=(1,),
-    )(me, im1, wide, delta2, got, k2, table2, slope1, rimz)
-    rows, got2, got3 = lax.optimization_barrier((rows, got2, got3))
+    )(me, im1, delta2, got, k2, table2, slope1, rimz)
+    packed, packed_out, got2, got3 = lax.optimization_barrier((packed, packed_out, got2, got3))
+    (rows,) = call(join_body, [((1152, 128), BF)])(
+        wide, across(wide_out), packed, across(packed_out)
+    )
     rows = sum_everywhere(rows)
     first_grad, second_grad, features = call(
         finish_body,
         [((864, 64), F32), ((1728, 128), F32), ((4, 128, 128), BF)],
         final=True,
-    )(me, rows, kept, got, got2, got3)
+    )(me, rows, across(rows), kept, got, got2, got3)
     features = features.transpose(2, 0, 1).reshape(1, 128, 16, 32)
     return (features, first_grad.reshape(27, 32, 64), second_grad.reshape(27, 64, 128))
 

time: 89.7 us -> 85.8 us (0.957)
  blocking collectives: 51.5 us -> 40.5 us
  starting transfers between devices: 14.9 us -> 19.4 us
  waiting for transfers between devices: 3.33 us -> 5.77 us
    all_to_all x3, blocking collectives: 51.5 us -> 40.5 us  [exchange(): return lax.all_to_all(chunks, axis, split_axis=0, concat_axis=0, tiled=True)]
    ppermute x0 -> x3, starting transfers between devices: none -> 4.62 us  [across(): return lax.ppermute(value, 'c', [(0, 1), (1, 0)])]
    ppermute x0 -> x3, waiting for transfers between devices: none -> 2.44 us  [across(): return lax.ppermute(value, 'c', [(0, 1), (1, 0)])]
    pallas_call x8 -> x9, Pallas kernels: 18.7 us -> 18.9 us  [run(): pl.pallas_call(body, in_specs=[scalar if arg.shape == (1,) else there if...]
  transfers between devices with their start and end apart: 7 -> 10, of which waited for: 2 -> 4; matrix products, arithmetic and copies ran while one was open for 0% -> 0% of each run, Pallas kernels for 13% -> 12%
where the time goes in v6:
time: 85.8 us; the launch traced here: 85.5 us
  blocking collectives  40.5 us (47%)
  starting transfers between devices  19.4 us (23%)
  Pallas kernels  18.9 us (22%)
  waiting for transfers between devices  5.77 us (7%)
    all_to_all x3, blocking collectives, exchange(): return lax.all_to_all(chunks, axis, split_axis=0, concat_axis=0, tiled=True)  40.5 us
    pallas_call x9, Pallas kernels, run(): pl.pallas_call(body, in_specs=[scalar if arg.shape == (1,) else there if...  18.9 us
    ppermute x6, starting transfers between devices, rotated(): return lax.ppermute(value, SPACE, [(i, (i + steps) % 4) for i in range(4)])  8.65 us
    ppermute x1, starting transfers between devices, shifted(): lax.ppermute(value, axis, [(source, source + steps) for source in range(i...  6.16 us
    ppermute x3, starting transfers between devices, across(): return lax.ppermute(value, 'c', [(0, 1), (1, 0)])  4.62 us
    ppermute x6, waiting for transfers between devices, rotated(): return lax.ppermute(value, SPACE, [(i, (i + steps) % 4) for i in range(4)])  3.33 us
    ppermute x3, waiting for transfers between devices, across(): return lax.ppermute(value, 'c', [(0, 1), (1, 0)])  2.44 us
  transfers between devices with their start and end apart: 10, of which 4 were waited for; matrix products, arithmetic and copies ran while one was open for 0% of the time, Pallas kernels for 12%

profile of v6, /device:TPU:1, one launch (start us, length us, event | category | flops | bytes accessed | tf_op | source)
XLA Modules:
  0.0 85.5 jit_solution(463184118329945879)
XLA Ops:
  0.6 4.0 %shard_map.85 = (bf16[4,512,512]{2,1,0:T(8,128)(2,1)S(1)}, bf16[4,32,512]{2,1,0:T(8,128)(2,1)}, bf16[128,576]{1,0:T(8,128)(2,1)S(1)}, bf16[64,288]{1,0:T(8,128)(2,1)S(1)}, bf16[512,512]{1,0:T(8,128)(2,1)S(1)}) custom-call(bf16[4,32,16,512]{3,2,1,0:T(8,128)(2,1)} %v_hbm.1, bf16[864,64]{1,0:T(8,128)(2,1)} %bitcast.19, ...), custom_call_target="tpu_custom_call" | custom-call | tf_op jit(solution)/shard_map/pallas_call | solution.py:325
  4.7 6.2 %collective-permute-start = (bf16[4,32,512]{2,1,0:T(8,128)(2,1)}, bf16[4,32,512]{2,1,0:T(8,128)(2,1)S(1)}, u32[]{:S(2)}, u32[]{:S(2)}) collective-permute-start(bf16[4,32,512]{2,1,0:T(8,128)(2,1)} %get-tuple-element.40), channel_id=1, source_target_pairs={{0,1},{1,2},{2,3},{4,5},{5,6},{6,7},{8,9},{9,10},{10,11},{12,13},{... | collective-permute-start | bytes 393224 | tf_op jit(solution)/shard_map/ppermute | solution.py:24
  10.9 4.4 %shard_map.86 = (bf16[4,576,1024]{2,1,0:T(8,128)(2,1)}, f32[4,64,1024]{2,1,0:T(8,128)S(1)}) custom-call(bf16[4,512,512]{2,1,0:T(8,128)(2,1)S(1)} %get-tuple-element.36.rows_ref, bf16[512,512]{1,0:T(8,128)(2,1)S(1)} %get-tuple-element.37.table_ref, bf16[128,576]{1,0:T(8,128)(2,1)S(1)} %get-tuple-element.38.wt_ref), custom_call_target="tpu_custom_call" | custom-call | tf_op jit(solution)/shard_map/pallas_call | solution.py:325
  15.3 1.4 %shard_map.87 = (bf16[4,64,1024]{2,1,0:T(8,128)(2,1)S(1)}, bf16[384,128]{1,0:T(8,128)(2,1)S(1)}, bf16[128,128]{1,0:T(8,128)(2,1)S(1)}, bf16[128,128]{1,0:T(8,128...) custom-call(s32[1]{0:T(128)} %bitcast.me_ref, ...), custom_call_target="tpu_custom_call" | custom-call | tf_op jit(solution)/shard_map/pallas_call | solution.py:325
  16.7 1.7 %collective-permute-start.1 = (bf16[384,128]{1,0:T(8,128)(2,1)S(1)}, bf16[384,128]{1,0:T(8,128)(2,1)S(1)}, u32[]{:S(2)}, u32[]{:S(2)}) collective-permute-start(bf16[384,128]{1,0:T(8,128)(2,1)S(1)} %get-tuple-element.44), channel_id=1, source_target_pairs={{0,1},{1,2},{2,3},{3,0},{4,5},{5,6},{6,7},{7,4},{8,9},{9,10},{10,1... | collective-permute-start | bytes 294920 | tf_op jit(solution)/shard_map/ppermute | solution.py:367
  18.4 0.5 collective-permute-start.3
  18.9 1.0 %shard_map.88 = (bf16[1728,512]{1,0:T(8,128)(2,1)S(1)}, f32[128,512]{1,0:T(8,128)S(1)}) custom-call(bf16[4,64,1024]{2,1,0:T(8,128)(2,1)S(1)} %get-tuple-element.42.hid_ref, bf16[512,512]{1,0:T(8,128)(2,1)S(1)} %copy-done, bf16[1728,128]{1,0:T(8,128)(2,1)S(1)} %bitcast.13), custom_call_target="tpu_custom_call" | custom-call | tf_op jit(solution)/shard_map/pallas_call | solution.py:325
  19.9 2.7 %collective-permute-done.2.got2 = bf16[128,128]{1,0:T(8,128)(2,1)S(1)} collective-permute-done((bf16[128,128]{1,0:T(8,128)(2,1)S(1)}, bf16[128,128]{1,0:T(8,128)(2,1)S(1)}, u32[]{:S(2)}, u32[]{:S(2)}) %collective-permute-start.2) | collective-permute-done | bytes 32800 | tf_op jit(solution)/shard_map/ppermute | solution.py:367
  22.7 0.6 collective-permute-done.3.got3
  23.3 0.9 %shard_map.89 = (bf16[256,128]{1,0:T(8,128)(2,1)S(1)}, bf16[128,128]{1,0:T(8,128)(2,1)S(1)}, bf16[128,128]{1,0:T(8,128)(2,1)S(1)}, bf16[128,128]{1,0:T(8,128)(2,...) custom-call(s32[1]{0:T(128)} %bitcast.me_ref, ...), custom_call_target="tpu_custom_call" | custom-call | tf_op jit(solution)/shard_map/pallas_call | solution.py:325
  24.2 0.7 shard_map.90
  24.9 0.2 collective-permute-start.4
  25.1 0.4 collective-permute-start.5
  25.5 3.0 %collective-permute-start.6 = (bf16[128,128]{1,0:T(8,128)(2,1)S(1)}, bf16[128,128]{1,0:T(8,128)(2,1)S(1)}, u32[]{:S(2)}, u32[]{:S(2)}) collective-permute-start(bf16[128,128]{1,0:T(8,128)(2,1)S(1)} %get-tuple-element.59), channel_id=1, source_target_pairs={{0,2},{1,3},{2,0},{3,1},{4,6},{5,7},{6,4},{7,5},{8,10},{9,11},{10,... | collective-permute-start | bytes 98312 | tf_op jit(solution)/shard_map/ppermute | solution.py:367
  28.5 3.1 %collective-permute-start.7 = (bf16[128,128]{1,0:T(8,128)(2,1)S(1)}, bf16[128,128]{1,0:T(8,128)(2,1)S(1)}, u32[]{:S(2)}, u32[]{:S(2)}) collective-permute-start(bf16[128,128]{1,0:T(8,128)(2,1)S(1)} %get-tuple-element.60), channel_id=1, source_target_pairs={{0,1},{1,2},{2,3},{3,0},{4,5},{5,6},{6,7},{7,4},{8,9},{9,10},{10,1... | collective-permute-start | bytes 98312 | tf_op jit(solution)/shard_map/ppermute | solution.py:367
  31.6 5.1 %shard_map.91 = (f32[216,128]{1,0:T(8,128)S(1)}, bf16[216,128]{1,0:T(8,128)(2,1)S(1)}) custom-call(s32[1]{0:T(128)} %bitcast.me_ref, bf16[4,576,1024]{2,1,0:T(8,128)(2,1)} %get-tuple-element.53.im_hbm, bf16[4,128,128]{2,1,0:T(8,128)(2,1)S(1)} %get-tuple-element.50.delta_ref, bf16[256,128]{1,0:T(8,128)(2,1)S(1)} %collective-permute-done.5.got_ref, ...), custom_call_target="tpu_custom_call" | custom-call | tf_op jit(solution)/shard_map/pallas_call | solution.py:325
  36.8 0.1 collective-permute-start.8
  36.9 1.2 %collective-permute-done.8.got_packed = bf16[216,128]{1,0:T(8,128)(2,1)S(1)} collective-permute-done((bf16[216,128]{1,0:T(8,128)(2,1)S(1)}, bf16[216,128]{1,0:T(8,128)(2,1)S(1)}, u32[]{:S(2)}, u32[]{:S(2)}) %collective-permute-start.8) | collective-permute-done | bytes 55328 | tf_op jit(solution)/shard_map/ppermute | solution.py:363
  38.1 13.2 %all_to_all.15 = bf16[16,72,128]{2,1,0:T(8,128)(2,1)S(1)} all-to-all(bf16[16,72,128]{2,1,0:T(8,128)(2,1)S(1)} %bitcast.18), channel_id=1, replica_groups=mesh['y'=4,'z'=8,'xl'=2,'xh'=2,'c'=2] {'y','xl','xh'}, dimensions={0} | all-to-all | bytes 589824 | tf_op jit(solution)/shard_map/all_to_all | solution.py:342
  51.5 16.2 %all_to_all.16 = bf16[8,72,128]{2,1,0:T(8,128)(2,1)S(1)} all-to-all(bf16[8,72,128]{2,1,0:T(8,128)(2,1)S(1)} %broadcast_in_dim.4), channel_id=1, replica_groups=mesh['y'=4,'z'=8,'xl'=2,'xh'=2,'c'=2] {'z'}, dimensions={0} | all-to-all | bytes 294912 | tf_op jit(solution)/shard_map/all_to_all | solution.py:342
  67.7 11.0 %all_to_all.17 = bf16[16,72,128]{2,1,0:T(8,128)(2,1)S(1)} all-to-all(bf16[16,72,128]{2,1,0:T(8,128)(2,1)S(1)} %broadcast_in_dim.5), channel_id=1, replica_groups=mesh['y'=4,'z'=8,'xl'=2,'xh'=2,'c'=2] {'y','xl','xh'}, dimensions={0} | all-to-all | bytes 589824 | tf_op jit(solution)/shard_map/all_to_all | solution.py:342
  78.8 4.3 %collective-permute-start.9 = (bf16[1152,128]{1,0:T(8,128)(2,1)S(1)}, bf16[1152,128]{1,0:T(8,128)(2,1)S(1)}, u32[]{:S(2)}, u32[]{:S(2)}) collective-permute-start(bf16[1152,128]{1,0:T(8,128)(2,1)S(1)} %bitcast.16), channel_id=1, source_target_pairs={{0,1},{1,0},{2,3},{3,2},{4,5},{5,4},{6,7},{7,6},{8,9},{9,8},{10,11... | collective-permute-start | bytes 884744 | tf_op jit(solution)/shard_map/ppermute | solution.py:363
  83.1 1.2 %collective-permute-done.9.other_ref = bf16[1152,128]{1,0:T(8,128)(2,1)S(1)} collective-permute-done((bf16[1152,128]{1,0:T(8,128)(2,1)S(1)}, bf16[1152,128]{1,0:T(8,128)(2,1)S(1)}, u32[]{:S(2)}, u32[]{:S(2)}) %collective-permute-start.9) | collective-permute-done | bytes 294944 | tf_op jit(solution)/shard_map/ppermute | solution.py:363
  84.3 1.2 %shard_map.93 = (f32[864,64]{1,0:T(8,128)}, f32[1728,128]{1,0:T(8,128)}, bf16[4,128,128]{2,1,0:T(8,128)(2,1)}) custom-call(s32[1]{0:T(128)} %bitcast.me_ref, bf16[1152,128]{1,0:T(8,128)(2,1)S(1)} %bitcast.17, bf16[1152,128]{1,0:T(8,128)(2,1)S(1)} %collective-permute-done.9.other_ref, bf16[128,128]{1,0:T(8,128)(2,1)S(1)} %get-tuple-element.63.kept_ref, ...), custom_call_target="tpu_custom_call" | custom-call | tf_op jit(solution)/shard_map/pallas_call | solution.py:325
  (18 shorter events, 0.2 us)
Async XLA Ops:
  4.7 10.7 %copy-start.2 = (bf16[512,512]{1,0:T(8,128)(2,1)S(1)}, bf16[512,512]{1,0:T(8,128)(2,1)}, u32[]{:S(2)}) copy-start(bf16[512,512]{1,0:T(8,128)(2,1)} %constant.16.clone.table_hbm.table_ref) | copy-start | bytes 1572868
  4.7 10.6 %collective-permute-start = (bf16[4,32,512]{2,1,0:T(8,128)(2,1)}, bf16[4,32,512]{2,1,0:T(8,128)(2,1)S(1)}, u32[]{:S(2)}, u32[]{:S(2)}) collective-permute-start(bf16[4,32,512]{2,1,0:T(8,128)(2,1)} %get-tuple-element.40), channel_id=1, source_target_pairs={{0,1},{1,2},{2,3},{4,5},{5,6},{6,7},{8,9},{9,10},{10,11},{12,13},{... | collective-permute-start | bytes 393224 | tf_op jit(solution)/shard_map/ppermute | solution.py:24
  10.9 8.1 %copy-start = (bf16[512,512]{1,0:T(8,128)(2,1)S(1)}, bf16[512,512]{1,0:T(8,128)(2,1)}, u32[]{:S(2)}) copy-start(bf16[512,512]{1,0:T(8,128)(2,1)} %constant.17.clone.table_ref) | copy-start | bytes 1572868
  10.9 8.1 %copy-start.1 = (bf16[27,64,128]{2,1,0:T(8,128)(2,1)S(1)}, bf16[27,64,128]{2,1,0:T(8,128)(2,1)}, u32[]{:S(2)}) copy-start(bf16[27,64,128]{2,1,0:T(8,128)(2,1)} %param.8) | copy-start | bytes 1327108
  16.7 6.5 %collective-permute-start.1 = (bf16[384,128]{1,0:T(8,128)(2,1)S(1)}, bf16[384,128]{1,0:T(8,128)(2,1)S(1)}, u32[]{:S(2)}, u32[]{:S(2)}) collective-permute-start(bf16[384,128]{1,0:T(8,128)(2,1)S(1)} %get-tuple-element.44), channel_id=1, source_target_pairs={{0,1},{1,2},{2,3},{3,0},{4,5},{5,6},{6,7},{7,4},{8,9},{9,10},{10,1... | collective-permute-start | bytes 294920 | tf_op jit(solution)/shard_map/ppermute | solution.py:367
  18.4 4.3 %collective-permute-start.2 = (bf16[128,128]{1,0:T(8,128)(2,1)S(1)}, bf16[128,128]{1,0:T(8,128)(2,1)S(1)}, u32[]{:S(2)}, u32[]{:S(2)}) collective-permute-start(bf16[128,128]{1,0:T(8,128)(2,1)S(1)} %get-tuple-element.47), channel_id=1, source_target_pairs={{0,2},{1,3},{2,0},{3,1},{4,6},{5,7},{6,4},{7,5},{8,10},{9,11},{10,... | collective-permute-start | bytes 98312 | tf_op jit(solution)/shard_map/ppermute | solution.py:367
  18.4 4.8 %collective-permute-start.3 = (bf16[128,128]{1,0:T(8,128)(2,1)S(1)}, bf16[128,128]{1,0:T(8,128)(2,1)S(1)}, u32[]{:S(2)}, u32[]{:S(2)}) collective-permute-start(bf16[128,128]{1,0:T(8,128)(2,1)S(1)} %get-tuple-element.48), channel_id=1, source_target_pairs={{0,3},{1,0},{2,1},{3,2},{4,7},{5,4},{6,5},{7,6},{8,11},{9,8},{10,9... | collective-permute-start | bytes 98312 | tf_op jit(solution)/shard_map/ppermute | solution.py:367
  24.9 13.2 %collective-permute-start.4 = (bf16[864,128]{1,0:T(8,128)(2,1)S(1)}, bf16[864,128]{1,0:T(8,128)(2,1)S(1)}, u32[]{:S(2)}, u32[]{:S(2)}) collective-permute-start(bf16[864,128]{1,0:T(8,128)(2,1)S(1)} %get-tuple-element.52), channel_id=1, source_target_pairs={{0,1},{1,0},{2,3},{3,2},{4,5},{5,4},{6,7},{7,6},{8,9},{9,8},{10,11... | collective-permute-start | bytes 663560 | tf_op jit(solution)/shard_map/ppermute | solution.py:363
  25.1 6.5 %collective-permute-start.5 = (bf16[256,128]{1,0:T(8,128)(2,1)S(1)}, bf16[256,128]{1,0:T(8,128)(2,1)S(1)}, u32[]{:S(2)}, u32[]{:S(2)}) collective-permute-start(bf16[256,128]{1,0:T(8,128)(2,1)S(1)} %get-tuple-element.54), channel_id=1, source_target_pairs={{0,3},{1,0},{2,1},{3,2},{4,7},{5,4},{6,5},{7,6},{8,11},{9,8},{10,9... | collective-permute-start | bytes 196616 | tf_op jit(solution)/shard_map/ppermute | solution.py:367
  25.5 11.2 %collective-permute-start.6 = (bf16[128,128]{1,0:T(8,128)(2,1)S(1)}, bf16[128,128]{1,0:T(8,128)(2,1)S(1)}, u32[]{:S(2)}, u32[]{:S(2)}) collective-permute-start(bf16[128,128]{1,0:T(8,128)(2,1)S(1)} %get-tuple-element.59), channel_id=1, source_target_pairs={{0,2},{1,3},{2,0},{3,1},{4,6},{5,7},{6,4},{7,5},{8,10},{9,11},{10,... | collective-permute-start | bytes 98312 | tf_op jit(solution)/shard_map/ppermute | solution.py:367
  28.5 8.3 %collective-permute-start.7 = (bf16[128,128]{1,0:T(8,128)(2,1)S(1)}, bf16[128,128]{1,0:T(8,128)(2,1)S(1)}, u32[]{:S(2)}, u32[]{:S(2)}) collective-permute-start(bf16[128,128]{1,0:T(8,128)(2,1)S(1)} %get-tuple-element.60), channel_id=1, source_target_pairs={{0,1},{1,2},{2,3},{3,0},{4,5},{5,6},{6,7},{7,4},{8,9},{9,10},{10,1... | collective-permute-start | bytes 98312 | tf_op jit(solution)/shard_map/ppermute | solution.py:367
  36.8 1.3 %collective-permute-start.8 = (bf16[216,128]{1,0:T(8,128)(2,1)S(1)}, bf16[216,128]{1,0:T(8,128)(2,1)S(1)}, u32[]{:S(2)}, u32[]{:S(2)}) collective-permute-start(bf16[216,128]{1,0:T(8,128)(2,1)S(1)} %get-tuple-element.62), channel_id=1, source_target_pairs={{0,1},{1,0},{2,3},{3,2},{4,5},{5,4},{6,7},{7,6},{8,9},{9,8},{10,11... | collective-permute-start | bytes 165896 | tf_op jit(solution)/shard_map/ppermute | solution.py:363
  78.8 5.5 %collective-permute-start.9 = (bf16[1152,128]{1,0:T(8,128)(2,1)S(1)}, bf16[1152,128]{1,0:T(8,128)(2,1)S(1)}, u32[]{:S(2)}, u32[]{:S(2)}) collective-permute-start(bf16[1152,128]{1,0:T(8,128)(2,1)S(1)} %bitcast.16), channel_id=1, source_target_pairs={{0,1},{1,0},{2,3},{3,2},{4,5},{5,4},{6,7},{7,6},{8,9},{9,8},{10,11... | collective-permute-start | bytes 884744 | tf_op jit(solution)/shard_map/ppermute | solution.py:363

commit v7 on v6

--- a/solution.py
+++ b/solution.py
@@ -354,8 +354,14 @@
 
 def sum_everywhere(rows):
     rows = reduce_stage(rows, XY_GROUP)
-    got = exchange(jnp.broadcast_to(rows[None], (lax.axis_size("z"),) + rows.shape), "z")
-    rows = jnp.sum(got.astype(F32), 0).astype(BF)
+    rows = rows.astype(F32)
+    count = lax.axis_size("z")
+    steps = [[place ^ step for place in range(count)] for step in (1, 2) if 2 * step < count]
+    for peers in steps + [[count - 1 - place for place in range(count)]] * (count > 1):
+        sent = rows if peers in steps else rows.astype(BF)
+        got = lax.ppermute(sent, "z", list(enumerate(peers)))
+        rows = sent.astype(F32) + got.astype(F32)
+    rows = rows.astype(BF)
     return gather_stage(rows, XY_GROUP)
 
 

time: 85.8 us -> 84.8 us (0.988)
  blocking collectives: 40.5 us -> 24.3 us
  starting transfers between devices: 19.4 us -> 30.8 us
  waiting for transfers between devices: 5.77 us -> 9.61 us
    all_to_all x3 -> x2, blocking collectives: 40.5 us -> 24.3 us  [exchange(): return lax.all_to_all(chunks, axis, split_axis=0, concat_axis=0, tiled=True)]
    ppermute x0 -> x3, starting transfers between devices: none -> 9.57 us  [sum_everywhere(): got = lax.ppermute(sent, 'z', list(enumerate(peers)))]
    ppermute x0 -> x3, waiting for transfers between devices: none -> 3.85 us  [sum_everywhere(): got = lax.ppermute(sent, 'z', list(enumerate(peers)))]
    ppermute x3, starting transfers between devices: 4.62 us -> 6.38 us  [across(): return lax.ppermute(value, 'c', [(0, 1), (1, 0)])]
  transfers between devices with their start and end apart: 10 -> 13, of which waited for: 4 -> 7; matrix products, arithmetic and copies ran while one was open for 0% -> 0% of each run, Pallas kernels for 12% -> 13%
where the time goes in v7:
time: 84.8 us; the launch traced here: 84.6 us
  starting transfers between devices  30.8 us (36%)
  blocking collectives  24.3 us (29%)
  Pallas kernels  18.9 us (22%)
  waiting for transfers between devices  9.61 us (11%)
    all_to_all x2, blocking collectives, exchange(): return lax.all_to_all(chunks, axis, split_axis=0, concat_axis=0, tiled=True)  24.3 us
    pallas_call x9, Pallas kernels, run(): pl.pallas_call(body, in_specs=[scalar if arg.shape == (1,) else there if...  18.9 us
    ppermute x3, starting transfers between devices, sum_everywhere(): got = lax.ppermute(sent, 'z', list(enumerate(peers)))  9.57 us
    ppermute x6, starting transfers between devices, rotated(): return lax.ppermute(value, SPACE, [(i, (i + steps) % 4) for i in range(4)])  8.65 us
    ppermute x3, starting transfers between devices, across(): return lax.ppermute(value, 'c', [(0, 1), (1, 0)])  6.38 us
    ppermute x1, starting transfers between devices, shifted(): lax.ppermute(value, axis, [(source, source + steps) for source in range(i...  6.16 us
    ppermute x3, waiting for transfers between devices, sum_everywhere(): got = lax.ppermute(sent, 'z', list(enumerate(peers)))  3.85 us
    ppermute x6, waiting for transfers between devices, rotated(): return lax.ppermute(value, SPACE, [(i, (i + steps) % 4) for i in range(4)])  3.33 us
  transfers between devices with their start and end apart: 13, of which 7 were waited for; matrix products, arithmetic and copies ran while one was open for 0% of the time, Pallas kernels for 13%

profile of v7, /device:TPU:1, one launch (start us, length us, event | category | flops | bytes accessed | tf_op | source)
XLA Modules:
  0.0 84.6 jit_solution(11273919576661288788)
XLA Ops:
  0.6 4.0 %shard_map.85 = (bf16[4,512,512]{2,1,0:T(8,128)(2,1)S(1)}, bf16[4,32,512]{2,1,0:T(8,128)(2,1)}, bf16[128,576]{1,0:T(8,128)(2,1)S(1)}, bf16[64,288]{1,0:T(8,128)(2,1)S(1)}, bf16[512,512]{1,0:T(8,128)(2,1)S(1)}) custom-call(bf16[4,32,16,512]{3,2,1,0:T(8,128)(2,1)} %v_hbm.1, bf16[864,64]{1,0:T(8,128)(2,1)} %bitcast.19, ...), custom_call_target="tpu_custom_call" | custom-call | tf_op jit(solution)/shard_map/pallas_call | solution.py:325
  4.7 6.2 %collective-permute-start = (bf16[4,32,512]{2,1,0:T(8,128)(2,1)}, bf16[4,32,512]{2,1,0:T(8,128)(2,1)S(1)}, u32[]{:S(2)}, u32[]{:S(2)}) collective-permute-start(bf16[4,32,512]{2,1,0:T(8,128)(2,1)} %get-tuple-element.40), channel_id=1, source_target_pairs={{0,1},{1,2},{2,3},{4,5},{5,6},{6,7},{8,9},{9,10},{10,11},{12,13},{... | collective-permute-start | bytes 393224 | tf_op jit(solution)/shard_map/ppermute | solution.py:24
  10.9 4.4 %shard_map.86 = (bf16[4,576,1024]{2,1,0:T(8,128)(2,1)}, f32[4,64,1024]{2,1,0:T(8,128)S(1)}) custom-call(bf16[4,512,512]{2,1,0:T(8,128)(2,1)S(1)} %get-tuple-element.36.rows_ref, bf16[512,512]{1,0:T(8,128)(2,1)S(1)} %get-tuple-element.37.table_ref, bf16[128,576]{1,0:T(8,128)(2,1)S(1)} %get-tuple-element.38.wt_ref), custom_call_target="tpu_custom_call" | custom-call | tf_op jit(solution)/shard_map/pallas_call | solution.py:325
  15.3 1.4 %shard_map.87 = (bf16[4,64,1024]{2,1,0:T(8,128)(2,1)S(1)}, bf16[384,128]{1,0:T(8,128)(2,1)S(1)}, bf16[128,128]{1,0:T(8,128)(2,1)S(1)}, bf16[128,128]{1,0:T(8,128...) custom-call(s32[1]{0:T(128)} %bitcast.me_ref, ...), custom_call_target="tpu_custom_call" | custom-call | tf_op jit(solution)/shard_map/pallas_call | solution.py:325
  16.7 1.7 %collective-permute-start.1 = (bf16[384,128]{1,0:T(8,128)(2,1)S(1)}, bf16[384,128]{1,0:T(8,128)(2,1)S(1)}, u32[]{:S(2)}, u32[]{:S(2)}) collective-permute-start(bf16[384,128]{1,0:T(8,128)(2,1)S(1)} %get-tuple-element.44), channel_id=1, source_target_pairs={{0,1},{1,2},{2,3},{3,0},{4,5},{5,6},{6,7},{7,4},{8,9},{9,10},{10,1... | collective-permute-start | bytes 294920 | tf_op jit(solution)/shard_map/ppermute | solution.py:373
  18.9 1.0 %shard_map.88 = (bf16[1728,512]{1,0:T(8,128)(2,1)S(1)}, f32[128,512]{1,0:T(8,128)S(1)}) custom-call(bf16[4,64,1024]{2,1,0:T(8,128)(2,1)S(1)} %get-tuple-element.42.hid_ref, bf16[512,512]{1,0:T(8,128)(2,1)S(1)} %copy-done, bf16[1728,128]{1,0:T(8,128)(2,1)S(1)} %bitcast.13), custom_call_target="tpu_custom_call" | custom-call | tf_op jit(solution)/shard_map/pallas_call | solution.py:325
  19.9 2.7 %collective-permute-done.2.got2 = bf16[128,128]{1,0:T(8,128)(2,1)S(1)} collective-permute-done((bf16[128,128]{1,0:T(8,128)(2,1)S(1)}, bf16[128,128]{1,0:T(8,128)(2,1)S(1)}, u32[]{:S(2)}, u32[]{:S(2)}) %collective-permute-start.2) | collective-permute-done | bytes 32800 | tf_op jit(solution)/shard_map/ppermute | solution.py:373
  23.3 0.9 %shard_map.89 = (bf16[256,128]{1,0:T(8,128)(2,1)S(1)}, bf16[128,128]{1,0:T(8,128)(2,1)S(1)}, bf16[128,128]{1,0:T(8,128)(2,1)S(1)}, bf16[128,128]{1,0:T(8,128)(2,...) custom-call(s32[1]{0:T(128)} %bitcast.me_ref, ...), custom_call_target="tpu_custom_call" | custom-call | tf_op jit(solution)/shard_map/pallas_call | solution.py:325
  24.2 0.7 shard_map.90
  25.5 3.0 %collective-permute-start.6 = (bf16[128,128]{1,0:T(8,128)(2,1)S(1)}, bf16[128,128]{1,0:T(8,128)(2,1)S(1)}, u32[]{:S(2)}, u32[]{:S(2)}) collective-permute-start(bf16[128,128]{1,0:T(8,128)(2,1)S(1)} %get-tuple-element.59), channel_id=1, source_target_pairs={{0,2},{1,3},{2,0},{3,1},{4,6},{5,7},{6,4},{7,5},{8,10},{9,11},{10,... | collective-permute-start | bytes 98312 | tf_op jit(solution)/shard_map/ppermute | solution.py:373
  28.5 3.1 %collective-permute-start.7 = (bf16[128,128]{1,0:T(8,128)(2,1)S(1)}, bf16[128,128]{1,0:T(8,128)(2,1)S(1)}, u32[]{:S(2)}, u32[]{:S(2)}) collective-permute-start(bf16[128,128]{1,0:T(8,128)(2,1)S(1)} %get-tuple-element.60), channel_id=1, source_target_pairs={{0,1},{1,2},{2,3},{3,0},{4,5},{5,6},{6,7},{7,4},{8,9},{9,10},{10,1... | collective-permute-start | bytes 98312 | tf_op jit(solution)/shard_map/ppermute | solution.py:373
  31.6 5.1 %shard_map.91 = (f32[216,128]{1,0:T(8,128)S(1)}, bf16[216,128]{1,0:T(8,128)(2,1)S(1)}) custom-call(s32[1]{0:T(128)} %bitcast.me_ref, bf16[4,576,1024]{2,1,0:T(8,128)(2,1)} %get-tuple-element.53.im_hbm, bf16[4,128,128]{2,1,0:T(8,128)(2,1)S(1)} %get-tuple-element.50.delta_ref, bf16[256,128]{1,0:T(8,128)(2,1)S(1)} %collective-permute-done.5.got_ref, ...), custom_call_target="tpu_custom_call" | custom-call | tf_op jit(solution)/shard_map/pallas_call | solution.py:325
  36.9 1.2 %collective-permute-done.8.got_packed = bf16[216,128]{1,0:T(8,128)(2,1)S(1)} collective-permute-done((bf16[216,128]{1,0:T(8,128)(2,1)S(1)}, bf16[216,128]{1,0:T(8,128)(2,1)S(1)}, u32[]{:S(2)}, u32[]{:S(2)}) %collective-permute-start.8) | collective-permute-done | bytes 55328 | tf_op jit(solution)/shard_map/ppermute | solution.py:369
  38.1 13.2 %all_to_all.10 = bf16[16,72,128]{2,1,0:T(8,128)(2,1)S(1)} all-to-all(bf16[16,72,128]{2,1,0:T(8,128)(2,1)S(1)} %bitcast.18), channel_id=1, replica_groups=mesh['y'=4,'z'=8,'xl'=2,'xh'=2,'c'=2] {'y','xl','xh'}, dimensions={0} | all-to-all | bytes 589824 | tf_op jit(solution)/shard_map/all_to_all | solution.py:342
  51.5 1.7 %collective-permute-start.9 = (f32[72,128]{1,0:T(8,128)S(1)}, f32[72,128]{1,0:T(8,128)S(1)}, u32[]{:S(2)}, u32[]{:S(2)}) collective-permute-start(f32[72,128]{1,0:T(8,128)S(1)} %convert_element_type.17), channel_id=1, source_target_pairs={{0,8},{8,0},{16,24},{24,16},{32,40},{40,32},{48,56},{56,48},{1,9},... | collective-permute-start | bytes 110600 | tf_op jit(solution)/shard_map/ppermute | solution.py:362
  53.2 1.3 %collective-permute-done.9 = f32[72,128]{1,0:T(8,128)S(1)} collective-permute-done((f32[72,128]{1,0:T(8,128)S(1)}, f32[72,128]{1,0:T(8,128)S(1)}, u32[]{:S(2)}, u32[]{:S(2)}) %collective-permute-start.9) | collective-permute-done | bytes 36896 | tf_op jit(solution)/shard_map/ppermute | solution.py:362
  54.5 3.0 %collective-permute-start.10 = (f32[72,128]{1,0:T(8,128)S(1)}, f32[72,128]{1,0:T(8,128)S(1)}, u32[]{:S(2)}, u32[]{:S(2)}) collective-permute-start(f32[72,128]{1,0:T(8,128)S(1)} %convert_add_fusion), channel_id=1, source_target_pairs={{0,16},{8,24},{16,0},{24,8},{32,48},{40,56},{48,32},{56,40},{1,17}... | collective-permute-start | bytes 110600 | tf_op jit(solution)/shard_map/ppermute | solution.py:362
  57.5 1.3 %collective-permute-done.10 = f32[72,128]{1,0:T(8,128)S(1)} collective-permute-done((f32[72,128]{1,0:T(8,128)S(1)}, f32[72,128]{1,0:T(8,128)S(1)}, u32[]{:S(2)}, u32[]{:S(2)}) %collective-permute-start.10) | collective-permute-done | bytes 36896 | tf_op jit(solution)/shard_map/ppermute | solution.py:362
  58.9 4.9 %collective-permute-start.11 = (bf16[72,128]{1,0:T(8,128)(2,1)S(1)}, bf16[72,128]{1,0:T(8,128)(2,1)S(1)}, u32[]{:S(2)}, u32[]{:S(2)}) collective-permute-start(bf16[72,128]{1,0:T(8,128)(2,1)S(1)} %add_convert_fusion.1), channel_id=1, source_target_pairs={{0,56},{8,48},{16,40},{24,32},{32,24},{40,16},{48,8},{56,0},{1,57}... | collective-permute-start | bytes 55304 | tf_op jit(solution)/shard_map/ppermute | solution.py:362
  63.7 1.2 %collective-permute-done.11 = bf16[72,128]{1,0:T(8,128)(2,1)S(1)} collective-permute-done((bf16[72,128]{1,0:T(8,128)(2,1)S(1)}, bf16[72,128]{1,0:T(8,128)(2,1)S(1)}, u32[]{:S(2)}, u32[]{:S(2)}) %collective-permute-start.11) | collective-permute-done | bytes 18464 | tf_op jit(solution)/shard_map/ppermute | solution.py:362
  65.0 11.1 %all_to_all.11 = bf16[16,72,128]{2,1,0:T(8,128)(2,1)S(1)} all-to-all(bf16[16,72,128]{2,1,0:T(8,128)(2,1)S(1)} %broadcast_in_dim.2), channel_id=1, replica_groups=mesh['y'=4,'z'=8,'xl'=2,'xh'=2,'c'=2] {'y','xl','xh'}, dimensions={0} | all-to-all | bytes 589824 | tf_op jit(solution)/shard_map/all_to_all | solution.py:342
  76.1 6.1 %collective-permute-start.12 = (bf16[1152,128]{1,0:T(8,128)(2,1)S(1)}, bf16[1152,128]{1,0:T(8,128)(2,1)S(1)}, u32[]{:S(2)}, u32[]{:S(2)}) collective-permute-start(bf16[1152,128]{1,0:T(8,128)(2,1)S(1)} %bitcast.16), channel_id=1, source_target_pairs={{0,1},{1,0},{2,3},{3,2},{4,5},{5,4},{6,7},{7,6},{8,9},{9,8},{10,11... | collective-permute-start | bytes 884744 | tf_op jit(solution)/shard_map/ppermute | solution.py:369
  82.1 1.2 %collective-permute-done.12.other_ref = bf16[1152,128]{1,0:T(8,128)(2,1)S(1)} collective-permute-done((bf16[1152,128]{1,0:T(8,128)(2,1)S(1)}, bf16[1152,128]{1,0:T(8,128)(2,1)S(1)}, u32[]{:S(2)}, u32[]{:S(2)}) %collective-permute-start.12) | collective-permute-done | bytes 294944 | tf_op jit(solution)/shard_map/ppermute | solution.py:369
  83.4 1.2 %shard_map.93 = (f32[864,64]{1,0:T(8,128)}, f32[1728,128]{1,0:T(8,128)}, bf16[4,128,128]{2,1,0:T(8,128)(2,1)}) custom-call(s32[1]{0:T(128)} %bitcast.me_ref, bf16[1152,128]{1,0:T(8,128)(2,1)S(1)} %bitcast.17, bf16[1152,128]{1,0:T(8,128)(2,1)S(1)} %collective-permute-done.12.other_ref, bf16[128,128]{1,0:T(8,128)(2,1)S(1)} %get-tuple-element.63.kept_ref, ...), custom_call_target="tpu_custom_call" | custom-call | tf_op jit(solution)/shard_map/pallas_call | solution.py:325
  (25 shorter events, 2.0 us)
Async XLA Ops:
  4.7 10.7 %copy-start.2 = (bf16[512,512]{1,0:T(8,128)(2,1)S(1)}, bf16[512,512]{1,0:T(8,128)(2,1)}, u32[]{:S(2)}) copy-start(bf16[512,512]{1,0:T(8,128)(2,1)} %constant.15.clone.table_hbm.table_ref) | copy-start | bytes 1572868
  4.7 10.6 %collective-permute-start = (bf16[4,32,512]{2,1,0:T(8,128)(2,1)}, bf16[4,32,512]{2,1,0:T(8,128)(2,1)S(1)}, u32[]{:S(2)}, u32[]{:S(2)}) collective-permute-start(bf16[4,32,512]{2,1,0:T(8,128)(2,1)} %get-tuple-element.40), channel_id=1, source_target_pairs={{0,1},{1,2},{2,3},{4,5},{5,6},{6,7},{8,9},{9,10},{10,11},{12,13},{... | collective-permute-start | bytes 393224 | tf_op jit(solution)/shard_map/ppermute | solution.py:24
  10.9 8.1 %copy-start = (bf16[512,512]{1,0:T(8,128)(2,1)S(1)}, bf16[512,512]{1,0:T(8,128)(2,1)}, u32[]{:S(2)}) copy-start(bf16[512,512]{1,0:T(8,128)(2,1)} %constant.16.clone.table_ref) | copy-start | bytes 1572868
  10.9 8.1 %copy-start.1 = (bf16[27,64,128]{2,1,0:T(8,128)(2,1)S(1)}, bf16[27,64,128]{2,1,0:T(8,128)(2,1)}, u32[]{:S(2)}) copy-start(bf16[27,64,128]{2,1,0:T(8,128)(2,1)} %param.8) | copy-start | bytes 1327108
  16.7 6.5 %collective-permute-start.1 = (bf16[384,128]{1,0:T(8,128)(2,1)S(1)}, bf16[384,128]{1,0:T(8,128)(2,1)S(1)}, u32[]{:S(2)}, u32[]{:S(2)}) collective-permute-start(bf16[384,128]{1,0:T(8,128)(2,1)S(1)} %get-tuple-element.44), channel_id=1, source_target_pairs={{0,1},{1,2},{2,3},{3,0},{4,5},{5,6},{6,7},{7,4},{8,9},{9,10},{10,1... | collective-permute-start | bytes 294920 | tf_op jit(solution)/shard_map/ppermute | solution.py:373
  18.4 4.3 %collective-permute-start.2 = (bf16[128,128]{1,0:T(8,128)(2,1)S(1)}, bf16[128,128]{1,0:T(8,128)(2,1)S(1)}, u32[]{:S(2)}, u32[]{:S(2)}) collective-permute-start(bf16[128,128]{1,0:T(8,128)(2,1)S(1)} %get-tuple-element.47), channel_id=1, source_target_pairs={{0,2},{1,3},{2,0},{3,1},{4,6},{5,7},{6,4},{7,5},{8,10},{9,11},{10,... | collective-permute-start | bytes 98312 | tf_op jit(solution)/shard_map/ppermute | solution.py:373
  18.4 4.8 %collective-permute-start.3 = (bf16[128,128]{1,0:T(8,128)(2,1)S(1)}, bf16[128,128]{1,0:T(8,128)(2,1)S(1)}, u32[]{:S(2)}, u32[]{:S(2)}) collective-permute-start(bf16[128,128]{1,0:T(8,128)(2,1)S(1)} %get-tuple-element.48), channel_id=1, source_target_pairs={{0,3},{1,0},{2,1},{3,2},{4,7},{5,4},{6,5},{7,6},{8,11},{9,8},{10,9... | collective-permute-start | bytes 98312 | tf_op jit(solution)/shard_map/ppermute | solution.py:373
  24.9 13.2 %collective-permute-start.4 = (bf16[864,128]{1,0:T(8,128)(2,1)S(1)}, bf16[864,128]{1,0:T(8,128)(2,1)S(1)}, u32[]{:S(2)}, u32[]{:S(2)}) collective-permute-start(bf16[864,128]{1,0:T(8,128)(2,1)S(1)} %get-tuple-element.52), channel_id=1, source_target_pairs={{0,1},{1,0},{2,3},{3,2},{4,5},{5,4},{6,7},{7,6},{8,9},{9,8},{10,11... | collective-permute-start | bytes 663560 | tf_op jit(solution)/shard_map/ppermute | solution.py:369
  25.1 6.5 %collective-permute-start.5 = (bf16[256,128]{1,0:T(8,128)(2,1)S(1)}, bf16[256,128]{1,0:T(8,128)(2,1)S(1)}, u32[]{:S(2)}, u32[]{:S(2)}) collective-permute-start(bf16[256,128]{1,0:T(8,128)(2,1)S(1)} %get-tuple-element.54), channel_id=1, source_target_pairs={{0,3},{1,0},{2,1},{3,2},{4,7},{5,4},{6,5},{7,6},{8,11},{9,8},{10,9... | collective-permute-start | bytes 196616 | tf_op jit(solution)/shard_map/ppermute | solution.py:373
  25.5 11.2 %collective-permute-start.6 = (bf16[128,128]{1,0:T(8,128)(2,1)S(1)}, bf16[128,128]{1,0:T(8,128)(2,1)S(1)}, u32[]{:S(2)}, u32[]{:S(2)}) collective-permute-start(bf16[128,128]{1,0:T(8,128)(2,1)S(1)} %get-tuple-element.59), channel_id=1, source_target_pairs={{0,2},{1,3},{2,0},{3,1},{4,6},{5,7},{6,4},{7,5},{8,10},{9,11},{10,... | collective-permute-start | bytes 98312 | tf_op jit(solution)/shard_map/ppermute | solution.py:373
  28.5 8.3 %collective-permute-start.7 = (bf16[128,128]{1,0:T(8,128)(2,1)S(1)}, bf16[128,128]{1,0:T(8,128)(2,1)S(1)}, u32[]{:S(2)}, u32[]{:S(2)}) collective-permute-start(bf16[128,128]{1,0:T(8,128)(2,1)S(1)} %get-tuple-element.60), channel_id=1, source_target_pairs={{0,1},{1,2},{2,3},{3,0},{4,5},{5,6},{6,7},{7,4},{8,9},{9,10},{10,1... | collective-permute-start | bytes 98312 | tf_op jit(solution)/shard_map/ppermute | solution.py:373
  36.8 1.3 %collective-permute-start.8 = (bf16[216,128]{1,0:T(8,128)(2,1)S(1)}, bf16[216,128]{1,0:T(8,128)(2,1)S(1)}, u32[]{:S(2)}, u32[]{:S(2)}) collective-permute-start(bf16[216,128]{1,0:T(8,128)(2,1)S(1)} %get-tuple-element.62), channel_id=1, source_target_pairs={{0,1},{1,0},{2,3},{3,2},{4,5},{5,4},{6,7},{7,6},{8,9},{9,8},{10,11... | collective-permute-start | bytes 165896 | tf_op jit(solution)/shard_map/ppermute | solution.py:369
  51.5 3.1 %collective-permute-start.9 = (f32[72,128]{1,0:T(8,128)S(1)}, f32[72,128]{1,0:T(8,128)S(1)}, u32[]{:S(2)}, u32[]{:S(2)}) collective-permute-start(f32[72,128]{1,0:T(8,128)S(1)} %convert_element_type.17), channel_id=1, source_target_pairs={{0,8},{8,0},{16,24},{24,16},{32,40},{40,32},{48,56},{56,48},{1,9},... | collective-permute-start | bytes 110600 | tf_op jit(solution)/shard_map/ppermute | solution.py:362
  54.5 4.3 %collective-permute-start.10 = (f32[72,128]{1,0:T(8,128)S(1)}, f32[72,128]{1,0:T(8,128)S(1)}, u32[]{:S(2)}, u32[]{:S(2)}) collective-permute-start(f32[72,128]{1,0:T(8,128)S(1)} %convert_add_fusion), channel_id=1, source_target_pairs={{0,16},{8,24},{16,0},{24,8},{32,48},{40,56},{48,32},{56,40},{1,17}... | collective-permute-start | bytes 110600 | tf_op jit(solution)/shard_map/ppermute | solution.py:362
  58.9 6.0 %collective-permute-start.11 = (bf16[72,128]{1,0:T(8,128)(2,1)S(1)}, bf16[72,128]{1,0:T(8,128)(2,1)S(1)}, u32[]{:S(2)}, u32[]{:S(2)}) collective-permute-start(bf16[72,128]{1,0:T(8,128)(2,1)S(1)} %add_convert_fusion.1), channel_id=1, source_target_pairs={{0,56},{8,48},{16,40},{24,32},{32,24},{40,16},{48,8},{56,0},{1,57}... | collective-permute-start | bytes 55304 | tf_op jit(solution)/shard_map/ppermute | solution.py:362
  76.1 7.3 %collective-permute-start.12 = (bf16[1152,128]{1,0:T(8,128)(2,1)S(1)}, bf16[1152,128]{1,0:T(8,128)(2,1)S(1)}, u32[]{:S(2)}, u32[]{:S(2)}) collective-permute-start(bf16[1152,128]{1,0:T(8,128)(2,1)S(1)} %bitcast.16), channel_id=1, source_target_pairs={{0,1},{1,0},{2,3},{3,2},{4,5},{5,4},{6,7},{7,6},{8,9},{9,8},{10,11... | collective-permute-start | bytes 884744 | tf_op jit(solution)/shard_map/ppermute | solution.py:369
